TPU v7x, 32 devices: a whole 2x2x4 slice. The times are simulated.
32 devices in a mesh: node: 4 (over y, core), edge: 8 (over z, x).
Axes of the slice: x: 2, y: 2, z: 4, core: 2. Of those that a mesh axis runs over, the one named last changes fastest.
Arguments:
- atoms: bfloat16 [4096, 1152], P(('node', 'edge')), may hold values from -6 to 6
- cotangent: bfloat16 [4096, 1152], P(('node', 'edge')), may hold values from -6 to 6
- params: float32 [409600], P('node'), may hold values from -4 to 4
- adam_m: float32 [409600], P('node'), may hold values from -4 to 4
- adam_v: float32 [409600], P('node'), may hold values from 0.3 to 3
- sends: int32 [4, 8, 128], P('node', 'edge'), may hold values from 0 to 127
- edge_slot: int32 [4096, 4], P(('node', 'edge')), may hold values from 0 to 127
- rot_index: int32 [4096, 4], P(('node', 'edge')), may hold values from 0 to 63
- rot_table: float32 [64, 9, 9], replicated, may hold values from -1.2 to 2, as said below
- edge_gain: float32 [4096, 4], P(('node', 'edge')), may hold values from 0.3 to 3
- live_tiles: int32 [4, 8], P('node', 'edge'), may hold values from 1 to 4, as said below
Outputs:
- output: bfloat16 [4096, 1152], P(('node', 'edge'))
- grad_atoms: bfloat16 [4096, 1152], P(('node', 'edge'))
- new_params: float32 [409600], P('node')
- new_moment_one: float32 [409600], P('node')
- new_moment_two: float32 [409600], P('node')
Inputs may be any that keep to these rules, and one draw needn't show every extreme that they name: The first live_tiles[n, e] edge tiles of a device are live; some device has all 4 tiles live. `rot_table`: rotations of degrees 0, 1 and 2 act on harmonics 0, 1 to 3 and 4 to 8 only.
All inputs are finite; a program needn't handle non-finite values.
Results may differ from a plain program's by a relative error of at most 0.0015.
The roundings to bfloat16 on the way count: a program that leaves them out, or rounds other values in their place, can miss the bound.
Values may be sent and summed in bfloat16 or wider, within the bound.
No kernel may reach another device: no remote copies, remote signals or barrier semaphores. Data moves between devices by JAX's collectives and lax.ppermute only.
A program may use at most 64 MiB of HBM per device.

v0:
```python
import jax
import jax.numpy as jnp
from jax import lax
from jax.sharding import PartitionSpec as P

C = 128
HARM = 9
FFH = 256
K = 4
TILE_ATOMS = 32
ROTS = 64


harmonic_order = (0, 2, 6, 3, 7, 1, 5, 8, 4)
highest = lax.Precision.HIGHEST
norm_epsilon = 1e-06
first_beta = 0.8
second_beta = 0.95
step_count = 100
learn_rate = 0.01
decay_rate = 0.01
adam_epsilon = 1e-08
grad_boost = 4.0


def unpack_weights(weights):
    lengths = [9 * C * C, 4 * C * C, 4 * C * C, C * C, C * C, C * FFH, C * FFH, FFH * C]
    starts = [0]
    for length in lengths:
        starts.append(starts[-1] + length)

    def take_piece(number, shape_pair):
        return weights[starts[number] : starts[number + 1]].reshape(shape_pair)

    zero_weight = take_piece(0, (3 * C, 3 * C))
    one_real = take_piece(1, (2 * C, 2 * C))
    one_imag = take_piece(2, (2 * C, 2 * C))
    two_real = take_piece(3, (C, C))
    two_imag = take_piece(4, (C, C))
    gate_weight = take_piece(5, (C, FFH))
    up_weight = take_piece(6, (C, FFH))
    down_weight = take_piece(7, (FFH, C))
    one_block = jnp.concatenate(
        [
            jnp.concatenate([one_real, one_imag], axis=1),
            jnp.concatenate([-one_imag, one_real], axis=1),
        ],
        axis=0,
    )
    two_block = jnp.concatenate(
        [
            jnp.concatenate([two_real, two_imag], axis=1),
            jnp.concatenate([-two_imag, two_real], axis=1),
        ],
        axis=0,
    )
    return (zero_weight, one_block, two_block, gate_weight, up_weight, down_weight)


def edge_forward(sources, rotation, edge_gains, matrices):
    zero_weight, one_block, two_block = (matrices[0], matrices[1], matrices[2])
    total_edges = sources.shape[0]
    rotated = jnp.einsum(
        "eij,ejc->eic", rotation, sources.astype(jnp.float32), precision=highest
    ).astype(jnp.bfloat16)
    zero_part = jnp.dot(
        rotated[:, 0:3].reshape(total_edges, 3 * C), zero_weight, preferred_element_type=jnp.float32
    ) * (3 * C) ** (-0.5)
    one_part = jnp.dot(
        rotated[:, 3:7].reshape(total_edges, 4 * C), one_block, preferred_element_type=jnp.float32
    ) * (4 * C) ** (-0.5)
    two_part = jnp.dot(
        rotated[:, 7:9].reshape(total_edges, 2 * C), two_block, preferred_element_type=jnp.float32
    ) * (2 * C) ** (-0.5)
    mixed = (
        jnp.concatenate([zero_part, one_part, two_part], axis=1).reshape(total_edges, HARM, C)
        * edge_gains[:, None, None]
    )
    messages = jnp.einsum("eji,ejc->eic", rotation, mixed, precision=highest)
    return (rotated, messages)


def edge_backward(rotated, rotation, edge_gains, upstream, matrices):
    zero_weight, one_block, two_block = (matrices[0], matrices[1], matrices[2])
    total_edges = rotated.shape[0]
    grad_mixed = (
        jnp.einsum("eij,ejc->eic", rotation, upstream, precision=highest)
        * edge_gains[:, None, None]
    ).astype(jnp.bfloat16)
    zero_in = rotated[:, 0:3].reshape(total_edges, 3 * C)
    one_in = rotated[:, 3:7].reshape(total_edges, 4 * C)
    two_in = rotated[:, 7:9].reshape(total_edges, 2 * C)
    zero_out = grad_mixed[:, 0:3].reshape(total_edges, 3 * C)
    one_out = grad_mixed[:, 3:7].reshape(total_edges, 4 * C)
    two_out = grad_mixed[:, 7:9].reshape(total_edges, 2 * C)
    zero_grad = jnp.dot(zero_in.T, zero_out, preferred_element_type=jnp.float32) * (3 * C) ** (-0.5)
    one_grad = jnp.dot(one_in.T, one_out, preferred_element_type=jnp.float32) * (4 * C) ** (-0.5)
    two_grad = jnp.dot(two_in.T, two_out, preferred_element_type=jnp.float32) * (2 * C) ** (-0.5)
    back_zero = jnp.dot(zero_out, zero_weight.T, preferred_element_type=jnp.float32) * (3 * C) ** (
        -0.5
    )
    back_one = jnp.dot(one_out, one_block.T, preferred_element_type=jnp.float32) * (4 * C) ** (-0.5)
    back_two = jnp.dot(two_out, two_block.T, preferred_element_type=jnp.float32) * (2 * C) ** (-0.5)
    grad_rotated = jnp.concatenate([back_zero, back_one, back_two], axis=1).reshape(
        total_edges, HARM, C
    )
    grad_sources = jnp.einsum("eij,eic->ejc", rotation, grad_rotated, precision=highest)
    return (grad_sources, (zero_grad, one_grad, two_grad))


def ffn_forward(atoms_block, aggregate, matrices):
    gate_weight, up_weight, down_weight = (matrices[3], matrices[4], matrices[5])
    number = atoms_block.shape[0]
    height = atoms_block.astype(jnp.float32).reshape(number, HARM, C) + aggregate
    inverse = lax.rsqrt(jnp.mean(height * height, axis=(1, 2), keepdims=True) + norm_epsilon)
    normed = height * inverse
    normed_low = normed.astype(jnp.bfloat16)
    gate_value = jax.nn.sigmoid(
        jnp.dot(normed_low[:, 0, :], gate_weight, preferred_element_type=jnp.float32) * C ** (-0.5)
    )
    up_value = jnp.dot(
        normed_low.reshape(number * HARM, C), up_weight, preferred_element_type=jnp.float32
    ).reshape(number, HARM, FFH) * C ** (-0.5)
    hidden_low = (up_value * gate_value[:, None, :]).astype(jnp.bfloat16)
    projected = jnp.dot(
        hidden_low.reshape(number * HARM, FFH), down_weight, preferred_element_type=jnp.float32
    ).reshape(number, HARM, C)
    output = (height + projected * FFH ** (-0.5)).astype(jnp.bfloat16)
    return (output, (inverse, normed, normed_low, gate_value, up_value, hidden_low))


def ffn_backward(stored, cotangent, matrices):
    gate_weight, up_weight, down_weight = (matrices[3], matrices[4], matrices[5])
    inverse, normed, normed_low, gate_value, up_value, hidden_low = stored
    number = cotangent.shape[0]
    upstream = cotangent.reshape(number * HARM, C)
    down_grad = jnp.dot(
        hidden_low.reshape(number * HARM, FFH).T, upstream, preferred_element_type=jnp.float32
    ) * FFH ** (-0.5)
    grad_hidden = jnp.dot(upstream, down_weight.T, preferred_element_type=jnp.float32).reshape(
        number, HARM, FFH
    ) * FFH ** (-0.5)
    grad_up = (grad_hidden * gate_value[:, None, :]).astype(jnp.bfloat16)
    grad_gate = (jnp.sum(grad_hidden * up_value, axis=1) * gate_value * (1.0 - gate_value)).astype(
        jnp.bfloat16
    )
    up_grad = jnp.dot(
        normed_low.reshape(number * HARM, C).T,
        grad_up.reshape(number * HARM, FFH),
        preferred_element_type=jnp.float32,
    ) * C ** (-0.5)
    gate_grad = jnp.dot(
        normed_low[:, 0, :].T, grad_gate, preferred_element_type=jnp.float32
    ) * C ** (-0.5)
    grad_normed = jnp.dot(
        grad_up.reshape(number * HARM, FFH), up_weight.T, preferred_element_type=jnp.float32
    ).reshape(number, HARM, C) * C ** (-0.5)
    grad_normed = grad_normed.at[:, 0, :].add(
        jnp.dot(grad_gate, gate_weight.T, preferred_element_type=jnp.float32) * C ** (-0.5)
    )
    grad_height = cotangent.astype(jnp.float32).reshape(number, HARM, C) + inverse * (
        grad_normed - normed * jnp.mean(grad_normed * normed, axis=(1, 2), keepdims=True)
    )
    return (grad_height, (gate_grad, up_grad, down_grad))


def flat_grads(zero_grad, one_grad, two_grad, gate_grad, up_grad, down_grad):
    half_one = 2 * C
    one_real = one_grad[:half_one, :half_one] + one_grad[half_one:, half_one:]
    one_imag = one_grad[:half_one, half_one:] - one_grad[half_one:, :half_one]
    two_real = two_grad[:C, :C] + two_grad[C:, C:]
    two_imag = two_grad[:C, C:] - two_grad[C:, :C]
    pieces = [zero_grad, one_real, one_imag, two_real, two_imag, gate_grad, up_grad, down_grad]
    return jnp.concatenate([matrix.reshape(-1) for matrix in pieces])


def adam_step(params, moment_one, moment_two, gradient):
    new_one = first_beta * moment_one + (1.0 - first_beta) * gradient
    new_two = second_beta * moment_two + (1.0 - second_beta) * gradient * gradient
    corrected = (
        new_one
        / (1.0 - first_beta**step_count)
        / (jnp.sqrt(new_two / (1.0 - second_beta**step_count)) + adam_epsilon)
    )
    return (params - learn_rate * (corrected + decay_rate * params), new_one, new_two)


def shards(
    atoms,
    cotangent,
    params,
    adam_m,
    adam_v,
    sends,
    edge_slot,
    rot_index,
    rot_table,
    edge_gain,
    live_tiles,
):
    node_size = lax.axis_size("node")
    edge_size = lax.axis_size("edge")
    weights = lax.all_gather(params.astype(jnp.bfloat16), "node", axis=0, tiled=True)
    matrices = unpack_weights(weights)
    rot_rows = rot_table[:, jnp.array(harmonic_order, dtype=jnp.int32), :].reshape(
        ROTS, HARM * HARM
    )
    outgoing = sends.reshape(-1)
    local_atoms = atoms.shape[0]
    features = atoms.shape[1]
    slot_count = outgoing.shape[0]
    per_peer = slot_count // edge_size
    wanted = lax.all_to_all(
        outgoing.reshape(edge_size, per_peer), "edge", split_axis=0, concat_axis=0, tiled=True
    )
    blocks = lax.all_gather(atoms, "edge", axis=0, tiled=True)
    offsets = jnp.arange(edge_size, dtype=jnp.int32)[:, None] * local_atoms
    slot_rows = blocks[(wanted + offsets).reshape(-1)]
    tile_edges = TILE_ATOMS * K
    live_count = live_tiles.reshape(-1)[0]
    edge_total = local_atoms * K
    slots_flat = edge_slot.reshape(-1)
    index_flat = rot_index.reshape(-1)
    gains_flat = edge_gain.reshape(-1)
    rot_range = jnp.arange(ROTS, dtype=jnp.int32)

    def tile_inputs(tile_number):
        first_edge = tile_number * tile_edges
        slots_here = lax.dynamic_slice_in_dim(slots_flat, first_edge, tile_edges)
        index_here = lax.dynamic_slice_in_dim(index_flat, first_edge, tile_edges)
        gains_here = lax.dynamic_slice_in_dim(gains_flat, first_edge, tile_edges)
        onehot = (index_here[:, None] == rot_range[None, :]).astype(jnp.float32)
        rotation = jnp.dot(onehot, rot_rows, precision=highest).reshape(tile_edges, HARM, HARM)
        return (slots_here, rotation, gains_here)

    def forward_tile(tile_number, loop_state):
        aggregate, rotated_all = loop_state
        slots_here, rotation, gains_here = tile_inputs(tile_number)
        sources = slot_rows[slots_here].reshape(tile_edges, HARM, C)
        rotated, messages = edge_forward(sources, rotation, gains_here, matrices)
        summed = messages.reshape(TILE_ATOMS, K, HARM, C).sum(axis=1) * K ** (-0.5)
        aggregate = lax.dynamic_update_slice_in_dim(aggregate, summed, tile_number * TILE_ATOMS, 0)
        rotated_all = lax.dynamic_update_slice_in_dim(
            rotated_all, rotated, tile_number * tile_edges, 0
        )
        return (aggregate, rotated_all)

    empty_state = (
        jnp.zeros((local_atoms, HARM, C), jnp.float32),
        jnp.zeros((edge_total, HARM, C), jnp.bfloat16),
    )
    aggregate, rotated_all = lax.fori_loop(0, live_count, forward_tile, empty_state)
    output, stored = ffn_forward(atoms, aggregate, matrices)
    grad_height, ffn_grads = ffn_backward(stored, cotangent, matrices)

    def backward_tile(tile_number, loop_state):
        slot_grad, zero_acc, one_acc, two_acc = loop_state
        slots_here, rotation, gains_here = tile_inputs(tile_number)
        rotated = lax.dynamic_slice_in_dim(rotated_all, tile_number * tile_edges, tile_edges, 0)
        height_here = lax.dynamic_slice_in_dim(grad_height, tile_number * TILE_ATOMS, TILE_ATOMS, 0)
        upstream = jnp.broadcast_to(height_here[:, None], (TILE_ATOMS, K, HARM, C)).reshape(
            tile_edges, HARM, C
        ) * K ** (-0.5)
        grad_sources, weight_parts = edge_backward(
            rotated, rotation, gains_here, upstream, matrices
        )
        slot_grad = slot_grad.at[slots_here].add(grad_sources.reshape(tile_edges, HARM * C))
        return (
            slot_grad,
            zero_acc + weight_parts[0],
            one_acc + weight_parts[1],
            two_acc + weight_parts[2],
        )

    initial = (
        jnp.zeros((slot_count, features), jnp.float32),
        jnp.zeros((3 * C, 3 * C), jnp.float32),
        jnp.zeros((4 * C, 4 * C), jnp.float32),
        jnp.zeros((2 * C, 2 * C), jnp.float32),
    )
    slot_grad, zero_grad, one_grad, two_grad = lax.fori_loop(0, live_count, backward_tile, initial)
    returned = lax.all_to_all(
        slot_grad.reshape(edge_size, per_peer, features),
        "edge",
        split_axis=0,
        concat_axis=0,
        tiled=True,
    ).reshape(slot_count, features)
    gathered_back = jnp.zeros((local_atoms, features), jnp.float32).at[outgoing].add(returned)
    grad_atoms = (grad_height.reshape(local_atoms, features) + gathered_back).astype(jnp.bfloat16)
    all_atoms = local_atoms * node_size * edge_size
    gradient = flat_grads(
        zero_grad, one_grad, two_grad, ffn_grads[0], ffn_grads[1], ffn_grads[2]
    ) * (grad_boost * all_atoms ** (-0.5))
    partial_rows = lax.psum_scatter(
        gradient.astype(jnp.bfloat16), "node", scatter_dimension=0, tiled=True
    )
    own_grad = lax.psum(partial_rows, "edge").astype(jnp.float32)
    new_params, new_one, new_two = adam_step(params, adam_m, adam_v, own_grad)
    return (output.reshape(local_atoms, features), grad_atoms, new_params, new_one, new_two)


def solution(mesh):
    return jax.shard_map(
        shards,
        mesh=mesh,
        in_specs=(
            P(("node", "edge"), None),
            P(("node", "edge"), None),
            P("node"),
            P("node"),
            P("node"),
            P("node", "edge", None),
            P(("node", "edge"), None),
            P(("node", "edge"), None),
            P(),
            P(("node", "edge"), None),
            P("node", "edge"),
        ),
        out_specs=(
            P(("node", "edge"), None),
            P(("node", "edge"), None),
            P("node"),
            P("node"),
            P("node"),
        ),
        check_vma=False,
    )
```

profile of v0, /device:TPU:0, one launch (start us, length us, event | category | flops | bytes accessed | tf_op | source)
XLA Modules:
  0.0 378.8 jit_solution(16567656678296600095)
XLA Ops:
  8.5 1.3 reduce.8
  10.5 7.3 %all-to-all-start = ((s32[8,1,16]{2,1,0:T(1,128)}), s32[8,1,16]{2,1,0:T(1,128)S(1)}, u32[]{:S(2)}, u32[]{:S(2)}) async-start(s32[8,1,16]{2,1,0:T(1,128)} %bitcast.3), calls=%async_computation | async-start | bytes 8192 | tf_op jit(solution)/shard_map/all_to_all | solution.py:213
  17.8 2.0 copy.104
  22.3 8.8 %all_gather.7 = bf16[409600]{0:T(1024)(128)(2,1)S(1)} all-gather(bf16[102400]{0:T(1024)(128)(2,1)S(1)} %convert_element_type.38), channel_id=1, replica_groups=mesh['node'=4,'edge'=8] {'node'}, dimensions={0}, use_global_device_ids=true | all-gather | bytes 1024000 | tf_op jit(solution)/shard_map/all_gather | solution.py:203
  32.1 1.4 fusion.40
  37.6 27.0 %all-gather.2.cloned.1.call-done = bf16[1024,1152]{1,0:T(8,128)(2,1)} async-done(((bf16[128,1152]{1,0:T(8,128)(2,1)}), bf16[1024,1152]{1,0:T(8,128)(2,1)}) %all-gather.2.cloned.1.call-update) | async-done | bytes 2359312 | tf_op jit(solution)/shard_map/all_gather | solution.py:216
  64.6 3.1 gather_fusion.2
  69.9 51.9 %while.31 = (s32[]{:T(128)}, f32[128,9,128]{2,1,0:T(8,128)}, bf16[512,9,128]{0,2,1:T(8,128)(2,1)}, s32[]{:T(128)}, s32[512]{0:T(512)S(1)}, /*index=5*/f32[64,81]...) while((s32[]{:T(128)}, f32[128,9,128]{2,1,0:T(8,128)}, ...), condition=%wide.region_2.0_spmd.clone, body=%wide.region_0.0_spmd.clone.sunk | while | flops 162342272 | bytes 14705741 | solution.py:252
  74.3 1.7 convolution_multiply_fusion.22
  80.4 1.9 broadcast_multiply_fusion.5
  82.3 1.6 copy.185
  83.9 1.2 bitcast_reduce_fusion.2
  91.3 1.7 convolution_multiply_fusion.22
  97.4 1.9 broadcast_multiply_fusion.5
  99.4 1.6 copy.185
  100.9 1.2 bitcast_reduce_fusion.2
  108.4 1.7 convolution_multiply_fusion.22
  114.5 1.9 broadcast_multiply_fusion.5
  116.5 1.6 copy.185
  118.0 1.2 bitcast_reduce_fusion.2
  121.7 1.5 copy.110
  123.2 1.4 multiply_reduce_fusion.2
  124.9 1.3 multiply_reduce_fusion
  128.8 1.4 copy.116
  133.8 73.2 %while.32 = (s32[]{:T(128)}, f32[128,1152]{1,0:T(8,128)}, f32[384,384]{1,0:T(8,128)}, f32[512,512]{1,0:T(8,128)}, f32[256,256]{1,0:T(8,128)}, /*index=5*/s32[]{:...) while((s32[]{:T(128)}, f32[128,1152]{1,0:T(8,128)}, ...), condition=%wide.region_8.9_spmd.clone, body=%wide.region_6.8_spmd.clone.sunk | while | flops 284963200 | bytes 33641452 | solution.py:281
  138.7 1.9 fusion.148
  140.7 1.8 convolution_multiply_fusion.25
  145.9 1.2 fusion.149
  147.6 3.6 scatter_fusion
  153.7 2.6 fusion.151
  162.8 1.9 fusion.148
  164.8 1.8 convolution_multiply_fusion.25
  170.0 1.2 fusion.149
  171.7 3.6 scatter_fusion
  177.9 2.6 fusion.151
  186.9 1.9 fusion.148
  188.9 1.8 convolution_multiply_fusion.25
  194.1 1.2 fusion.149
  195.8 3.6 scatter_fusion
  202.0 2.6 fusion.151
  208.1 1.3 subtract_bitcast_fusion
  213.5 1.5 fusion.27
  217.4 72.8 %all-reduce.6.cloned.1.call-done = bf16[409600]{0:T(1024)(128)(2,1)} async-done(((bf16[409600]{0:T(1024)(128)(2,1)}), bf16[409600]{0:T(1024)(128)(2,1)}) %all-reduce.6.cloned.1.call-update) | async-done | bytes 819216
  290.2 1.6 dynamic-slice.9
  294.2 5.5 %all-to-all-start.1 = ((f32[8,16,1152]{2,1,0:T(8,128)}), f32[8,16,1152]{2,1,0:T(8,128)S(1)}, u32[]{:S(2)}, u32[]{:S(2)}) async-start(f32[8,16,1152]{2,1,0:T(8,128)} %bitcast.17), calls=%async_computation.1 | async-start | bytes 1179648 | tf_op jit(solution)/shard_map/all_to_all | solution.py:282
  299.7 67.6 %all-reduce.4.cloned.1.call-done = bf16[102400]{0:T(1024)(128)(2,1)} async-done(((bf16[102400]{0:T(1024)(128)(2,1)}), bf16[102400]{0:T(1024)(128)(2,1)}) %all-reduce.4.cloned.1.call-update) | async-done | bytes 204816 | tf_op jit(solution)/shard_map/psum | solution.py:298
  367.3 2.2 multiply_subtract_fusion
  369.5 2.0 scatter_fusion.1
  (367 shorter events, 93.9 us)
Async XLA Ops:
  7.2 26.3 %copy-start = (f32[64,9,9]{0,2,1:T(8,128)S(1)}, f32[64,9,9]{0,2,1:T(8,128)}, u32[]{:S(2)}) copy-start(f32[64,9,9]{0,2,1:T(8,128)} %param.26) | copy-start | bytes 62212
  7.2 13.7 %copy-start.27 = (bf16[128,1152]{1,0:T(8,128)(2,1)S(1)}, bf16[128,1152]{1,0:T(8,128)(2,1)}, u32[]{:S(2)}) copy-start(bf16[128,1152]{1,0:T(8,128)(2,1)} %param.19) | copy-start | bytes 884740
  7.2 14.8 %copy-start.34 = (s32[128,4]{0,1:T(4,128)S(1)}, s32[128,4]{0,1:T(4,128)}, u32[]{:S(2)}) copy-start(s32[128,4]{0,1:T(4,128)} %param.25) | copy-start | bytes 6148
  7.2 15.0 %copy-start.25 = (f32[102400]{0:T(1024)S(1)}, f32[102400]{0:T(1024)}, u32[]{:S(2)}) copy-start(f32[102400]{0:T(1024)} %param.20) | copy-start | bytes 1228804
  7.2 57.4 %all-gather.2.cloned.1.call-start = ((), (), s32[]{:S(2)}) async-start(), calls=%async_computation.2 | async-start | bytes 2654208 | tf_op jit(solution)/shard_map/all_gather | solution.py:216
  10.5 26.4 %all-to-all-start = ((s32[8,1,16]{2,1,0:T(1,128)}), s32[8,1,16]{2,1,0:T(1,128)S(1)}, u32[]{:S(2)}, u32[]{:S(2)}) async-start(s32[8,1,16]{2,1,0:T(1,128)} %bitcast.3), calls=%async_computation | async-start | bytes 8192 | tf_op jit(solution)/shard_map/all_to_all | solution.py:213
  17.7 272.5 %all-reduce.6.cloned.1.call-start = ((), (), s32[]{:S(2)}) async-start(), calls=%async_computation.4 | async-start | bytes 1638400
  20.9 11.1 %copy-start.23 = (bf16[128,1152]{0,1:T(8,128)(2,1)}, bf16[128,1152]{0,1:T(8,128)(2,1)S(1)}, u32[]{:S(2)}) copy-start(bf16[128,1152]{0,1:T(8,128)(2,1)S(1)} %copy.113) | copy-start | bytes 884740
  22.2 9.1 %copy-start.39 = (s32[9]{0:T(128)S(1)}, s32[9]{0:T(128)}, u32[]{:S(2)}) copy-start(s32[9]{0:T(128)} %constant.134) | copy-start | bytes 112
  70.5 6.7 %copy-start.3 = (bf16[384,384]{1,0:T(8,128)(2,1)}, bf16[384,384]{1,0:T(8,128)(2,1)S(1)}, u32[]{:S(2)}) copy-start(bf16[384,384]{1,0:T(8,128)(2,1)S(1)} %get-tuple-element.635) | copy-start | bytes 884740 | tf_op jit(solution)/shard_map/while
  87.6 6.7 %copy-start.3 = (bf16[384,384]{1,0:T(8,128)(2,1)}, bf16[384,384]{1,0:T(8,128)(2,1)S(1)}, u32[]{:S(2)}) copy-start(bf16[384,384]{1,0:T(8,128)(2,1)S(1)} %get-tuple-element.635) | copy-start | bytes 884740 | tf_op jit(solution)/shard_map/while
  104.7 6.7 %copy-start.3 = (bf16[384,384]{1,0:T(8,128)(2,1)}, bf16[384,384]{1,0:T(8,128)(2,1)S(1)}, u32[]{:S(2)}) copy-start(bf16[384,384]{1,0:T(8,128)(2,1)S(1)} %get-tuple-element.635) | copy-start | bytes 884740 | tf_op jit(solution)/shard_map/while
  124.6 4.1 %copy-start.14 = (f32[128,9,128]{0,2,1:T(8,128)}, f32[128,9,128]{0,2,1:T(8,128)S(1)}, u32[]{:S(2)}) copy-start(f32[128,9,128]{0,2,1:T(8,128)S(1)} %get-tuple-element.412) | copy-start | bytes 1769476
  128.8 4.2 %copy-start.19 = (f32[128,9,128]{0,2,1:T(8,128)}, f32[128,9,128]{0,2,1:T(8,128)S(1)}, u32[]{:S(2)}) copy-start(f32[128,9,128]{0,2,1:T(8,128)S(1)} %multiply_add_fusion) | copy-start | bytes 1769476
  134.6 8.0 %copy-start.1 = (bf16[512,512]{1,0:T(8,128)(2,1)}, bf16[512,512]{1,0:T(8,128)(2,1)S(1)}, u32[]{:S(2)}) copy-start(bf16[512,512]{1,0:T(8,128)(2,1)S(1)} %get-tuple-element.700) | copy-start | bytes 1572868 | tf_op jit(solution)/shard_map/while
  134.6 9.2 %copy-start.5 = (bf16[384,384]{1,0:T(8,128)(2,1)}, bf16[384,384]{1,0:T(8,128)(2,1)S(1)}, u32[]{:S(2)}) copy-start(bf16[384,384]{1,0:T(8,128)(2,1)S(1)} %get-tuple-element.699) | copy-start | bytes 884740 | tf_op jit(solution)/shard_map/while
  147.6 4.6 %copy-start.9 = (f32[384,384]{1,0:T(8,128)S(1)}, f32[384,384]{1,0:T(8,128)}, u32[]{:S(2)}) copy-start(f32[384,384]{1,0:T(8,128)} %get-tuple-element.668) | copy-start | bytes 1769476 | tf_op jit(solution)/shard_map/while
  152.5 4.9 %copy-start.10 = (f32[384,384]{1,0:T(8,128)}, f32[384,384]{1,0:T(8,128)S(1)}, u32[]{:S(2)}) copy-start(f32[384,384]{1,0:T(8,128)S(1)} %fusion.150) | copy-start | bytes 1769476 | tf_op jit(solution)/shard_map/while
  152.5 4.6 %copy-start.13 = (bf16[128,2,128]{2,1,0:T(2,128)(2,1)S(1)}, bf16[128,2,128]{2,1,0:T(2,128)(2,1)}, u32[]{:S(2)}) copy-start(bf16[128,2,128]{2,1,0:T(2,128)(2,1)} %copy-done.12) | copy-start | bytes 196612 | tf_op jit(solution)/shard_map/while
  152.5 4.6 %copy-start.16 = (f32[256,256]{1,0:T(8,128)S(1)}, f32[256,256]{1,0:T(8,128)}, u32[]{:S(2)}) copy-start(f32[256,256]{1,0:T(8,128)} %get-tuple-element.670) | copy-start | bytes 786436 | tf_op jit(solution)/shard_map/while
  153.7 4.4 %copy-start.2 = (bf16[512,512]{1,0:T(8,128)(2,1)S(1)}, bf16[512,512]{1,0:T(8,128)(2,1)}, u32[]{:S(2)}) copy-start(bf16[512,512]{1,0:T(8,128)(2,1)} %copy-done.1) | copy-start | bytes 1572868 | tf_op jit(solution)/shard_map/while
  153.7 4.4 %copy-start.6 = (bf16[384,384]{1,0:T(8,128)(2,1)S(1)}, bf16[384,384]{1,0:T(8,128)(2,1)}, u32[]{:S(2)}) copy-start(bf16[384,384]{1,0:T(8,128)(2,1)} %copy-done.5) | copy-start | bytes 884740 | tf_op jit(solution)/shard_map/while
  153.7 4.3 %copy-start.38 = (s32[512]{0:T(512)S(1)}, s32[512]{0:T(512)}, u32[]{:S(2)}) copy-start(s32[512]{0:T(512)} %copy-done.37) | copy-start | bytes 6148 | tf_op jit(solution)/shard_map/while
  158.7 8.0 %copy-start.1 = (bf16[512,512]{1,0:T(8,128)(2,1)}, bf16[512,512]{1,0:T(8,128)(2,1)S(1)}, u32[]{:S(2)}) copy-start(bf16[512,512]{1,0:T(8,128)(2,1)S(1)} %get-tuple-element.700) | copy-start | bytes 1572868 | tf_op jit(solution)/shard_map/while
  158.8 9.2 %copy-start.5 = (bf16[384,384]{1,0:T(8,128)(2,1)}, bf16[384,384]{1,0:T(8,128)(2,1)S(1)}, u32[]{:S(2)}) copy-start(bf16[384,384]{1,0:T(8,128)(2,1)S(1)} %get-tuple-element.699) | copy-start | bytes 884740 | tf_op jit(solution)/shard_map/while
  171.7 4.6 %copy-start.9 = (f32[384,384]{1,0:T(8,128)S(1)}, f32[384,384]{1,0:T(8,128)}, u32[]{:S(2)}) copy-start(f32[384,384]{1,0:T(8,128)} %get-tuple-element.668) | copy-start | bytes 1769476 | tf_op jit(solution)/shard_map/while
  176.6 4.9 %copy-start.10 = (f32[384,384]{1,0:T(8,128)}, f32[384,384]{1,0:T(8,128)S(1)}, u32[]{:S(2)}) copy-start(f32[384,384]{1,0:T(8,128)S(1)} %fusion.150) | copy-start | bytes 1769476 | tf_op jit(solution)/shard_map/while
  176.6 4.6 %copy-start.13 = (bf16[128,2,128]{2,1,0:T(2,128)(2,1)S(1)}, bf16[128,2,128]{2,1,0:T(2,128)(2,1)}, u32[]{:S(2)}) copy-start(bf16[128,2,128]{2,1,0:T(2,128)(2,1)} %copy-done.12) | copy-start | bytes 196612 | tf_op jit(solution)/shard_map/while
  176.6 4.6 %copy-start.16 = (f32[256,256]{1,0:T(8,128)S(1)}, f32[256,256]{1,0:T(8,128)}, u32[]{:S(2)}) copy-start(f32[256,256]{1,0:T(8,128)} %get-tuple-element.670) | copy-start | bytes 786436 | tf_op jit(solution)/shard_map/while
  177.8 4.4 %copy-start.2 = (bf16[512,512]{1,0:T(8,128)(2,1)S(1)}, bf16[512,512]{1,0:T(8,128)(2,1)}, u32[]{:S(2)}) copy-start(bf16[512,512]{1,0:T(8,128)(2,1)} %copy-done.1) | copy-start | bytes 1572868 | tf_op jit(solution)/shard_map/while
  177.8 4.4 %copy-start.6 = (bf16[384,384]{1,0:T(8,128)(2,1)S(1)}, bf16[384,384]{1,0:T(8,128)(2,1)}, u32[]{:S(2)}) copy-start(bf16[384,384]{1,0:T(8,128)(2,1)} %copy-done.5) | copy-start | bytes 884740 | tf_op jit(solution)/shard_map/while
  177.8 4.3 %copy-start.38 = (s32[512]{0:T(512)S(1)}, s32[512]{0:T(512)}, u32[]{:S(2)}) copy-start(s32[512]{0:T(512)} %copy-done.37) | copy-start | bytes 6148 | tf_op jit(solution)/shard_map/while
  182.9 8.0 %copy-start.1 = (bf16[512,512]{1,0:T(8,128)(2,1)}, bf16[512,512]{1,0:T(8,128)(2,1)S(1)}, u32[]{:S(2)}) copy-start(bf16[512,512]{1,0:T(8,128)(2,1)S(1)} %get-tuple-element.700) | copy-start | bytes 1572868 | tf_op jit(solution)/shard_map/while
  182.9 9.2 %copy-start.5 = (bf16[384,384]{1,0:T(8,128)(2,1)}, bf16[384,384]{1,0:T(8,128)(2,1)S(1)}, u32[]{:S(2)}) copy-start(bf16[384,384]{1,0:T(8,128)(2,1)S(1)} %get-tuple-element.699) | copy-start | bytes 884740 | tf_op jit(solution)/shard_map/while
  195.8 4.6 %copy-start.9 = (f32[384,384]{1,0:T(8,128)S(1)}, f32[384,384]{1,0:T(8,128)}, u32[]{:S(2)}) copy-start(f32[384,384]{1,0:T(8,128)} %get-tuple-element.668) | copy-start | bytes 1769476 | tf_op jit(solution)/shard_map/while
  200.7 4.9 %copy-start.10 = (f32[384,384]{1,0:T(8,128)}, f32[384,384]{1,0:T(8,128)S(1)}, u32[]{:S(2)}) copy-start(f32[384,384]{1,0:T(8,128)S(1)} %fusion.150) | copy-start | bytes 1769476 | tf_op jit(solution)/shard_map/while
  200.7 4.6 %copy-start.13 = (bf16[128,2,128]{2,1,0:T(2,128)(2,1)S(1)}, bf16[128,2,128]{2,1,0:T(2,128)(2,1)}, u32[]{:S(2)}) copy-start(bf16[128,2,128]{2,1,0:T(2,128)(2,1)} %copy-done.12) | copy-start | bytes 196612 | tf_op jit(solution)/shard_map/while
  200.8 4.6 %copy-start.16 = (f32[256,256]{1,0:T(8,128)S(1)}, f32[256,256]{1,0:T(8,128)}, u32[]{:S(2)}) copy-start(f32[256,256]{1,0:T(8,128)} %get-tuple-element.670) | copy-start | bytes 786436 | tf_op jit(solution)/shard_map/while
  201.9 4.4 %copy-start.2 = (bf16[512,512]{1,0:T(8,128)(2,1)S(1)}, bf16[512,512]{1,0:T(8,128)(2,1)}, u32[]{:S(2)}) copy-start(bf16[512,512]{1,0:T(8,128)(2,1)} %copy-done.1) | copy-start | bytes 1572868 | tf_op jit(solution)/shard_map/while
  201.9 4.4 %copy-start.6 = (bf16[384,384]{1,0:T(8,128)(2,1)S(1)}, bf16[384,384]{1,0:T(8,128)(2,1)}, u32[]{:S(2)}) copy-start(bf16[384,384]{1,0:T(8,128)(2,1)} %copy-done.5) | copy-start | bytes 884740 | tf_op jit(solution)/shard_map/while
  202.0 4.3 %copy-start.38 = (s32[512]{0:T(512)S(1)}, s32[512]{0:T(512)}, u32[]{:S(2)}) copy-start(s32[512]{0:T(512)} %copy-done.37) | copy-start | bytes 6148 | tf_op jit(solution)/shard_map/while
  215.1 76.8 %copy-start.15 = (f32[128,9,128]{0,2,1:T(8,128)S(1)}, f32[128,9,128]{0,2,1:T(8,128)}, u32[]{:S(2)}) copy-start(f32[128,9,128]{0,2,1:T(8,128)} %copy-done.14) | copy-start | bytes 1769476
  216.1 77.9 %copy-start.20 = (f32[128,9,128]{0,2,1:T(8,128)S(1)}, f32[128,9,128]{0,2,1:T(8,128)}, u32[]{:S(2)}) copy-start(f32[128,9,128]{0,2,1:T(8,128)} %copy-done.19) | copy-start | bytes 1769476
  216.1 151.2 %all-reduce.4.cloned.1.call-start = ((), (), s32[]{:S(2)}) async-start(), calls=%async_computation.3 | async-start | bytes 409600 | tf_op jit(solution)/shard_map/psum | solution.py:298
  293.0 74.3 %copy-start.26 = (f32[102400]{0:T(1024)S(1)}, f32[102400]{0:T(1024)}, u32[]{:S(2)}) copy-start(f32[102400]{0:T(1024)} %param.20) | copy-start | bytes 1228804
  293.1 74.3 %copy-start.31 = (f32[102400]{0:T(1024)S(1)}, f32[102400]{0:T(1024)}, u32[]{:S(2)}) copy-start(f32[102400]{0:T(1024)} %param.22) | copy-start | bytes 1228804
  293.1 74.3 %copy-start.32 = (f32[102400]{0:T(1024)S(1)}, f32[102400]{0:T(1024)}, u32[]{:S(2)}) copy-start(f32[102400]{0:T(1024)} %param.21) | copy-start | bytes 1228804
  294.2 75.3 %all-to-all-start.1 = ((f32[8,16,1152]{2,1,0:T(8,128)}), f32[8,16,1152]{2,1,0:T(8,128)S(1)}, u32[]{:S(2)}, u32[]{:S(2)}) async-start(f32[8,16,1152]{2,1,0:T(8,128)} %bitcast.17), calls=%async_computation.1 | async-start | bytes 1179648 | tf_op jit(solution)/shard_map/all_to_all | solution.py:282
  (31 other events, 53.5 us)
Sparse Core Ops, SparseCore 0:
  10.2 54.3 all-gather.1
  216.2 73.9 all-reduce.5
  294.1 73.1 all-reduce.3
where the time goes:
time: 382 us; the launch traced here: 379 us
  waiting for transfers between devices  168 us (44%)
  local copies, waits for them, and re-layouts  72.2 us (19%)
  matrix products  52.5 us (14%)
  other arithmetic  42.5 us (11%)
  between operations  15 us (4%)
  starting transfers between devices  12.9 us (3%)
  blocking collectives  8.8 us (2%)
  loops' own time  6.67 us (2%)
    unnamed x4, waiting for transfers between devices  73.5 us
    psum x1, waiting for transfers between devices, shards(): own_grad = lax.psum(partial_rows, 'edge').astype(jnp.float32)  67.6 us
    all_gather x1, waiting for transfers between devices, shards(): blocks = lax.all_gather(atoms, 'edge', axis=0, tiled=True)  27 us
    scatter-add x3, other arithmetic, backward_tile(): slot_grad.at[slots_here].add(grad_sources.reshape(tile_edges, HARM * C))  10.9 us
    unnamed x71, local copies, waits for them, and re-layouts  9.29 us
    all_gather x1, blocking collectives, shards(): lax.all_gather(params.astype(jnp.bfloat16), 'node', axis=0, tiled=True)  8.8 us
    dot_general x3, matrix products, edge_backward(): jnp.dot(one_in.T, one_out, preferred_element_type=jnp.float32)  7.7 us
  transfers between devices with their start and end apart: 5, of which 3 were waited for; matrix products, arithmetic and copies ran while one was open for 5% of the time, Pallas kernels for 0%

commit v1 on v0

v1 whole, which is shorter than its diff:
```python
import functools

import jax
import jax.numpy as jnp
from jax import lax
from jax.experimental import pallas as pl
from jax.experimental.pallas import tpu as pltpu
from jax.sharding import PartitionSpec as P

C = 128
HARM = 9
FFH = 256
K = 4
TILE_ATOMS = 32
ROTS = 64
EDGE_ROWS = 16

harmonic_order = (0, 2, 6, 3, 7, 1, 5, 8, 4)
norm_epsilon = 1e-06
first_beta = 0.8
second_beta = 0.95
step_count = 100
learn_rate = 0.01
decay_rate = 0.01
adam_epsilon = 1e-08
grad_boost = 4.0

F32 = jnp.float32
BF16 = jnp.bfloat16

degree_block = (0, 1, 1, 1, 2, 2, 2, 2, 2)
entries = [
    (row, col, harmonic_order[row] * HARM + col)
    for row in range(HARM)
    for col in range(HARM)
    if degree_block[harmonic_order[row]] == degree_block[col]
]
place_of = {(row, col): place for place, (row, col, _) in enumerate(entries)}
cols_of = [[col for r, col, _ in entries if r == row] for row in range(HARM)]
rows_of = [[row for row, c, _ in entries if c == col] for col in range(HARM)]

ZERO, ONE, TWO = 3 * C, 4 * C, 2 * C
row_scale = [ZERO**-0.5] * 3 + [ONE**-0.5] * 4 + [TWO**-0.5] * 2
piece_rows = [9 * C, 4 * C, 4 * C, C, C, 2 * C, 2 * C, 2 * C]
piece_start = [sum(piece_rows[:i]) for i in range(len(piece_rows))]
PACK_ROWS = sum(piece_rows)


def lanes(number, width=C):
    return slice(number * width, (number + 1) * width)


def dot(left, right, left_dim=1, right_dim=0):
    return lax.dot_general(
        left, right, (((left_dim,), (right_dim,)), ((), ())), preferred_element_type=F32
    )


def split_parts(value, count):
    parts = []
    for _ in range(count):
        part = value.astype(BF16)
        parts.append(part)
        value = value - part.astype(F32)
    return parts


def as_low(mask):
    return jnp.where(mask, 1.0, 0.0).astype(BF16)


def pick_kernel(sends_ref, atoms_ref, rows_ref):
    shape = (atoms_ref.shape[0], sends_ref.shape[1])
    picks = as_low(lax.broadcasted_iota(jnp.int32, shape, 0) == sends_ref[...])
    rows_ref[...] = dot(picks, atoms_ref[...], 0, 0).astype(BF16)


def main_kernel(node_count, edge_parts, all_atoms, *refs):
    (
        live_ref,
        rows_ref,
        atoms_ref,
        cot_ref,
        slot_ref,
        index_ref,
        gain_ref,
        table_ref,
    ) = refs[:8]
    shard_refs = refs[8 : 8 + node_count]
    (
        output_ref,
        height_grad_ref,
        slot_grad_ref,
        grads_ref,
        packed,
        zero_w,
        one_w,
        two_w,
        gate_w,
        up_w,
        down_w,
        turn,
        gains,
        source,
        rotated,
        mixed,
        height,
        normed_low,
        up_value,
        hidden,
        cot_low,
        grad_up,
        grad_mixed,
    ) = refs[8 + node_count :]
    atoms_n = atoms_ref.shape[0]
    slots_n = rows_ref.shape[0]
    edges_n = atoms_n * K
    node = lax.axis_index("node")

    shard_rows = PACK_ROWS // node_count
    for distance in range(node_count):
        first = pl.multiple_of((node ^ distance) * shard_rows, 8)
        packed[pl.ds(first, shard_rows), :] = shard_refs[distance][...].astype(F32)

    def unpack(piece, rows, width):
        return [
            packed[pl.ds(piece_start[piece] + part, rows, stride=width), :].astype(BF16)
            for part in range(width)
        ]

    for part, block in enumerate(unpack(0, ZERO, 3)):
        zero_w[:, lanes(part)] = block
    for part, block in enumerate(unpack(1, 2 * C, 2)):
        one_w[0 : 2 * C, lanes(part)] = block
        one_w[2 * C : 4 * C, lanes(part + 2)] = block
    for part, block in enumerate(unpack(2, 2 * C, 2)):
        one_w[0 : 2 * C, lanes(part + 2)] = block
        one_w[2 * C : 4 * C, lanes(part)] = -block
    (block,) = unpack(3, C, 1)
    two_w[0:C, 0:C] = block
    two_w[C : 2 * C, C : 2 * C] = block
    (block,) = unpack(4, C, 1)
    two_w[0:C, C : 2 * C] = block
    two_w[C : 2 * C, 0:C] = -block
    for part, block in enumerate(unpack(5, C, 2)):
        gate_w[:, lanes(part)] = block
    for part, block in enumerate(unpack(6, C, 2)):
        up_w[:, lanes(part)] = block
    (block,) = unpack(7, FFH, 1)
    down_w[...] = block

    table = jnp.concatenate(split_parts(table_ref[...], 3), axis=0)
    table_range = lax.broadcasted_iota(jnp.int32, (atoms_n, ROTS), 1)
    slot_range = lax.broadcasted_iota(jnp.int32, (atoms_n, slots_n), 1)
    atom_range = lax.broadcasted_iota(jnp.int32, (atoms_n, C), 0)
    is_live = atom_range < live_ref[0, 0] * TILE_ATOMS
    for k in range(K):
        rows = slice(k * atoms_n, (k + 1) * atoms_n)
        chosen = as_low(index_ref[:, k : k + 1] == table_range)
        turns = dot(jnp.concatenate([chosen] * 3, axis=1), table)
        for place, (_, _, entry) in enumerate(entries):
            turn[place, rows, :] = jnp.broadcast_to(turns[:, entry : entry + 1], (atoms_n, C))
        gain = jnp.broadcast_to(gain_ref[:, k : k + 1], (atoms_n, C))
        gains[rows, :] = jnp.where(is_live, gain, 0.0) * K**-0.5
        taken = as_low(slot_ref[:, k : k + 1] == slot_range)
        source[rows, :] = dot(taken, rows_ref[...])

    def rotate(step, carry):
        rows = pl.ds(pl.multiple_of(step * EDGE_ROWS, EDGE_ROWS), EDGE_ROWS)
        values = [source[rows, lanes(col)] for col in range(HARM)]
        for row in range(HARM):
            total = sum(turn[place_of[row, col], rows, :] * values[col] for col in cols_of[row])
            rotated[rows, lanes(row)] = total.astype(BF16)
        return carry

    lax.fori_loop(0, edges_n // EDGE_ROWS, rotate, 0)
    mixed[:, 0:ZERO] = dot(rotated[:, 0:ZERO], zero_w[...])
    mixed[:, ZERO : ZERO + ONE] = dot(rotated[:, ZERO : ZERO + ONE], one_w[...])
    mixed[:, ZERO + ONE :] = dot(rotated[:, ZERO + ONE :], two_w[...])

    def atom_slice(step, base=0):
        return pl.ds(pl.multiple_of(base + step * EDGE_ROWS, EDGE_ROWS), EDGE_ROWS)

    def gather_messages(step, carry):
        here = atom_slice(step)
        totals = [atoms_ref[here, lanes(col)].astype(F32) for col in range(HARM)]
        for k in range(K):
            rows = atom_slice(step, k * atoms_n)
            gain = gains[rows, :]
            for row in range(HARM):
                value = mixed[rows, lanes(row)] * (gain * row_scale[row])
                for col in cols_of[row]:
                    totals[col] = totals[col] + turn[place_of[row, col], rows, :] * value
        squares = sum(total * total for total in totals)
        mean = jnp.sum(squares, axis=1, keepdims=True) * (1.0 / (HARM * C))
        inverse = lax.rsqrt(mean + norm_epsilon)
        for col in range(HARM):
            height[atom_slice(step, col * atoms_n), :] = totals[col]
            normed_low[atom_slice(step, col * atoms_n), :] = (totals[col] * inverse).astype(BF16)
            cot_low[atom_slice(step, col * atoms_n), :] = cot_ref[here, lanes(col)]
        return carry

    lax.fori_loop(0, atoms_n // EDGE_ROWS, gather_messages, 0)

    gate = jax.nn.sigmoid(dot(normed_low[0:atoms_n, :], gate_w[...]) * C**-0.5)
    up_value[...] = dot(normed_low[...], up_w[...]) * C**-0.5
    for col in range(HARM):
        rows = lanes(col, atoms_n)
        hidden[rows, :] = (up_value[rows, :] * gate).astype(BF16)
    projected = dot(hidden[...], down_w[...]) * FFH**-0.5
    for col in range(HARM):
        rows = lanes(col, atoms_n)
        output_ref[:, lanes(col)] = (height[rows, :] + projected[rows, :]).astype(BF16)
    grad_hidden = dot(cot_low[...], down_w[...], 1, 1) * FFH**-0.5
    gate_sum = jnp.zeros_like(gate)
    for col in range(HARM):
        rows = lanes(col, atoms_n)
        grad_up[rows, :] = (grad_hidden[rows, :] * gate).astype(BF16)
        gate_sum = gate_sum + grad_hidden[rows, :] * up_value[rows, :]
    grad_gate = (gate_sum * gate * (1.0 - gate)).astype(BF16)
    grad_normed = dot(grad_up[...], up_w[...], 1, 1) * C**-0.5
    gate_normed = dot(grad_gate, gate_w[...], 1, 1) * C**-0.5
    heights = [height[lanes(col, atoms_n), :] for col in range(HARM)]
    squares = sum(value * value for value in heights)
    mean = jnp.sum(squares, axis=1, keepdims=True) * (1.0 / (HARM * C))
    inverse = lax.rsqrt(mean + norm_epsilon)
    along = [grad_normed[lanes(col, atoms_n), :] for col in range(HARM)]
    along[0] = along[0] + gate_normed
    overlap = sum(along[col] * heights[col] for col in range(HARM)) * inverse
    overlap = jnp.sum(overlap, axis=1, keepdims=True) * (1.0 / (HARM * C))
    for col in range(HARM):
        rows = lanes(col, atoms_n)
        height_grad_ref[rows, :] = cot_low[rows, :].astype(F32) + inverse * (
            along[col] - heights[col] * (inverse * overlap)
        )

    def rotate_grads(step, carry):
        values = [height_grad_ref[atom_slice(step, col * atoms_n), :] for col in range(HARM)]
        for k in range(K):
            rows = atom_slice(step, k * atoms_n)
            gain = gains[rows, :]
            for row in range(HARM):
                total = sum(turn[place_of[row, col], rows, :] * values[col] for col in cols_of[row])
                grad_mixed[rows, lanes(row)] = (total * gain).astype(BF16)
        return carry

    lax.fori_loop(0, atoms_n // EDGE_ROWS, rotate_grads, 0)
    boost = grad_boost * all_atoms**-0.5

    def pack_piece(piece, rows, width, value):
        for part in range(width):
            packed[pl.ds(piece_start[piece] + part, rows, stride=width), :] = value[:, lanes(part)]

    zero_grad = dot(rotated[:, 0:ZERO], grad_mixed[:, 0:ZERO], 0, 0) * (row_scale[0] * boost)
    pack_piece(0, ZERO, 3, zero_grad)
    one_in = rotated[:, ZERO : ZERO + ONE]
    one_out = grad_mixed[:, ZERO : ZERO + ONE]
    one_grad = dot(one_in, one_out, 0, 0) * (row_scale[3] * boost)
    half = 2 * C
    pack_piece(1, half, 2, one_grad[:half, :half] + one_grad[half:, half:])
    pack_piece(2, half, 2, one_grad[:half, half:] - one_grad[half:, :half])
    two_grad = dot(rotated[:, ZERO + ONE :], grad_mixed[:, ZERO + ONE :], 0, 0)
    two_grad = two_grad * (row_scale[7] * boost)
    pack_piece(3, C, 1, two_grad[:C, :C] + two_grad[C:, C:])
    pack_piece(4, C, 1, two_grad[:C, C:] - two_grad[C:, :C])
    pack_piece(5, C, 2, dot(normed_low[0:atoms_n, :], grad_gate, 0, 0) * (C**-0.5 * boost))
    pack_piece(6, C, 2, dot(normed_low[...], grad_up[...], 0, 0) * (C**-0.5 * boost))
    pack_piece(7, FFH, 1, dot(hidden[...], cot_low[...], 0, 0) * (FFH**-0.5 * boost))
    part_rows = shard_rows // edge_parts
    edge_low = lax.axis_index("edge") & (edge_parts - 1)
    bits = node_count.bit_length() - 1
    for place in range(node_count):
        distance = int(format(place, "b").zfill(bits)[::-1], 2) if bits else 0
        for part in range(edge_parts):
            first = (node ^ distance) * shard_rows + (edge_low ^ part) * part_rows
            values = packed[pl.ds(pl.multiple_of(first, 8), part_rows), :]
            grads_ref[lanes(place * edge_parts + part, part_rows), :] = values.astype(BF16)

    mixed[:, 0:ZERO] = dot(grad_mixed[:, 0:ZERO], zero_w[...], 1, 1)
    mixed[:, ZERO : ZERO + ONE] = dot(grad_mixed[:, ZERO : ZERO + ONE], one_w[...], 1, 1)
    mixed[:, ZERO + ONE :] = dot(grad_mixed[:, ZERO + ONE :], two_w[...], 1, 1)

    def rotate_back(step, carry):
        rows = pl.ds(pl.multiple_of(step * EDGE_ROWS, EDGE_ROWS), EDGE_ROWS)
        values = [mixed[rows, lanes(row)] * row_scale[row] for row in range(HARM)]
        for col in range(HARM):
            source[rows, lanes(col)] = sum(
                turn[place_of[row, col], rows, :] * values[row] for row in rows_of[col]
            )
        return carry

    lax.fori_loop(0, edges_n // EDGE_ROWS, rotate_back, 0)
    parts = []
    for k in range(K):
        parts.append(as_low(slot_ref[:, k : k + 1] == slot_range))
    taken = jnp.concatenate(parts, axis=0)
    for col in range(HARM):
        pieces = split_parts(source[:, lanes(col)], 3)
        slot_grad_ref[:, lanes(col)] = sum(dot(taken, piece, 0, 0) for piece in pieces)


def finish_kernel(sends_ref, height_grad_ref, back_ref, grad_ref):
    atoms_n = grad_ref.shape[0]
    shape = (atoms_n, sends_ref.shape[1])
    picks = as_low(lax.broadcasted_iota(jnp.int32, shape, 0) == sends_ref[...])
    for col in range(HARM):
        pieces = split_parts(back_ref[:, lanes(col)], 3)
        total = sum(dot(picks, piece) for piece in pieces)
        grad_ref[:, lanes(col)] = (height_grad_ref[lanes(col, atoms_n), :] + total).astype(BF16)


def adam_step(params, moment_one, moment_two, gradient):
    new_one = first_beta * moment_one + (1.0 - first_beta) * gradient
    new_two = second_beta * moment_two + (1.0 - second_beta) * gradient * gradient
    corrected = (
        new_one
        / (1.0 - first_beta**step_count)
        / (jnp.sqrt(new_two / (1.0 - second_beta**step_count)) + adam_epsilon)
    )
    return (params - learn_rate * (corrected + decay_rate * params), new_one, new_two)


def swap(value, axis, bit):
    size = lax.axis_size(axis)
    return lax.ppermute(value, axis, [(i, i ^ (1 << bit)) for i in range(size)])


def shards(
    atoms,
    cotangent,
    params,
    adam_m,
    adam_v,
    sends,
    edge_slot,
    rot_index,
    rot_table,
    edge_gain,
    live_tiles,
):
    node_size = lax.axis_size("node")
    edge_size = lax.axis_size("edge")
    node_bits = node_size.bit_length() - 1
    edge_bits = edge_size.bit_length() - 1
    atoms_n, features = atoms.shape
    slots_n = sends.shape[-1]
    per_peer = slots_n // edge_size
    edges_n = atoms_n * K
    edge_parts = 2 if edge_bits else 1
    vmem = pl.BlockSpec(memory_space=pltpu.VMEM)
    smem = pl.BlockSpec(memory_space=pltpu.SMEM)

    own = params.reshape(-1, C).astype(BF16)
    shard_list = [own]
    by_distance = {0: own}
    for bit in reversed(range(node_bits)):
        for distance in list(by_distance):
            by_distance[distance | (1 << bit)] = swap(by_distance[distance], "node", bit)
    shard_list = [by_distance[distance] for distance in range(node_size)]

    send_rows = sends.reshape(1, slots_n)
    outgoing = pl.pallas_call(
        pick_kernel,
        out_shape=jax.ShapeDtypeStruct((slots_n, features), BF16),
        in_specs=[vmem] * 2,
        out_specs=vmem,
        name="pick",
    )(send_rows, atoms)
    slot_rows = lax.all_to_all(
        outgoing.reshape(edge_size, per_peer, features),
        "edge",
        split_axis=0,
        concat_axis=0,
        tiled=True,
    ).reshape(slots_n, features)

    f32_rows = functools.partial(pltpu.VMEM, dtype=F32)
    low_rows = functools.partial(pltpu.VMEM, dtype=BF16)
    output, height_grad, slot_grad, grads = pl.pallas_call(
        functools.partial(main_kernel, node_size, edge_parts, atoms_n * node_size * edge_size),
        out_shape=(
            jax.ShapeDtypeStruct((atoms_n, features), BF16),
            jax.ShapeDtypeStruct((HARM * atoms_n, C), F32),
            jax.ShapeDtypeStruct((slots_n, features), F32),
            jax.ShapeDtypeStruct((PACK_ROWS, C), BF16),
        ),
        in_specs=[smem] + [vmem] * (7 + node_size),
        out_specs=(vmem,) * 4,
        scratch_shapes=[
            pltpu.VMEM((PACK_ROWS, C), F32),
            pltpu.VMEM((ZERO, ZERO), BF16),
            pltpu.VMEM((ONE, ONE), BF16),
            pltpu.VMEM((TWO, TWO), BF16),
            pltpu.VMEM((C, FFH), BF16),
            pltpu.VMEM((C, FFH), BF16),
            pltpu.VMEM((FFH, C), BF16),
            pltpu.VMEM((len(entries), edges_n, C), F32),
            pltpu.VMEM((edges_n, C), F32),
            pltpu.VMEM((edges_n, features), F32),
            pltpu.VMEM((edges_n, features), BF16),
            pltpu.VMEM((edges_n, features), F32),
            pltpu.VMEM((HARM * atoms_n, C), F32),
            pltpu.VMEM((HARM * atoms_n, C), BF16),
            pltpu.VMEM((HARM * atoms_n, FFH), F32),
            pltpu.VMEM((HARM * atoms_n, FFH), BF16),
            pltpu.VMEM((HARM * atoms_n, C), BF16),
            pltpu.VMEM((HARM * atoms_n, FFH), BF16),
            pltpu.VMEM((edges_n, features), BF16),
        ],
        name="layer",
    )(
        live_tiles,
        slot_rows,
        atoms,
        cotangent,
        edge_slot,
        rot_index,
        edge_gain,
        rot_table.reshape(ROTS, HARM * HARM),
        *shard_list,
    )

    for bit in range(node_bits):
        half = grads.shape[0] // 2
        came = swap(grads[half:], "node", bit)
        grads = (grads[:half].astype(F32) + came.astype(F32)).astype(BF16)
    if edge_bits:
        half = grads.shape[0] // 2
        came = swap(grads[half:], "edge", 0)
        grads = (grads[:half].astype(F32) + came.astype(F32)).astype(BF16)
        for bit in range(1, edge_bits):
            came = swap(grads, "edge", bit)
            grads = (grads.astype(F32) + came.astype(F32)).astype(BF16)
        other = swap(grads, "edge", 0)
        is_low = (lax.axis_index("edge") & 1) == 0
        grads = jnp.concatenate(
            [jnp.where(is_low, grads, other), jnp.where(is_low, other, grads)], axis=0
        )

    returned = lax.all_to_all(
        slot_grad.reshape(edge_size, per_peer, features),
        "edge",
        split_axis=0,
        concat_axis=0,
        tiled=True,
    ).reshape(slots_n, features)
    grad_atoms = pl.pallas_call(
        finish_kernel,
        out_shape=jax.ShapeDtypeStruct((atoms_n, features), BF16),
        in_specs=[vmem] * 3,
        out_specs=vmem,
        name="finish",
    )(send_rows, height_grad, returned)

    def rows_of_lanes(value):
        return value.reshape(-1, C)

    new_params, new_one, new_two = adam_step(
        rows_of_lanes(params), rows_of_lanes(adam_m), rows_of_lanes(adam_v), grads.astype(F32)
    )
    return (
        output,
        grad_atoms,
        new_params.reshape(-1),
        new_one.reshape(-1),
        new_two.reshape(-1),
    )


def solution(mesh):
    return jax.shard_map(
        shards,
        mesh=mesh,
        in_specs=(
            P(("node", "edge"), None),
            P(("node", "edge"), None),
            P("node"),
            P("node"),
            P("node"),
            P("node", "edge", None),
            P(("node", "edge"), None),
            P(("node", "edge"), None),
            P(),
            P(("node", "edge"), None),
            P("node", "edge"),
        ),
        out_specs=(
            P(("node", "edge"), None),
            P(("node", "edge"), None),
            P("node"),
            P("node"),
            P("node"),
        ),
        check_vma=False,
    )
```

time: 382 us -> 87.9 us (0.23)
  waiting for transfers between devices: 168 us -> 30.6 us
  local copies, waits for them, and re-layouts: 72.2 us -> 6.66 us
  matrix products: 52.5 us -> 0 us
  other arithmetic: 42.5 us -> 1.51 us
  Pallas kernels: 0 us -> 22.1 us
  between operations: 15 us -> 1.47 us
  starting transfers between devices: 12.9 us -> 25.1 us
  blocking collectives: 8.8 us -> 0 us
  loops' own time: 6.67 us -> 0 us
    unnamed x4 -> x0, waiting for transfers between devices: 73.5 us -> none
    psum x1 -> x0, waiting for transfers between devices: 67.6 us -> none  [shards(): own_grad = lax.psum(partial_rows, 'edge').astype(jnp.float32)]
    dot_general x54 -> x0, matrix products: 52.5 us -> none  [the longest x3 7.7 us: edge_backward(): jnp.dot(one_in.T, one_out, preferred_element_type=jnp.float32)]
    all_gather x1 -> x0, waiting for transfers between devices: 27 us -> none  [shards(): blocks = lax.all_gather(atoms, 'edge', axis=0, tiled=True)]
    pallas_call x0 -> x3, Pallas kernels: none -> 22.1 us  [the longest x1 17.8 us: shards(): pl.pallas_call(functools.partial(main_kernel, node_size, edge_parts, atom...]
    ppermute x0 -> x9, waiting for transfers between devices: none -> 20.9 us  [swap(): return lax.ppermute(value, axis, [(i, i ^ 1 << bit) for i in range(size)])]
    ppermute x0 -> x9, starting transfers between devices: none -> 13 us  [swap(): return lax.ppermute(value, axis, [(i, i ^ 1 << bit) for i in range(size)])]
    scatter-add x4 -> x0, other arithmetic: 12.9 us -> none  [the longest x3 10.9 us: backward_tile(): slot_grad.at[slots_here].add(grad_sources.reshape(tile_edges, HARM * C))]
  transfers between devices with their start and end apart: 5 -> 11, of which waited for: 3 -> 7; matrix products, arithmetic and copies ran while one was open for 5% -> 5% of each run, Pallas kernels for 0% -> 0%
where the time goes in v1:
time: 87.9 us; the launch traced here: 87.4 us
  waiting for transfers between devices  30.6 us (35%)
  starting transfers between devices  25.1 us (29%)
  Pallas kernels  22.1 us (25%)
  local copies, waits for them, and re-layouts  6.66 us (8%)
  other arithmetic  1.51 us (2%)
  between operations  1.47 us (2%)
    ppermute x9, waiting for transfers between devices, swap(): return lax.ppermute(value, axis, [(i, i ^ 1 << bit) for i in range(size)])  20.9 us
    pallas_call x1, Pallas kernels, shards(): pl.pallas_call(functools.partial(main_kernel, node_size, edge_parts, atom...  17.8 us
    ppermute x9, starting transfers between devices, swap(): return lax.ppermute(value, axis, [(i, i ^ 1 << bit) for i in range(size)])  13 us
    all_to_all x1, waiting for transfers between devices, shards(): lax.all_to_all(slot_grad.reshape(edge_size, per_peer, features), 'edge',...  9.63 us
    all_to_all x1, starting transfers between devices, shards(): lax.all_to_all(outgoing.reshape(edge_size, per_peer, features), 'edge', s...  7.42 us
    unnamed x31, local copies, waits for them, and re-layouts  4.83 us
    all_to_all x1, starting transfers between devices, shards(): lax.all_to_all(slot_grad.reshape(edge_size, per_peer, features), 'edge',...  4.68 us
    pallas_call x1, Pallas kernels, shards(): pl.pallas_call(finish_kernel, out_shape=jax.ShapeDtypeStruct((atoms_n, fe...  2.36 us
  transfers between devices with their start and end apart: 11, of which 7 were waited for; matrix products, arithmetic and copies ran while one was open for 5% of the time, Pallas kernels for 0%

profile of v1, /device:TPU:0, one launch (start us, length us, event | category | flops | bytes accessed | tf_op | source)
XLA Modules:
  0.0 87.4 jit_solution(11568419158007684812)
XLA Ops:
  0.6 2.0 %pick.1 = bf16[128,1152]{1,0:T(8,128)(2,1)} custom-call(s32[1,128]{1,0:T(1,128)} %bitcast.21, bf16[128,1152]{1,0:T(8,128)(2,1)} %refs_2_.1), custom_call_target="tpu_custom_call" | custom-call | tf_op jit(solution)/shard_map/pick/pallas_call | solution.py:362
  2.6 7.4 %all-to-all-start = ((bf16[8,16,1152]{2,1,0:T(8,128)(2,1)}), bf16[8,16,1152]{2,1,0:T(8,128)(2,1)S(1)}, u32[]{:S(2)}, u32[]{:S(2)}) async-start(bf16[8,16,1152]{2,1,0:T(8,128)(2,1)} %bitcast.19), calls=%async_computation | async-start | bytes 589824 | tf_op jit(solution)/shard_map/all_to_all | solution.py:369
  10.0 0.0 copy-done.1
  10.0 0.0 copy-start.10
  10.1 0.0 copy-start.4
  10.1 1.6 %collective-permute-start.1 = (bf16[800,128]{1,0:T(8,128)(2,1)S(1)}, bf16[800,128]{1,0:T(8,128)(2,1)S(1)}, u32[]{:S(2)}, u32[]{:S(2)}) collective-permute-start(bf16[800,128]{1,0:T(8,128)(2,1)S(1)} %convert_bitcast_fusion.refs_8_), channel_id=1, source_target_pairs={{0,16},{8,24},{16,0},{24,8},{1,17},{9,25},{17,1},{25,9},{2,18},{10... | collective-permute-start | bytes 614408 | tf_op jit(solution)/shard_map/ppermute | solution.py:325
  11.7 0.0 collective-permute-start
  11.7 5.0 %collective-permute-done.1.refs_10_ = bf16[800,128]{1,0:T(8,128)(2,1)S(1)} collective-permute-done((bf16[800,128]{1,0:T(8,128)(2,1)S(1)}, bf16[800,128]{1,0:T(8,128)(2,1)S(1)}, u32[]{:S(2)}, u32[]{:S(2)}) %collective-permute-start.1) | collective-permute-done | bytes 204832 | tf_op jit(solution)/shard_map/ppermute | solution.py:325
  16.7 0.0 collective-permute-start.2
  16.7 0.0 copy-done.10
  16.7 0.0 copy-start.11
  16.7 0.7 copy.23.refs_7_
  17.4 0.0 copy-done.11
  17.4 0.7 copy.20.refs_4_
  18.2 0.7 copy.21.refs_5_
  18.9 0.0 copy-done.13
  18.9 0.7 copy.22.refs_6_
  20.3 0.0 collective-permute-done.refs_9_
  20.3 0.0 copy-start.8
  20.3 0.0 collective-permute-done.2.refs_11_
  20.3 0.0 all-to-all-done
  20.3 0.0 copy-start.2
  20.4 0.6 copy-done.8
  21.0 0.1 copy-done.9
  21.0 0.1 copy-done.2
  21.2 17.8 %layer.1 = (bf16[128,1152]{1,0:T(8,128)(2,1)}, f32[1152,128]{1,0:T(8,128)}, f32[128,1152]{1,0:T(8,128)}, bf16[3200,128]{1,0:T(8,128)(2,1)}) custom-call(s32[1,1]{1,0:T(1,128)S(6)} %copy.24.refs_0_, bf16[128,1152]{1,0:T(8,128)(2,1)} %bitcast.20, bf16[128,1152]{1,0:T(8,128)(2,1)} %refs_2_.1, bf16[128,1152]{1,0:T(8,128)(2,1)} %refs_3_.1, ...), custom_call_target="tpu_custom_call" | custom-call | tf_op jit(solution)/shard_map/layer/pallas_call | solution.py:379
  39.0 1.1 %slice.19 = bf16[1600,128]{1,0:T(8,128)(2,1)S(1)} slice(bf16[3200,128]{1,0:T(8,128)(2,1)} %get-tuple-element.12), slice={[1600:3200], [0:128]} | slice | bytes 819200 | tf_op jit(solution)/shard_map/slice | solution.py:425
  40.1 0.6 collective-permute-start.3
  40.6 1.4 %collective-permute-done.3 = bf16[1600,128]{1,0:T(8,128)(2,1)S(1)} collective-permute-done((bf16[1600,128]{1,0:T(8,128)(2,1)S(1)}, bf16[1600,128]{1,0:T(8,128)(2,1)S(1)}, u32[]{:S(2)}, u32[]{:S(2)}) %collective-permute-start.3) | collective-permute-done | bytes 409632 | tf_op jit(solution)/shard_map/ppermute | solution.py:325
  42.0 0.0 copy-done.3
  42.0 0.1 add_convert_fusion
  42.1 1.6 %collective-permute-start.4 = (bf16[800,128]{1,0:T(8,128)(2,1)S(1)}, bf16[800,128]{1,0:T(8,128)(2,1)S(1)}, u32[]{:S(2)}, u32[]{:S(2)}) collective-permute-start(bf16[800,128]{1,0:T(8,128)(2,1)S(1)} %slice.25), channel_id=1, source_target_pairs={{0,16},{8,24},{16,0},{24,8},{1,17},{9,25},{17,1},{25,9},{2,18},{10... | collective-permute-start | bytes 614408 | tf_op jit(solution)/shard_map/ppermute | solution.py:325
  43.7 5.8 %collective-permute-done.4 = bf16[800,128]{1,0:T(8,128)(2,1)S(1)} collective-permute-done((bf16[800,128]{1,0:T(8,128)(2,1)S(1)}, bf16[800,128]{1,0:T(8,128)(2,1)S(1)}, u32[]{:S(2)}, u32[]{:S(2)}) %collective-permute-start.4) | collective-permute-done | bytes 204832 | tf_op jit(solution)/shard_map/ppermute | solution.py:325
  49.5 0.1 add_convert_fusion.1
  49.6 1.8 %collective-permute-start.5 = (bf16[400,128]{1,0:T(8,128)(2,1)S(1)}, bf16[400,128]{1,0:T(8,128)(2,1)S(1)}, u32[]{:S(2)}, u32[]{:S(2)}) collective-permute-start(bf16[400,128]{1,0:T(8,128)(2,1)S(1)} %slice.27), channel_id=1, source_target_pairs={{0,1},{1,0},{2,3},{3,2},{4,5},{5,4},{6,7},{7,6},{8,9},{9,8},{10,11... | collective-permute-start | bytes 307208 | tf_op jit(solution)/shard_map/ppermute | solution.py:325
  51.4 2.9 %collective-permute-done.5 = bf16[400,128]{1,0:T(8,128)(2,1)S(1)} collective-permute-done((bf16[400,128]{1,0:T(8,128)(2,1)S(1)}, bf16[400,128]{1,0:T(8,128)(2,1)S(1)}, u32[]{:S(2)}, u32[]{:S(2)}) %collective-permute-start.5) | collective-permute-done | bytes 102432 | tf_op jit(solution)/shard_map/ppermute | solution.py:325
  54.4 1.8 %collective-permute-start.6 = (bf16[400,128]{1,0:T(8,128)(2,1)S(1)}, bf16[400,128]{1,0:T(8,128)(2,1)S(1)}, u32[]{:S(2)}, u32[]{:S(2)}) collective-permute-start(bf16[400,128]{1,0:T(8,128)(2,1)S(1)} %add_convert_fusion.4), channel_id=1, source_target_pairs={{0,2},{1,3},{2,0},{3,1},{4,6},{5,7},{6,4},{7,5},{8,10},{9,11},{10,... | collective-permute-start | bytes 307208 | tf_op jit(solution)/shard_map/ppermute | solution.py:325
  56.2 2.9 %collective-permute-done.6 = bf16[400,128]{1,0:T(8,128)(2,1)S(1)} collective-permute-done((bf16[400,128]{1,0:T(8,128)(2,1)S(1)}, bf16[400,128]{1,0:T(8,128)(2,1)S(1)}, u32[]{:S(2)}, u32[]{:S(2)}) %collective-permute-start.6) | collective-permute-done | bytes 102432 | tf_op jit(solution)/shard_map/ppermute | solution.py:325
  59.1 2.8 %collective-permute-start.7 = (bf16[400,128]{1,0:T(8,128)(2,1)S(1)}, bf16[400,128]{1,0:T(8,128)(2,1)S(1)}, u32[]{:S(2)}, u32[]{:S(2)}) collective-permute-start(bf16[400,128]{1,0:T(8,128)(2,1)S(1)} %add_convert_fusion.3), channel_id=1, source_target_pairs={{0,4},{1,5},{2,6},{3,7},{4,0},{5,1},{6,2},{7,3},{8,12},{9,13},{10,... | collective-permute-start | bytes 307208 | tf_op jit(solution)/shard_map/ppermute | solution.py:325
  61.9 2.9 %collective-permute-done.7 = bf16[400,128]{1,0:T(8,128)(2,1)S(1)} collective-permute-done((bf16[400,128]{1,0:T(8,128)(2,1)S(1)}, bf16[400,128]{1,0:T(8,128)(2,1)S(1)}, u32[]{:S(2)}, u32[]{:S(2)}) %collective-permute-start.7) | collective-permute-done | bytes 102432 | tf_op jit(solution)/shard_map/ppermute | solution.py:325
  64.8 2.9 %collective-permute-start.8 = (bf16[400,128]{1,0:T(8,128)(2,1)S(1)}, bf16[400,128]{1,0:T(8,128)(2,1)S(1)}, u32[]{:S(2)}, u32[]{:S(2)}) collective-permute-start(bf16[400,128]{1,0:T(8,128)(2,1)S(1)} %add_convert_fusion.2), channel_id=1, source_target_pairs={{0,1},{1,0},{2,3},{3,2},{4,5},{5,4},{6,7},{7,6},{8,9},{9,8},{10,11... | collective-permute-start | bytes 307208 | tf_op jit(solution)/shard_map/ppermute | solution.py:325
  67.7 4.7 %all-to-all-start.1 = ((f32[8,16,1152]{2,1,0:T(8,128)}), f32[8,16,1152]{2,1,0:T(8,128)S(1)}, u32[]{:S(2)}, u32[]{:S(2)}) async-start(f32[8,16,1152]{2,1,0:T(8,128)} %bitcast.4), calls=%async_computation.1 | async-start | bytes 1179648 | tf_op jit(solution)/shard_map/all_to_all | solution.py:440
  72.4 0.0 collective-permute-done.8
  72.4 0.9 %copy-done.5 = f32[102400]{0:T(1024)S(1)} copy-done((f32[102400]{0:T(1024)S(1)}, f32[102400]{0:T(1024)}, u32[]{:S(2)}) %copy-start.5) | copy-done | bytes 409624
  73.4 1.2 %multiply_subtract_fusion = (f32[102400]{0:T(1024)}, f32[102400]{0:T(1024)}, f32[102400]{0:T(1024)}) fusion(f32[102400]{0:T(1024)S(1)} %copy-done.1, bf16[400,128]{1,0:T(8,128)(2,1)S(1)} %get-tuple-element.17, bf16[400,128]{1,0:T(8,128)(2,1)S(1)} %get-tuple-element.16, f32[102400]{0:T(1024)S(1)} %copy-done.5, f32[102400]{0:T(1024)S(1)} %copy-done.6), kind=kLoop, calls=%fused_computation.6 | loop fusion | flops 1945600 | bytes 2662400 | tf_op jit(solution)/shard_map/sub | solution.py:320
  74.6 9.6 %all-to-all-done.1 = f32[8,16,1152]{2,1,0:T(8,128)S(1)} async-done(((f32[8,16,1152]{2,1,0:T(8,128)}), f32[8,16,1152]{2,1,0:T(8,128)S(1)}, u32[]{:S(2)}, u32[]{:S(2)}) %all-to-all-start.1) | async-done | bytes 589856 | tf_op jit(solution)/shard_map/all_to_all | solution.py:440
  84.2 0.8 copy-done
  85.0 2.4 %finish.1 = bf16[128,1152]{1,0:T(8,128)(2,1)} custom-call(s32[1,128]{1,0:T(1,128)} %bitcast.22, f32[1152,128]{1,0:T(8,128)} %get-tuple-element.10.height_grad_ref, f32[128,1152]{1,0:T(8,128)} %bitcast.18), custom_call_target="tpu_custom_call" | custom-call | tf_op jit(solution)/shard_map/finish/pallas_call | solution.py:447
  (21 shorter events, 0.2 us)
Async XLA Ops:
  2.6 7.4 %copy-start.1 = (f32[102400]{0:T(1024)S(1)}, f32[102400]{0:T(1024)}, u32[]{:S(2)}) copy-start(f32[102400]{0:T(1024)} %param.13) | copy-start | bytes 1228804
  2.6 17.7 %all-to-all-start = ((bf16[8,16,1152]{2,1,0:T(8,128)(2,1)}), bf16[8,16,1152]{2,1,0:T(8,128)(2,1)S(1)}, u32[]{:S(2)}, u32[]{:S(2)}) async-start(bf16[8,16,1152]{2,1,0:T(8,128)(2,1)} %bitcast.19), calls=%async_computation | async-start | bytes 589824 | tf_op jit(solution)/shard_map/all_to_all | solution.py:369
  10.0 6.7 %copy-start.10 = (f32[64,9,9]{0,2,1:T(8,128)S(1)}, f32[64,9,9]{0,2,1:T(8,128)}, u32[]{:S(2)}) copy-start(f32[64,9,9]{0,2,1:T(8,128)} %param.19) | copy-start | bytes 62212
  10.1 10.3 %copy-start.4 = (bf16[800,128]{1,0:T(8,128)(2,1)}, bf16[800,128]{1,0:T(8,128)(2,1)S(1)}, u32[]{:S(2)}) copy-start(bf16[800,128]{1,0:T(8,128)(2,1)S(1)} %convert_bitcast_fusion.refs_8_) | copy-start | bytes 614404
  10.1 6.6 %collective-permute-start.1 = (bf16[800,128]{1,0:T(8,128)(2,1)S(1)}, bf16[800,128]{1,0:T(8,128)(2,1)S(1)}, u32[]{:S(2)}, u32[]{:S(2)}) collective-permute-start(bf16[800,128]{1,0:T(8,128)(2,1)S(1)} %convert_bitcast_fusion.refs_8_), channel_id=1, source_target_pairs={{0,16},{8,24},{16,0},{24,8},{1,17},{9,25},{17,1},{25,9},{2,18},{10... | collective-permute-start | bytes 614408 | tf_op jit(solution)/shard_map/ppermute | solution.py:325
  11.7 8.6 %collective-permute-start = (bf16[800,128]{1,0:T(8,128)(2,1)S(1)}, bf16[800,128]{1,0:T(8,128)(2,1)S(1)}, u32[]{:S(2)}, u32[]{:S(2)}) collective-permute-start(bf16[800,128]{1,0:T(8,128)(2,1)S(1)} %convert_bitcast_fusion.refs_8_), channel_id=1, source_target_pairs={{0,8},{8,0},{16,24},{24,16},{1,9},{9,1},{17,25},{25,17},{2,10},{10... | collective-permute-start | bytes 614408 | tf_op jit(solution)/shard_map/ppermute | solution.py:325
  16.7 3.7 %copy-start.7 = (bf16[800,128]{1,0:T(8,128)(2,1)}, bf16[800,128]{1,0:T(8,128)(2,1)S(1)}, u32[]{:S(2)}) copy-start(bf16[800,128]{1,0:T(8,128)(2,1)S(1)} %collective-permute-done.1.refs_10_) | copy-start | bytes 614404
  16.7 3.6 %collective-permute-start.2 = (bf16[800,128]{1,0:T(8,128)(2,1)S(1)}, bf16[800,128]{1,0:T(8,128)(2,1)S(1)}, u32[]{:S(2)}, u32[]{:S(2)}) collective-permute-start(bf16[800,128]{1,0:T(8,128)(2,1)S(1)} %collective-permute-done.1.refs_10_), channel_id=1, source_target_pairs={{0,8},{8,0},{16,24},{24,16},{1,9},{9,1},{17,25},{25,17},{2,10},{10... | collective-permute-start | bytes 614408 | tf_op jit(solution)/shard_map/ppermute | solution.py:325
  16.7 0.7 copy-start.11
  17.4 0.7 copy-start.12
  18.2 0.7 copy-start.13
  20.3 0.7 copy-start.8
  20.3 0.7 copy-start.9
  20.3 0.8 copy-start.2
  39.0 3.0 %copy-start.3 = (bf16[3200,128]{1,0:T(8,128)(2,1)S(1)}, bf16[3200,128]{1,0:T(8,128)(2,1)}, u32[]{:S(2)}) copy-start(bf16[3200,128]{1,0:T(8,128)(2,1)} %get-tuple-element.12) | copy-start | bytes 2457604
  40.1 1.9 %collective-permute-start.3 = (bf16[1600,128]{1,0:T(8,128)(2,1)S(1)}, bf16[1600,128]{1,0:T(8,128)(2,1)S(1)}, u32[]{:S(2)}, u32[]{:S(2)}) collective-permute-start(bf16[1600,128]{1,0:T(8,128)(2,1)S(1)} %slice.19), channel_id=1, source_target_pairs={{0,8},{8,0},{16,24},{24,16},{1,9},{9,1},{17,25},{25,17},{2,10},{10... | collective-permute-start | bytes 1228808 | tf_op jit(solution)/shard_map/ppermute | solution.py:325
  42.1 7.4 %collective-permute-start.4 = (bf16[800,128]{1,0:T(8,128)(2,1)S(1)}, bf16[800,128]{1,0:T(8,128)(2,1)S(1)}, u32[]{:S(2)}, u32[]{:S(2)}) collective-permute-start(bf16[800,128]{1,0:T(8,128)(2,1)S(1)} %slice.25), channel_id=1, source_target_pairs={{0,16},{8,24},{16,0},{24,8},{1,17},{9,25},{17,1},{25,9},{2,18},{10... | collective-permute-start | bytes 614408 | tf_op jit(solution)/shard_map/ppermute | solution.py:325
  49.6 4.7 %collective-permute-start.5 = (bf16[400,128]{1,0:T(8,128)(2,1)S(1)}, bf16[400,128]{1,0:T(8,128)(2,1)S(1)}, u32[]{:S(2)}, u32[]{:S(2)}) collective-permute-start(bf16[400,128]{1,0:T(8,128)(2,1)S(1)} %slice.27), channel_id=1, source_target_pairs={{0,1},{1,0},{2,3},{3,2},{4,5},{5,4},{6,7},{7,6},{8,9},{9,8},{10,11... | collective-permute-start | bytes 307208 | tf_op jit(solution)/shard_map/ppermute | solution.py:325
  54.4 4.7 %collective-permute-start.6 = (bf16[400,128]{1,0:T(8,128)(2,1)S(1)}, bf16[400,128]{1,0:T(8,128)(2,1)S(1)}, u32[]{:S(2)}, u32[]{:S(2)}) collective-permute-start(bf16[400,128]{1,0:T(8,128)(2,1)S(1)} %add_convert_fusion.4), channel_id=1, source_target_pairs={{0,2},{1,3},{2,0},{3,1},{4,6},{5,7},{6,4},{7,5},{8,10},{9,11},{10,... | collective-permute-start | bytes 307208 | tf_op jit(solution)/shard_map/ppermute | solution.py:325
  59.1 5.6 %collective-permute-start.7 = (bf16[400,128]{1,0:T(8,128)(2,1)S(1)}, bf16[400,128]{1,0:T(8,128)(2,1)S(1)}, u32[]{:S(2)}, u32[]{:S(2)}) collective-permute-start(bf16[400,128]{1,0:T(8,128)(2,1)S(1)} %add_convert_fusion.3), channel_id=1, source_target_pairs={{0,4},{1,5},{2,6},{3,7},{4,0},{5,1},{6,2},{7,3},{8,12},{9,13},{10,... | collective-permute-start | bytes 307208 | tf_op jit(solution)/shard_map/ppermute | solution.py:325
  64.8 7.6 %collective-permute-start.8 = (bf16[400,128]{1,0:T(8,128)(2,1)S(1)}, bf16[400,128]{1,0:T(8,128)(2,1)S(1)}, u32[]{:S(2)}, u32[]{:S(2)}) collective-permute-start(bf16[400,128]{1,0:T(8,128)(2,1)S(1)} %add_convert_fusion.2), channel_id=1, source_target_pairs={{0,1},{1,0},{2,3},{3,2},{4,5},{5,4},{6,7},{7,6},{8,9},{9,8},{10,11... | collective-permute-start | bytes 307208 | tf_op jit(solution)/shard_map/ppermute | solution.py:325
  67.7 4.7 %copy-start.6 = (f32[102400]{0:T(1024)S(1)}, f32[102400]{0:T(1024)}, u32[]{:S(2)}) copy-start(f32[102400]{0:T(1024)} %param.14) | copy-start | bytes 1228804
  67.7 16.5 %all-to-all-start.1 = ((f32[8,16,1152]{2,1,0:T(8,128)}), f32[8,16,1152]{2,1,0:T(8,128)S(1)}, u32[]{:S(2)}, u32[]{:S(2)}) async-start(f32[8,16,1152]{2,1,0:T(8,128)} %bitcast.4), calls=%async_computation.1 | async-start | bytes 1179648 | tf_op jit(solution)/shard_map/all_to_all | solution.py:440
  72.4 1.0 %copy-start.5 = (f32[102400]{0:T(1024)S(1)}, f32[102400]{0:T(1024)}, u32[]{:S(2)}) copy-start(f32[102400]{0:T(1024)} %param.15) | copy-start | bytes 1228804
  84.2 0.8 copy-start

commit v2 on v1

v2 whole, which is shorter than its diff:
```python
import functools

import jax
import jax.numpy as jnp
from jax import lax
from jax.experimental import pallas as pl
from jax.experimental.pallas import tpu as pltpu
from jax.sharding import PartitionSpec as P

C = 128
HARM = 9
FFH = 256
K = 4
TILE_ATOMS = 32
ROTS = 64
SUB = 8
TURN_ROWS = 88

harmonic_order = (0, 2, 6, 3, 7, 1, 5, 8, 4)
norm_epsilon = 1e-06
first_beta = 0.8
second_beta = 0.95
step_count = 100
learn_rate = 0.01
decay_rate = 0.01
adam_epsilon = 1e-08
grad_boost = 4.0

F32 = jnp.float32
BF16 = jnp.bfloat16

degree_block = (0, 1, 1, 1, 2, 2, 2, 2, 2)
entries = [
    (row, col, harmonic_order[row] * HARM + col)
    for row in range(HARM)
    for col in range(HARM)
    if degree_block[harmonic_order[row]] == degree_block[col]
]
place_of = {(row, col): place for place, (row, col, _) in enumerate(entries)}
cols_of = [[col for r, col, _ in entries if r == row] for row in range(HARM)]
rows_of = [[row for row, c, _ in entries if c == col] for col in range(HARM)]

ZERO, ONE, TWO = 3 * C, 4 * C, 2 * C
row_scale = [ZERO**-0.5] * 3 + [ONE**-0.5] * 4 + [TWO**-0.5] * 2
piece_rows = [9 * C, 4 * C, 4 * C, C, C, 2 * C, 2 * C, 2 * C]
piece_start = [sum(piece_rows[:i]) for i in range(len(piece_rows))]
PACK_ROWS = sum(piece_rows)


def lanes(number, width=C):
    return slice(number * width, (number + 1) * width)


def dot(left, right, left_dim=1, right_dim=0):
    return lax.dot_general(
        left, right, (((left_dim,), (right_dim,)), ((), ())), preferred_element_type=F32
    )


def split_parts(value, count):
    parts = []
    for _ in range(count):
        part = value.astype(BF16)
        parts.append(part)
        value = value - part.astype(F32)
    return parts


def as_low(mask):
    return jnp.where(mask, 1.0, 0.0).astype(BF16)


def pick_kernel(sends_ref, atoms_ref, rows_ref):
    shape = (atoms_ref.shape[0], sends_ref.shape[1])
    picks = as_low(lax.broadcasted_iota(jnp.int32, shape, 0) == sends_ref[...])
    rows_ref[...] = dot(picks, atoms_ref[...], 0, 0).astype(BF16)


def prepare_kernel(node_count, *refs):
    atoms_ref, cot_ref, index_ref, table_ref = refs[:4]
    shard_refs = refs[4 : 4 + node_count]
    (
        zero_ref,
        one_ref,
        two_ref,
        zero_t_ref,
        one_t_ref,
        two_t_ref,
        gate_ref,
        up_ref,
        down_ref,
        gate_t_ref,
        up_t_ref,
        down_t_ref,
        atoms_t_ref,
        cot_t_ref,
        turn_ref,
        packed,
    ) = refs[4 + node_count :]
    atoms_n = atoms_ref.shape[0]
    node = lax.axis_index("node")

    shard_rows = PACK_ROWS // node_count
    for distance in range(node_count):
        first = pl.multiple_of((node ^ distance) * shard_rows, 8)
        packed[pl.ds(first, shard_rows), :] = shard_refs[distance][...].astype(F32)

    def unpack(piece, rows, width, *targets):
        for part in range(width):
            first = piece_start[piece] + part
            block = packed[pl.ds(first, rows, stride=width), :].astype(BF16)
            for target, turned, row, col, sign in targets:
                value = block if sign > 0 else -block
                if turned:
                    target[col + part * C : col + (part + 1) * C, row : row + rows] = value.T
                else:
                    target[row : row + rows, col + part * C : col + (part + 1) * C] = value

    half = 2 * C
    unpack(0, ZERO, 3, (zero_ref, False, 0, 0, 1), (zero_t_ref, True, 0, 0, 1))
    for piece, (matrix, turned, rows) in (
        (1, (one_ref, one_t_ref, half)),
        (3, (two_ref, two_t_ref, C)),
    ):
        width = rows // C
        unpack(
            piece,
            rows,
            width,
            (matrix, False, 0, 0, 1),
            (matrix, False, rows, rows, 1),
            (turned, True, 0, 0, 1),
            (turned, True, rows, rows, 1),
        )
        unpack(
            piece + 1,
            rows,
            width,
            (matrix, False, 0, rows, 1),
            (matrix, False, rows, 0, -1),
            (turned, True, 0, rows, 1),
            (turned, True, rows, 0, -1),
        )
    unpack(5, C, 2, (gate_ref, False, 0, 0, 1), (gate_t_ref, True, 0, 0, 1))
    unpack(6, C, 2, (up_ref, False, 0, 0, 1), (up_t_ref, True, 0, 0, 1))
    unpack(7, FFH, 1, (down_ref, False, 0, 0, 1), (down_t_ref, True, 0, 0, 1))

    for col in range(HARM):
        atoms_t_ref[:, lanes(col, atoms_n)] = atoms_ref[:, lanes(col)].T
        cot_t_ref[:, lanes(col, atoms_n)] = cot_ref[:, lanes(col)].T
    pieces = split_parts(table_ref[...], 3)
    range_of_table = lax.broadcasted_iota(jnp.int32, (ROTS, atoms_n), 0)
    for k in range(K):
        chosen = as_low(range_of_table == index_ref[k : k + 1, :])
        turn_ref[pl.ds(k * TURN_ROWS, HARM * HARM), :] = sum(dot(piece, chosen) for piece in pieces)


def turns_of(turn_ref, k, factors=None):
    values = {}
    for row, col, entry in entries:
        value = turn_ref[pl.ds(k * TURN_ROWS + entry, SUB, stride=0), :]
        values[row, col] = value if factors is None else value * factors[row]
    return values


def over_channels(body):
    def step(number, carry):
        body(pl.multiple_of(number * 2 * SUB, 2 * SUB))
        return carry

    lax.fori_loop(0, C // (2 * SUB), step, 0)


def rows_at(harmonic, first, count=SUB):
    return pl.ds(pl.multiple_of(harmonic * C + first, SUB), count)


def main_kernel(edge_parts, node_count, all_atoms, *refs):
    (
        live_ref,
        rows_ref,
        slot_ref,
        gain_ref,
        zero_t,
        one_t,
        two_t,
        gate_w,
        up_w,
        down_w,
        gate_t,
        up_t,
        down_t,
        atoms_t,
        cot_t,
        turn,
        output_ref,
        height_grad,
        grad_mixed,
        keep_ref,
        send_ref,
        source,
        rotated,
        mixed,
        height,
        normed_low,
        up_value,
        hidden,
        grad_up,
        packed,
    ) = refs
    atoms_n = output_ref.shape[0]
    slots_n = rows_ref.shape[0]
    node = lax.axis_index("node")

    slot_range = lax.broadcasted_iota(jnp.int32, (slots_n, atoms_n), 0)
    for k in range(K):
        taken = as_low(slot_range == slot_ref[k : k + 1, :])
        source[:, lanes(k, atoms_n)] = dot(rows_ref[...], taken, 0, 0)
    is_live = lax.broadcasted_iota(jnp.int32, (1, atoms_n), 1) < live_ref[0, 0] * TILE_ATOMS
    gains = jnp.where(is_live, gain_ref[...], 0.0) * K**-0.5

    for k in range(K):
        here = lanes(k, atoms_n)
        turns = turns_of(turn, k)

        def rotate(first, here=here, turns=turns):
            halves = []
            for start in (0, SUB):
                values = [source[rows_at(col, first + start), here] for col in range(HARM)]
                halves.append(
                    [
                        sum(turns[row, col] * values[col] for col in cols_of[row])
                        for row in range(HARM)
                    ]
                )
            for row in range(HARM):
                pair = jnp.concatenate([halves[0][row], halves[1][row]], axis=0)
                rotated[rows_at(row, first, 2 * SUB), here] = pair.astype(BF16)

        over_channels(rotate)
    one_rows = slice(ZERO, ZERO + ONE)
    two_rows = slice(ZERO + ONE, HARM * C)
    mixed[0:ZERO, :] = dot(zero_t[...], rotated[0:ZERO, :])
    mixed[one_rows, :] = dot(one_t[...], rotated[one_rows, :])
    mixed[two_rows, :] = dot(two_t[...], rotated[two_rows, :])

    for k in range(K):
        here = lanes(k, atoms_n)
        gain = jnp.broadcast_to(gains[k : k + 1, :], (SUB, atoms_n))
        turns = turns_of(turn, k, [gain * scale for scale in row_scale])

        def gather_messages(first, k=k, here=here, turns=turns):
            if k == 0:
                starts = [
                    atoms_t[pl.ds(first, 2 * SUB), lanes(col, atoms_n)].astype(F32)
                    for col in range(HARM)
                ]
            for start in (0, SUB):
                values = [mixed[rows_at(row, first + start), here] for row in range(HARM)]
                target = pl.ds(pl.multiple_of(first + start, SUB), SUB)
                for col in range(HARM):
                    there = lanes(col, atoms_n)
                    base = starts[col][start : start + SUB] if k == 0 else height[target, there]
                    total = sum(turns[row, col] * values[row] for row in rows_of[col])
                    height[target, there] = base + total

        over_channels(gather_messages)

    def atom_sum(value):
        total = sum(value[:, lanes(col, atoms_n)] for col in range(HARM))
        return jnp.sum(total, axis=0, keepdims=True)

    def each(value):
        return jnp.concatenate([value] * HARM, axis=1)

    mean = atom_sum(height[...] * height[...]) * (1.0 / (HARM * C))
    inverse = lax.rsqrt(mean + norm_epsilon)
    normed_low[...] = (height[...] * each(inverse)).astype(BF16)
    gate = jax.nn.sigmoid(dot(gate_t[...], normed_low[:, 0:atoms_n]) * C**-0.5)
    gate_each = each(gate)
    up_value[...] = dot(up_t[...], normed_low[...]) * C**-0.5
    hidden[...] = (up_value[...] * gate_each).astype(BF16)
    result = height[...] + dot(down_t[...], hidden[...]) * FFH**-0.5
    result = result.astype(BF16)
    for col in range(HARM):
        output_ref[:, lanes(col)] = result[:, lanes(col, atoms_n)].T
    grad_hidden = dot(down_w[...], cot_t[...]) * FFH**-0.5
    grad_up[...] = (grad_hidden * gate_each).astype(BF16)
    gate_sum = grad_hidden * up_value[...]
    gate_sum = sum(gate_sum[:, lanes(col, atoms_n)] for col in range(HARM))
    grad_gate = (gate_sum * gate * (1.0 - gate)).astype(BF16)
    along = dot(up_w[...], grad_up[...]) * C**-0.5
    gate_along = dot(gate_w[...], grad_gate) * C**-0.5
    along = jnp.concatenate([along[:, 0:atoms_n] + gate_along, along[:, atoms_n:]], axis=1)
    overlap = atom_sum(along * height[...]) * (inverse * (1.0 / (HARM * C)))
    height_grad[...] = cot_t[...].astype(F32) + each(inverse) * (
        along - height[...] * each(inverse * overlap)
    )

    for k in range(K):
        here = lanes(k, atoms_n)
        gain = jnp.broadcast_to(gains[k : k + 1, :], (SUB, atoms_n))
        turns = turns_of(turn, k, [gain] * HARM)

        def rotate_grads(first, here=here, turns=turns):
            halves = []
            for start in (0, SUB):
                target = pl.ds(pl.multiple_of(first + start, SUB), SUB)
                values = [height_grad[target, lanes(col, atoms_n)] for col in range(HARM)]
                halves.append(
                    [
                        sum(turns[row, col] * values[col] for col in cols_of[row])
                        for row in range(HARM)
                    ]
                )
            for row in range(HARM):
                pair = jnp.concatenate([halves[0][row], halves[1][row]], axis=0)
                grad_mixed[rows_at(row, first, 2 * SUB), here] = pair.astype(BF16)

        over_channels(rotate_grads)
    boost = grad_boost * all_atoms**-0.5

    def pack_piece(piece, rows, width, value):
        for part in range(width):
            packed[pl.ds(piece_start[piece] + part, rows, stride=width), :] = value[:, lanes(part)]

    def weight_grad(left, right, scale):
        return dot(left, right, 1, 1) * (scale * boost)

    zero_grad = weight_grad(rotated[0:ZERO, :], grad_mixed[0:ZERO, :], row_scale[0])
    pack_piece(0, ZERO, 3, zero_grad)
    one_grad = weight_grad(rotated[one_rows, :], grad_mixed[one_rows, :], row_scale[3])
    half = 2 * C
    pack_piece(1, half, 2, one_grad[:half, :half] + one_grad[half:, half:])
    pack_piece(2, half, 2, one_grad[:half, half:] - one_grad[half:, :half])
    two_grad = weight_grad(rotated[two_rows, :], grad_mixed[two_rows, :], row_scale[7])
    pack_piece(3, C, 1, two_grad[:C, :C] + two_grad[C:, C:])
    pack_piece(4, C, 1, two_grad[:C, C:] - two_grad[C:, :C])
    pack_piece(5, C, 2, weight_grad(normed_low[:, 0:atoms_n], grad_gate, C**-0.5))
    pack_piece(6, C, 2, weight_grad(normed_low[...], grad_up[...], C**-0.5))
    pack_piece(7, FFH, 1, weight_grad(hidden[...], cot_t[...], FFH**-0.5))
    shard_rows = PACK_ROWS // node_count
    part_rows = shard_rows // edge_parts
    edge_low = lax.axis_index("edge") & (edge_parts - 1)
    bits = node_count.bit_length() - 1
    blocks = []
    for place in range(node_count):
        distance = int(format(place, "b").zfill(bits)[::-1], 2) if bits else 0
        for part in range(edge_parts):
            blocks.append((node ^ distance) * shard_rows + (edge_low ^ part) * part_rows)
    half = len(blocks) // 2
    for number, first in enumerate(blocks):
        values = packed[pl.ds(pl.multiple_of(first, 8), part_rows), :].astype(BF16)
        target = keep_ref if number < half else send_ref
        target[lanes(number % half, part_rows), :] = values


def slot_kernel(slot_ref, zero_w, one_w, two_w, turn, grad_mixed, height_grad, *refs):
    slot_grad_ref, height_rows_ref, mixed, source = refs
    slots_n = slot_grad_ref.shape[0]
    atoms_n = slot_ref.shape[1]
    one_rows = slice(ZERO, ZERO + ONE)
    two_rows = slice(ZERO + ONE, HARM * C)
    mixed[0:ZERO, :] = dot(zero_w[...], grad_mixed[0:ZERO, :])
    mixed[one_rows, :] = dot(one_w[...], grad_mixed[one_rows, :])
    mixed[two_rows, :] = dot(two_w[...], grad_mixed[two_rows, :])
    for k in range(K):
        here = lanes(k, atoms_n)
        turns = turns_of(turn, k, row_scale)

        def rotate_back(first, here=here, turns=turns):
            for start in (0, SUB):
                values = [mixed[rows_at(row, first + start), here] for row in range(HARM)]
                for col in range(HARM):
                    source[rows_at(col, first + start), here] = sum(
                        turns[row, col] * values[row] for row in rows_of[col]
                    )

        over_channels(rotate_back)
    slot_range = lax.broadcasted_iota(jnp.int32, (slots_n, atoms_n), 0)
    taken = jnp.concatenate(
        [as_low(slot_range == slot_ref[k : k + 1, :]) for k in range(K)], axis=1
    )
    pieces = split_parts(source[...], 3)
    slot_grad_ref[...] = sum(dot(taken, piece, 1, 1) for piece in pieces)
    for col in range(HARM):
        height_rows_ref[:, lanes(col)] = height_grad[:, lanes(col, atoms_n)].T


def finish_kernel(sends_ref, height_rows_ref, back_ref, grad_ref):
    shape = (grad_ref.shape[0], sends_ref.shape[1])
    picks = as_low(lax.broadcasted_iota(jnp.int32, shape, 0) == sends_ref[...])
    pieces = split_parts(back_ref[...], 3)
    total = sum(dot(picks, piece) for piece in pieces)
    grad_ref[...] = (height_rows_ref[...] + total).astype(BF16)


def adam_step(params, moment_one, moment_two, gradient):
    new_one = first_beta * moment_one + (1.0 - first_beta) * gradient
    new_two = second_beta * moment_two + (1.0 - second_beta) * gradient * gradient
    corrected = (
        new_one
        / (1.0 - first_beta**step_count)
        / (jnp.sqrt(new_two / (1.0 - second_beta**step_count)) + adam_epsilon)
    )
    return (params - learn_rate * (corrected + decay_rate * params), new_one, new_two)


def swap(value, axis, bit):
    size = lax.axis_size(axis)
    return lax.ppermute(value, axis, [(i, i ^ (1 << bit)) for i in range(size)])


def shards(
    atoms,
    cotangent,
    params,
    adam_m,
    adam_v,
    sends,
    edge_slot,
    rot_index,
    rot_table,
    edge_gain,
    live_tiles,
):
    node_size = lax.axis_size("node")
    edge_size = lax.axis_size("edge")
    node_bits = node_size.bit_length() - 1
    edge_bits = edge_size.bit_length() - 1
    atoms_n, features = atoms.shape
    slots_n = sends.shape[-1]
    per_peer = slots_n // edge_size
    edges_n = atoms_n * K
    edge_parts = 2 if edge_bits else 1
    vmem = pl.BlockSpec(memory_space=pltpu.VMEM)
    smem = pl.BlockSpec(memory_space=pltpu.SMEM)

    own = params.reshape(-1, C).astype(BF16)
    by_distance = {0: own}
    with jax.named_scope("weights"):
        for bit in reversed(range(node_bits)):
            for distance in list(by_distance):
                with jax.named_scope(f"hop{bit}"):
                    by_distance[distance | (1 << bit)] = swap(by_distance[distance], "node", bit)
    shard_list = [by_distance[distance] for distance in range(node_size)]

    def call(kernel, outs, ins, name, scratch=(), scalars=0):
        return pl.pallas_call(
            kernel,
            out_shape=tuple(jax.ShapeDtypeStruct(*out) for out in outs),
            in_specs=[smem] * scalars + [vmem] * (len(ins) - scalars),
            out_specs=(vmem,) * len(outs),
            scratch_shapes=[pltpu.VMEM(*part) for part in scratch],
            name=name,
        )(*ins)

    def peers_exchange(value):
        value = value.reshape(edge_size, per_peer, features)
        value = lax.all_to_all(value, "edge", split_axis=0, concat_axis=0, tiled=True)
        return value.reshape(slots_n, features)

    send_rows = sends.reshape(1, slots_n)
    slots_t, index_t, gains_t = edge_slot.T, rot_index.T, edge_gain.T
    table_t = jnp.transpose(rot_table, (1, 2, 0)).reshape(HARM * HARM, ROTS)
    wide = HARM * atoms_n
    with jax.named_scope("pick"):
        (outgoing,) = call(pick_kernel, [((slots_n, features), BF16)], (send_rows, atoms), "pick")
    with jax.named_scope("rows"):
        slot_rows = peers_exchange(outgoing)
    with jax.named_scope("prepare"):
        prepared = call(
            functools.partial(prepare_kernel, node_size),
            [
                ((ZERO, ZERO), BF16),
                ((ONE, ONE), BF16),
                ((TWO, TWO), BF16),
                ((ZERO, ZERO), BF16),
                ((ONE, ONE), BF16),
                ((TWO, TWO), BF16),
                ((C, FFH), BF16),
                ((C, FFH), BF16),
                ((FFH, C), BF16),
                ((FFH, C), BF16),
                ((FFH, C), BF16),
                ((C, FFH), BF16),
                ((C, wide), BF16),
                ((C, wide), BF16),
                ((K * TURN_ROWS, atoms_n), F32),
            ],
            (atoms, cotangent, index_t, table_t, *shard_list),
            "prepare",
            [((PACK_ROWS, C), F32)],
        )
    with jax.named_scope("layer"):
        output, height_grad, grad_mixed, keep, send = call(
            functools.partial(main_kernel, edge_parts, node_size, atoms_n * node_size * edge_size),
            [
                ((atoms_n, features), BF16),
                ((C, wide), F32),
                ((features, edges_n), BF16),
                ((PACK_ROWS // 2, C), BF16),
                ((PACK_ROWS // 2, C), BF16),
            ],
            (live_tiles, slot_rows, slots_t, gains_t, *prepared[3:]),
            "layer",
            [
                ((features, edges_n), F32),
                ((features, edges_n), BF16),
                ((features, edges_n), F32),
                ((C, wide), F32),
                ((C, wide), BF16),
                ((FFH, wide), F32),
                ((FFH, wide), BF16),
                ((FFH, wide), BF16),
                ((PACK_ROWS, C), F32),
            ],
            scalars=1,
        )
    with jax.named_scope("slots"):
        slot_grad, height_rows = call(
            slot_kernel,
            [((slots_n, features), F32), ((atoms_n, features), F32)],
            (slots_t, *prepared[:3], prepared[-1], grad_mixed, height_grad),
            "slots",
            [((features, edges_n), F32), ((features, edges_n), F32)],
        )

    def add_low(left, right):
        return (left.astype(F32) + right.astype(F32)).astype(BF16)

    hops = [("node", bit) for bit in range(node_bits)] + [("edge", 0)] * (edge_parts - 1)
    for number, (axis, bit) in enumerate(hops):
        if number:
            half = keep.shape[0] // 2
            keep, send = keep[:half], keep[half:]
        with jax.named_scope(f"grads_{axis}{bit}"):
            keep = add_low(keep, swap(send, axis, bit))
    grads = keep
    for bit in range(1, edge_bits):
        with jax.named_scope(f"grads_edge{bit}"):
            grads = add_low(grads, swap(grads, "edge", bit))
    if edge_bits:
        with jax.named_scope("grads_back"):
            other = swap(grads, "edge", 0)
        is_low = (lax.axis_index("edge") & 1) == 0
        grads = jnp.concatenate(
            [jnp.where(is_low, grads, other), jnp.where(is_low, other, grads)], axis=0
        )

    with jax.named_scope("back"):
        returned = peers_exchange(slot_grad)
    with jax.named_scope("finish"):
        (grad_atoms,) = call(
            finish_kernel,
            [((atoms_n, features), BF16)],
            (send_rows, height_rows, returned),
            "finish",
        )

    def rows_of_lanes(value):
        return value.reshape(-1, C)

    new_params, new_one, new_two = adam_step(
        rows_of_lanes(params), rows_of_lanes(adam_m), rows_of_lanes(adam_v), grads.astype(F32)
    )
    return (
        output,
        grad_atoms,
        new_params.reshape(-1),
        new_one.reshape(-1),
        new_two.reshape(-1),
    )


def solution(mesh):
    return jax.shard_map(
        shards,
        mesh=mesh,
        in_specs=(
            P(("node", "edge"), None),
            P(("node", "edge"), None),
            P("node"),
            P("node"),
            P("node"),
            P("node", "edge", None),
            P(("node", "edge"), None),
            P(("node", "edge"), None),
            P(),
            P(("node", "edge"), None),
            P("node", "edge"),
        ),
        out_specs=(
            P(("node", "edge"), None),
            P(("node", "edge"), None),
            P("node"),
            P("node"),
            P("node"),
        ),
        check_vma=False,
    )
```

time: 87.9 us -> 86.6 us (0.985)
  local copies, waits for them, and re-layouts: 6.66 us -> 2.95 us
  waiting for transfers between devices: 30.6 us -> 31.8 us
  other arithmetic: 1.51 us -> 2.53 us
    unnamed x31 -> x20, local copies, waits for them, and re-layouts: 4.83 us -> 2.25 us
    slice x3 -> x2, local copies, waits for them, and re-layouts: 1.13 us -> 0.02 us  [shards(): keep, send = (keep[:half], keep[half:])]
    convert_element_type x5, other arithmetic: 0.26 us -> 1.26 us  [add_low(): return (left.astype(F32) + right.astype(F32)).astype(BF16)]
    all_to_all x2, waiting for transfers between devices: 9.63 us -> 10.6 us  [peers_exchange(): lax.all_to_all(value, 'edge', split_axis=0, concat_axis=0, tiled=True)]
    pallas_call x3 -> x5, Pallas kernels: 22.1 us -> 22.5 us  [call(): pl.pallas_call(kernel, out_shape=tuple((jax.ShapeDtypeStruct(*out) for ou...]
  transfers between devices with their start and end apart: 11 -> 11, of which waited for: 7 -> 8; matrix products, arithmetic and copies ran while one was open for 5% -> 2% of each run, Pallas kernels for 0% -> 11%
where the time goes in v2:
time: 86.6 us; the launch traced here: 86.1 us
  waiting for transfers between devices  31.8 us (37%)
  starting transfers between devices  24.8 us (29%)
  Pallas kernels  22.5 us (26%)
  local copies, waits for them, and re-layouts  2.95 us (3%)
  other arithmetic  2.53 us (3%)
  between operations  1.42 us (2%)
    pallas_call x5, Pallas kernels, call(): pl.pallas_call(kernel, out_shape=tuple((jax.ShapeDtypeStruct(*out) for ou...  22.5 us
    ppermute x9, waiting for transfers between devices, swap(): return lax.ppermute(value, axis, [(i, i ^ 1 << bit) for i in range(size)])  21.2 us
    ppermute x9, starting transfers between devices, swap(): return lax.ppermute(value, axis, [(i, i ^ 1 << bit) for i in range(size)])  12.9 us
    all_to_all x2, starting transfers between devices, peers_exchange(): lax.all_to_all(value, 'edge', split_axis=0, concat_axis=0, tiled=True)  12 us
    all_to_all x2, waiting for transfers between devices, peers_exchange(): lax.all_to_all(value, 'edge', split_axis=0, concat_axis=0, tiled=True)  10.6 us
    unnamed x20, local copies, waits for them, and re-layouts  2.25 us
  transfers between devices with their start and end apart: 11, of which 8 were waited for; matrix products, arithmetic and copies ran while one was open for 2% of the time, Pallas kernels for 11%

profile of v2, /device:TPU:0, one launch (start us, length us, event | category | flops | bytes accessed | tf_op | source)
XLA Modules:
  0.0 86.1 jit_solution(15087238968437313703)
XLA Ops:
  0.6 0.0 copy-start.1
  0.6 0.0 copy-start.9
  0.7 2.0 %pick.1 = bf16[128,1152]{1,0:T(8,128)(2,1)} custom-call(s32[1,128]{1,0:T(1,128)} %bitcast.28, bf16[128,1152]{1,0:T(8,128)(2,1)} %refs_0_.2), custom_call_target="tpu_custom_call" | custom-call | tf_op jit(solution)/shard_map/pick/pick/pallas_call | solution.py:449
  2.7 7.3 %all-to-all-start = ((bf16[8,16,1152]{2,1,0:T(8,128)(2,1)}), bf16[8,16,1152]{2,1,0:T(8,128)(2,1)S(1)}, u32[]{:S(2)}, u32[]{:S(2)}) async-start(bf16[8,16,1152]{2,1,0:T(8,128)(2,1)} %bitcast.21), calls=%async_computation | async-start | bytes 589824 | tf_op jit(solution)/shard_map/rows/all_to_all | solution.py:460
  9.9 0.0 copy-done.1
  10.0 0.0 copy-start.3
  10.0 1.6 %collective-permute-start.1 = (bf16[800,128]{1,0:T(8,128)(2,1)S(1)}, bf16[800,128]{1,0:T(8,128)(2,1)S(1)}, u32[]{:S(2)}, u32[]{:S(2)}) collective-permute-start(bf16[800,128]{1,0:T(8,128)(2,1)S(1)} %convert_bitcast_fusion.refs_4_), channel_id=1, source_target_pairs={{0,16},{8,24},{16,0},{24,8},{1,17},{9,25},{17,1},{25,9},{2,18},{10... | collective-permute-start | bytes 614408 | tf_op jit(solution)/shard_map/weights/hop1/ppermute | solution.py:411
  11.6 0.0 collective-permute-start
  11.6 5.0 %collective-permute-done.1.refs_6_ = bf16[800,128]{1,0:T(8,128)(2,1)S(1)} collective-permute-done((bf16[800,128]{1,0:T(8,128)(2,1)S(1)}, bf16[800,128]{1,0:T(8,128)(2,1)S(1)}, u32[]{:S(2)}, u32[]{:S(2)}) %collective-permute-start.1) | collective-permute-done | bytes 204832 | tf_op jit(solution)/shard_map/weights/hop1/ppermute | solution.py:411
  16.6 0.0 copy-start.6
  16.6 0.0 collective-permute-start.2
  16.6 0.0 copy-done.9
  16.6 0.7 reshape.44.refs_3_
  17.9 0.0 collective-permute-done.refs_5_
  17.9 0.0 copy-start.7
  18.0 0.1 collective-permute-done.2.refs_7_
  18.1 0.0 copy-start.8
  18.1 0.0 copy-done.3
  18.1 0.0 copy-done.6
  18.1 0.6 copy-done.7
  18.6 0.1 copy-done.8
  18.7 3.3 %prepare.1 = (bf16[384,384]{1,0:T(8,128)(2,1)}, bf16[512,512]{1,0:T(8,128)(2,1)}, bf16[256,256]{1,0:T(8,128)(2,1)}, bf16[384,384]{1,0:T(8,128)(2,1)}, bf16[512,5...) custom-call(bf16[128,1152]{1,0:T(8,128)(2,1)} %refs_0_.2, ...), custom_call_target="tpu_custom_call" | custom-call | tf_op jit(solution)/shard_map/prepare/prepare/pallas_call | solution.py:449
  22.0 0.0 all-to-all-done
  22.0 0.0 copy-start.2
  22.0 0.7 copy-done.2
  22.7 8.9 %layer.1 = (bf16[128,1152]{1,0:T(8,128)(2,1)}, f32[128,1152]{1,0:T(8,128)}, bf16[1152,512]{1,0:T(8,128)(2,1)}, bf16[1600,128]{1,0:T(8,128)(2,1)}, bf16[1600,128]{1,0:T(8,128)(2,1)}) custom-call(s32[1,1]{1,0:T(1,128)S(6)} %copy.16.refs_0_, bf16[128,1152]{1,0:T(8,128)(2,1)} %bitcast.22, s32[4,128]{1,0:T(4,128)} %bitcast.25, f32[4,128]{1,0:T(4,128)} %bitcast.30, ...), custom_call_target="tpu_custom_call" | custom-call | tf_op jit(solution)/shard_map/layer/layer/pallas_call | solution.py:449
  31.6 0.4 collective-permute-start.3
  32.0 1.6 %collective-permute-done.3 = bf16[1600,128]{1,0:T(8,128)(2,1)S(1)} collective-permute-done((bf16[1600,128]{1,0:T(8,128)(2,1)}, bf16[1600,128]{1,0:T(8,128)(2,1)S(1)}, u32[]{:S(2)}, u32[]{:S(2)}) %collective-permute-start.3) | collective-permute-done | bytes 409632 | tf_op jit(solution)/shard_map/grads_node0/ppermute | solution.py:411
  33.6 1.1 %add_convert_fusion = bf16[1600,128]{1,0:T(8,128)(2,1)S(1)} fusion(bf16[1600,128]{1,0:T(8,128)(2,1)S(1)} %collective-permute-done.3, bf16[1600,128]{1,0:T(8,128)(2,1)} %get-tuple-element.47), kind=kLoop, calls=%fused_computation | loop fusion | flops 819200 | bytes 1228800 | tf_op jit(solution)/shard_map/grads_node0/convert_element_type | solution.py:530
  34.7 1.6 %collective-permute-start.4 = (bf16[800,128]{1,0:T(8,128)(2,1)S(1)}, bf16[800,128]{1,0:T(8,128)(2,1)S(1)}, u32[]{:S(2)}, u32[]{:S(2)}) collective-permute-start(bf16[800,128]{1,0:T(8,128)(2,1)S(1)} %slice.17), channel_id=1, source_target_pairs={{0,16},{8,24},{16,0},{24,8},{1,17},{9,25},{17,1},{25,9},{2,18},{10... | collective-permute-start | bytes 614408 | tf_op jit(solution)/shard_map/grads_node1/ppermute | solution.py:411
  36.3 5.8 %collective-permute-done.4 = bf16[800,128]{1,0:T(8,128)(2,1)S(1)} collective-permute-done((bf16[800,128]{1,0:T(8,128)(2,1)S(1)}, bf16[800,128]{1,0:T(8,128)(2,1)S(1)}, u32[]{:S(2)}, u32[]{:S(2)}) %collective-permute-start.4) | collective-permute-done | bytes 204832 | tf_op jit(solution)/shard_map/grads_node1/ppermute | solution.py:411
  42.2 0.1 add_convert_fusion.1
  42.2 1.8 %collective-permute-start.5 = (bf16[400,128]{1,0:T(8,128)(2,1)S(1)}, bf16[400,128]{1,0:T(8,128)(2,1)S(1)}, u32[]{:S(2)}, u32[]{:S(2)}) collective-permute-start(bf16[400,128]{1,0:T(8,128)(2,1)S(1)} %slice.19), channel_id=1, source_target_pairs={{0,1},{1,0},{2,3},{3,2},{4,5},{5,4},{6,7},{7,6},{8,9},{9,8},{10,11... | collective-permute-start | bytes 307208 | tf_op jit(solution)/shard_map/grads_edge0/ppermute | solution.py:411
  44.0 2.9 %collective-permute-done.5 = bf16[400,128]{1,0:T(8,128)(2,1)S(1)} collective-permute-done((bf16[400,128]{1,0:T(8,128)(2,1)S(1)}, bf16[400,128]{1,0:T(8,128)(2,1)S(1)}, u32[]{:S(2)}, u32[]{:S(2)}) %collective-permute-start.5) | collective-permute-done | bytes 102432 | tf_op jit(solution)/shard_map/grads_edge0/ppermute | solution.py:411
  47.0 1.8 %collective-permute-start.6 = (bf16[400,128]{1,0:T(8,128)(2,1)S(1)}, bf16[400,128]{1,0:T(8,128)(2,1)S(1)}, u32[]{:S(2)}, u32[]{:S(2)}) collective-permute-start(bf16[400,128]{1,0:T(8,128)(2,1)S(1)} %add_convert_fusion.4), channel_id=1, source_target_pairs={{0,2},{1,3},{2,0},{3,1},{4,6},{5,7},{6,4},{7,5},{8,10},{9,11},{10,... | collective-permute-start | bytes 307208 | tf_op jit(solution)/shard_map/grads_edge1/ppermute | solution.py:411
  48.8 2.9 %collective-permute-done.6 = bf16[400,128]{1,0:T(8,128)(2,1)S(1)} collective-permute-done((bf16[400,128]{1,0:T(8,128)(2,1)S(1)}, bf16[400,128]{1,0:T(8,128)(2,1)S(1)}, u32[]{:S(2)}, u32[]{:S(2)}) %collective-permute-start.6) | collective-permute-done | bytes 102432 | tf_op jit(solution)/shard_map/grads_edge1/ppermute | solution.py:411
  51.8 2.8 %collective-permute-start.7 = (bf16[400,128]{1,0:T(8,128)(2,1)S(1)}, bf16[400,128]{1,0:T(8,128)(2,1)S(1)}, u32[]{:S(2)}, u32[]{:S(2)}) collective-permute-start(bf16[400,128]{1,0:T(8,128)(2,1)S(1)} %add_convert_fusion.3), channel_id=1, source_target_pairs={{0,4},{1,5},{2,6},{3,7},{4,0},{5,1},{6,2},{7,3},{8,12},{9,13},{10,... | collective-permute-start | bytes 307208 | tf_op jit(solution)/shard_map/grads_edge2/ppermute | solution.py:411
  54.5 2.8 %collective-permute-done.7 = bf16[400,128]{1,0:T(8,128)(2,1)S(1)} collective-permute-done((bf16[400,128]{1,0:T(8,128)(2,1)S(1)}, bf16[400,128]{1,0:T(8,128)(2,1)S(1)}, u32[]{:S(2)}, u32[]{:S(2)}) %collective-permute-start.7) | collective-permute-done | bytes 102432 | tf_op jit(solution)/shard_map/grads_edge2/ppermute | solution.py:411
  57.4 2.9 %collective-permute-start.8 = (bf16[400,128]{1,0:T(8,128)(2,1)S(1)}, bf16[400,128]{1,0:T(8,128)(2,1)S(1)}, u32[]{:S(2)}, u32[]{:S(2)}) collective-permute-start(bf16[400,128]{1,0:T(8,128)(2,1)S(1)} %add_convert_fusion.2), channel_id=1, source_target_pairs={{0,1},{1,0},{2,3},{3,2},{4,5},{5,4},{6,7},{7,6},{8,9},{9,8},{10,11... | collective-permute-start | bytes 307208 | tf_op jit(solution)/shard_map/grads_back/ppermute | solution.py:411
  60.3 6.0 %slots.1 = (f32[128,1152]{1,0:T(8,128)}, f32[128,1152]{1,0:T(8,128)}) custom-call(s32[4,128]{1,0:T(4,128)} %bitcast.26, bf16[384,384]{1,0:T(8,128)(2,1)} %get-tuple-element.40.zero_w, bf16[512,512]{1,0:T(8,128)(2,1)} %get-tuple-element.41.one_w, bf16[256,256]{1,0:T(8,128)(2,1)} %get-tuple-element.42.two_w, f32[352,128]{1,0:T(8,128)} %get-tuple-element.38.refs_15_.turn, ...), custom_call_target="tpu_custom_call" | custom-call | tf_op jit(solution)/shard_map/slots/slots/pallas_call | solution.py:449
  66.3 4.7 %all-to-all-start.1 = ((f32[8,16,1152]{2,1,0:T(8,128)}), f32[8,16,1152]{2,1,0:T(8,128)S(1)}, u32[]{:S(2)}, u32[]{:S(2)}) async-start(f32[8,16,1152]{2,1,0:T(8,128)} %bitcast.23), calls=%async_computation.1 | async-start | bytes 1179648 | tf_op jit(solution)/shard_map/back/all_to_all | solution.py:460
  71.0 0.0 collective-permute-done.8
  71.0 0.0 copy-done.4
  71.0 0.0 copy-done.5
  71.1 1.2 %multiply_subtract_fusion = (f32[102400]{0:T(1024)}, f32[102400]{0:T(1024)}, f32[102400]{0:T(1024)}) fusion(f32[102400]{0:T(1024)S(1)} %copy-done.1, bf16[400,128]{1,0:T(8,128)(2,1)S(1)} %get-tuple-element.53, bf16[400,128]{1,0:T(8,128)(2,1)S(1)} %get-tuple-element.52, f32[102400]{0:T(1024)S(1)} %copy-done.4, f32[102400]{0:T(1024)S(1)} %copy-done.5), kind=kLoop, calls=%fused_computation.6 | loop fusion | flops 1945600 | bytes 2662400 | tf_op jit(solution)/shard_map/sub | solution.py:406
  72.3 10.6 %all-to-all-done.1 = f32[8,16,1152]{2,1,0:T(8,128)S(1)} async-done(((f32[8,16,1152]{2,1,0:T(8,128)}), f32[8,16,1152]{2,1,0:T(8,128)S(1)}, u32[]{:S(2)}, u32[]{:S(2)}) %all-to-all-start.1) | async-done | bytes 589856 | tf_op jit(solution)/shard_map/back/all_to_all | solution.py:460
  82.8 0.8 copy-done
  83.7 2.4 %finish.1 = bf16[128,1152]{1,0:T(8,128)(2,1)} custom-call(s32[1,128]{1,0:T(1,128)} %bitcast.29, f32[128,1152]{1,0:T(8,128)} %get-tuple-element.45.height_rows_ref, f32[128,1152]{1,0:T(8,128)} %bitcast.20), custom_call_target="tpu_custom_call" | custom-call | tf_op jit(solution)/shard_map/finish/finish/pallas_call | solution.py:449
  (10 shorter events, 0.2 us)
Async XLA Ops:
  0.6 9.3 %copy-start.1 = (f32[102400]{0:T(1024)S(1)}, f32[102400]{0:T(1024)}, u32[]{:S(2)}) copy-start(f32[102400]{0:T(1024)} %param.13) | copy-start | bytes 1228804
  0.6 16.0 %copy-start.9 = (f32[64,9,9]{0,2,1:T(8,128)S(1)}, f32[64,9,9]{0,2,1:T(8,128)}, u32[]{:S(2)}) copy-start(f32[64,9,9]{0,2,1:T(8,128)} %param.19) | copy-start | bytes 62212
  2.7 19.3 %all-to-all-start = ((bf16[8,16,1152]{2,1,0:T(8,128)(2,1)}), bf16[8,16,1152]{2,1,0:T(8,128)(2,1)S(1)}, u32[]{:S(2)}, u32[]{:S(2)}) async-start(bf16[8,16,1152]{2,1,0:T(8,128)(2,1)} %bitcast.21), calls=%async_computation | async-start | bytes 589824 | tf_op jit(solution)/shard_map/rows/all_to_all | solution.py:460
  10.0 8.1 %copy-start.3 = (bf16[800,128]{1,0:T(8,128)(2,1)}, bf16[800,128]{1,0:T(8,128)(2,1)S(1)}, u32[]{:S(2)}) copy-start(bf16[800,128]{1,0:T(8,128)(2,1)S(1)} %convert_bitcast_fusion.refs_4_) | copy-start | bytes 614404
  10.0 6.6 %collective-permute-start.1 = (bf16[800,128]{1,0:T(8,128)(2,1)S(1)}, bf16[800,128]{1,0:T(8,128)(2,1)S(1)}, u32[]{:S(2)}, u32[]{:S(2)}) collective-permute-start(bf16[800,128]{1,0:T(8,128)(2,1)S(1)} %convert_bitcast_fusion.refs_4_), channel_id=1, source_target_pairs={{0,16},{8,24},{16,0},{24,8},{1,17},{9,25},{17,1},{25,9},{2,18},{10... | collective-permute-start | bytes 614408 | tf_op jit(solution)/shard_map/weights/hop1/ppermute | solution.py:411
  11.6 6.4 %collective-permute-start = (bf16[800,128]{1,0:T(8,128)(2,1)S(1)}, bf16[800,128]{1,0:T(8,128)(2,1)S(1)}, u32[]{:S(2)}, u32[]{:S(2)}) collective-permute-start(bf16[800,128]{1,0:T(8,128)(2,1)S(1)} %convert_bitcast_fusion.refs_4_), channel_id=1, source_target_pairs={{0,8},{8,0},{16,24},{24,16},{1,9},{9,1},{17,25},{25,17},{2,10},{10... | collective-permute-start | bytes 614408 | tf_op jit(solution)/shard_map/weights/hop0/ppermute | solution.py:411
  16.6 1.5 %copy-start.6 = (bf16[800,128]{1,0:T(8,128)(2,1)}, bf16[800,128]{1,0:T(8,128)(2,1)S(1)}, u32[]{:S(2)}) copy-start(bf16[800,128]{1,0:T(8,128)(2,1)S(1)} %collective-permute-done.1.refs_6_) | copy-start | bytes 614404
  16.6 1.5 %collective-permute-start.2 = (bf16[800,128]{1,0:T(8,128)(2,1)S(1)}, bf16[800,128]{1,0:T(8,128)(2,1)S(1)}, u32[]{:S(2)}, u32[]{:S(2)}) collective-permute-start(bf16[800,128]{1,0:T(8,128)(2,1)S(1)} %collective-permute-done.1.refs_6_), channel_id=1, source_target_pairs={{0,8},{8,0},{16,24},{24,16},{1,9},{9,1},{17,25},{25,17},{2,10},{10... | collective-permute-start | bytes 614408 | tf_op jit(solution)/shard_map/weights/hop0/ppermute | solution.py:411
  17.9 0.7 copy-start.7
  18.1 0.7 copy-start.8
  22.0 0.7 copy-start.2
  31.6 2.0 %collective-permute-start.3 = (bf16[1600,128]{1,0:T(8,128)(2,1)}, bf16[1600,128]{1,0:T(8,128)(2,1)S(1)}, u32[]{:S(2)}, u32[]{:S(2)}) collective-permute-start(bf16[1600,128]{1,0:T(8,128)(2,1)} %get-tuple-element.48), channel_id=1, source_target_pairs={{0,8},{8,0},{16,24},{24,16},{1,9},{9,1},{17,25},{25,17},{2,10},{10... | collective-permute-start | bytes 1228808 | tf_op jit(solution)/shard_map/grads_node0/ppermute | solution.py:411
  34.7 7.4 %collective-permute-start.4 = (bf16[800,128]{1,0:T(8,128)(2,1)S(1)}, bf16[800,128]{1,0:T(8,128)(2,1)S(1)}, u32[]{:S(2)}, u32[]{:S(2)}) collective-permute-start(bf16[800,128]{1,0:T(8,128)(2,1)S(1)} %slice.17), channel_id=1, source_target_pairs={{0,16},{8,24},{16,0},{24,8},{1,17},{9,25},{17,1},{25,9},{2,18},{10... | collective-permute-start | bytes 614408 | tf_op jit(solution)/shard_map/grads_node1/ppermute | solution.py:411
  42.2 4.7 %collective-permute-start.5 = (bf16[400,128]{1,0:T(8,128)(2,1)S(1)}, bf16[400,128]{1,0:T(8,128)(2,1)S(1)}, u32[]{:S(2)}, u32[]{:S(2)}) collective-permute-start(bf16[400,128]{1,0:T(8,128)(2,1)S(1)} %slice.19), channel_id=1, source_target_pairs={{0,1},{1,0},{2,3},{3,2},{4,5},{5,4},{6,7},{7,6},{8,9},{9,8},{10,11... | collective-permute-start | bytes 307208 | tf_op jit(solution)/shard_map/grads_edge0/ppermute | solution.py:411
  47.0 4.7 %collective-permute-start.6 = (bf16[400,128]{1,0:T(8,128)(2,1)S(1)}, bf16[400,128]{1,0:T(8,128)(2,1)S(1)}, u32[]{:S(2)}, u32[]{:S(2)}) collective-permute-start(bf16[400,128]{1,0:T(8,128)(2,1)S(1)} %add_convert_fusion.4), channel_id=1, source_target_pairs={{0,2},{1,3},{2,0},{3,1},{4,6},{5,7},{6,4},{7,5},{8,10},{9,11},{10,... | collective-permute-start | bytes 307208 | tf_op jit(solution)/shard_map/grads_edge1/ppermute | solution.py:411
  51.8 5.6 %collective-permute-start.7 = (bf16[400,128]{1,0:T(8,128)(2,1)S(1)}, bf16[400,128]{1,0:T(8,128)(2,1)S(1)}, u32[]{:S(2)}, u32[]{:S(2)}) collective-permute-start(bf16[400,128]{1,0:T(8,128)(2,1)S(1)} %add_convert_fusion.3), channel_id=1, source_target_pairs={{0,4},{1,5},{2,6},{3,7},{4,0},{5,1},{6,2},{7,3},{8,12},{9,13},{10,... | collective-permute-start | bytes 307208 | tf_op jit(solution)/shard_map/grads_edge2/ppermute | solution.py:411
  57.4 13.6 %collective-permute-start.8 = (bf16[400,128]{1,0:T(8,128)(2,1)S(1)}, bf16[400,128]{1,0:T(8,128)(2,1)S(1)}, u32[]{:S(2)}, u32[]{:S(2)}) collective-permute-start(bf16[400,128]{1,0:T(8,128)(2,1)S(1)} %add_convert_fusion.2), channel_id=1, source_target_pairs={{0,1},{1,0},{2,3},{3,2},{4,5},{5,4},{6,7},{7,6},{8,9},{9,8},{10,11... | collective-permute-start | bytes 307208 | tf_op jit(solution)/shard_map/grads_back/ppermute | solution.py:411
  66.3 4.7 %copy-start.4 = (f32[102400]{0:T(1024)S(1)}, f32[102400]{0:T(1024)}, u32[]{:S(2)}) copy-start(f32[102400]{0:T(1024)} %param.15) | copy-start | bytes 1228804
  66.3 4.7 %copy-start.5 = (f32[102400]{0:T(1024)S(1)}, f32[102400]{0:T(1024)}, u32[]{:S(2)}) copy-start(f32[102400]{0:T(1024)} %param.14) | copy-start | bytes 1228804
  66.3 16.5 %all-to-all-start.1 = ((f32[8,16,1152]{2,1,0:T(8,128)}), f32[8,16,1152]{2,1,0:T(8,128)S(1)}, u32[]{:S(2)}, u32[]{:S(2)}) async-start(f32[8,16,1152]{2,1,0:T(8,128)} %bitcast.23), calls=%async_computation.1 | async-start | bytes 1179648 | tf_op jit(solution)/shard_map/back/all_to_all | solution.py:460
  82.8 0.8 copy-start

commit v3 on v2

--- a/solution.py
+++ b/solution.py
@@ -6,6 +6,7 @@
 from jax.experimental import pallas as pl
 from jax.experimental.pallas import tpu as pltpu
 from jax.sharding import PartitionSpec as P
+
 
 C = 128
 HARM = 9
@@ -36,7 +37,6 @@
     for col in range(HARM)
     if degree_block[harmonic_order[row]] == degree_block[col]
 ]
-place_of = {(row, col): place for place, (row, col, _) in enumerate(entries)}
 cols_of = [[col for r, col, _ in entries if r == row] for row in range(HARM)]
 rows_of = [[row for row, c, _ in entries if c == col] for col in range(HARM)]
 
@@ -77,8 +77,8 @@
 
 
 def prepare_kernel(node_count, *refs):
-    atoms_ref, cot_ref, index_ref, table_ref = refs[:4]
-    shard_refs = refs[4 : 4 + node_count]
+    live_ref, atoms_ref, cot_ref, index_ref, slot_ref, gain_ref, table_ref = refs[:7]
+    shard_refs = refs[7 : 7 + node_count]
     (
         zero_ref,
         one_ref,
@@ -95,9 +95,14 @@
         atoms_t_ref,
         cot_t_ref,
         turn_ref,
+        slot_out_ref,
+        gain_out_ref,
         packed,
-    ) = refs[4 + node_count :]
+    ) = refs[7 + node_count :]
     atoms_n = atoms_ref.shape[0]
+    slot_out_ref[...] = slot_ref[...]
+    is_live = lax.broadcasted_iota(jnp.int32, (K, atoms_n), 1) < live_ref[0, 0] * TILE_ATOMS
+    gain_out_ref[...] = jnp.where(is_live, gain_ref[...], 0.0) * K**-0.5
     node = lax.axis_index("node")
 
     shard_rows = PACK_ROWS // node_count
@@ -176,28 +181,17 @@
 
 
 def main_kernel(edge_parts, node_count, all_atoms, *refs):
+    rows_ref = refs[0]
+    sides = refs[1:18]
+    output_ref, height_grad, grad_mixed, keep_ref, send_ref, *kept = refs[18:28]
+    held = (*refs[28:40], *kept)
+    (gain_ref, zero_t, one_t, two_t, gate_w, up_w, down_w, gate_t, up_t, down_t, atoms_t, cot_t) = (
+        held[:12]
+    )
+    slot_ref, turn = kept[:2]
     (
-        live_ref,
-        rows_ref,
-        slot_ref,
-        gain_ref,
-        zero_t,
-        one_t,
-        two_t,
-        gate_w,
-        up_w,
-        down_w,
-        gate_t,
-        up_t,
-        down_t,
-        atoms_t,
-        cot_t,
-        turn,
-        output_ref,
-        height_grad,
-        grad_mixed,
-        keep_ref,
-        send_ref,
+        output_rows,
+        arrived,
         source,
         rotated,
         mixed,
@@ -207,17 +201,26 @@
         hidden,
         grad_up,
         packed,
-    ) = refs
+    ) = refs[40:]
+    copies = [
+        pltpu.make_async_copy(side, target, arrived.at[number])
+        for number, (side, target) in enumerate(zip(sides, held))
+    ]
+    early, late = [copies[i] for i in (12, 13, 0)], copies[1:12] + copies[14:]
+    for copy in early + late:
+        copy.start()
+    output_copy = pltpu.make_async_copy(output_rows, output_ref, arrived.at[len(copies)])
     atoms_n = output_ref.shape[0]
     slots_n = rows_ref.shape[0]
     node = lax.axis_index("node")
 
     slot_range = lax.broadcasted_iota(jnp.int32, (slots_n, atoms_n), 0)
+    for copy in early:
+        copy.wait()
     for k in range(K):
         taken = as_low(slot_range == slot_ref[k : k + 1, :])
         source[:, lanes(k, atoms_n)] = dot(rows_ref[...], taken, 0, 0)
-    is_live = lax.broadcasted_iota(jnp.int32, (1, atoms_n), 1) < live_ref[0, 0] * TILE_ATOMS
-    gains = jnp.where(is_live, gain_ref[...], 0.0) * K**-0.5
+    gains = gain_ref[...]
 
     for k in range(K):
         here = lanes(k, atoms_n)
@@ -238,6 +241,8 @@
                 rotated[rows_at(row, first, 2 * SUB), here] = pair.astype(BF16)
 
         over_channels(rotate)
+    for copy in late:
+        copy.wait()
     one_rows = slice(ZERO, ZERO + ONE)
     two_rows = slice(ZERO + ONE, HARM * C)
     mixed[0:ZERO, :] = dot(zero_t[...], rotated[0:ZERO, :])
@@ -283,7 +288,8 @@
     result = height[...] + dot(down_t[...], hidden[...]) * FFH**-0.5
     result = result.astype(BF16)
     for col in range(HARM):
-        output_ref[:, lanes(col)] = result[:, lanes(col, atoms_n)].T
+        output_rows[:, lanes(col)] = result[:, lanes(col, atoms_n)].T
+    output_copy.start()
     grad_hidden = dot(down_w[...], cot_t[...]) * FFH**-0.5
     grad_up[...] = (grad_hidden * gate_each).astype(BF16)
     gate_sum = grad_hidden * up_value[...]
@@ -353,10 +359,11 @@
         values = packed[pl.ds(pl.multiple_of(first, 8), part_rows), :].astype(BF16)
         target = keep_ref if number < half else send_ref
         target[lanes(number % half, part_rows), :] = values
-
-
-def slot_kernel(slot_ref, zero_w, one_w, two_w, turn, grad_mixed, height_grad, *refs):
-    slot_grad_ref, height_rows_ref, mixed, source = refs
+    output_copy.wait()
+
+
+def slot_kernel(slot_ref, turn, zero_w, one_w, two_w, grad_mixed, height_grad, *refs):
+    slot_grad_ref, height_rows_ref, mixed, source, slot_rows, arrived = refs
     slots_n = slot_grad_ref.shape[0]
     atoms_n = slot_ref.shape[1]
     one_rows = slice(ZERO, ZERO + ONE)
@@ -382,9 +389,12 @@
         [as_low(slot_range == slot_ref[k : k + 1, :]) for k in range(K)], axis=1
     )
     pieces = split_parts(source[...], 3)
-    slot_grad_ref[...] = sum(dot(taken, piece, 1, 1) for piece in pieces)
+    slot_rows[...] = sum(dot(taken, piece, 1, 1) for piece in pieces)
+    slot_copy = pltpu.make_async_copy(slot_rows, slot_grad_ref, arrived)
+    slot_copy.start()
     for col in range(HARM):
         height_rows_ref[:, lanes(col)] = height_grad[:, lanes(col, atoms_n)].T
+    slot_copy.wait()
 
 
 def finish_kernel(sends_ref, height_rows_ref, back_ref, grad_ref):
@@ -433,27 +443,36 @@
     per_peer = slots_n // edge_size
     edges_n = atoms_n * K
     edge_parts = 2 if edge_bits else 1
-    vmem = pl.BlockSpec(memory_space=pltpu.VMEM)
-    smem = pl.BlockSpec(memory_space=pltpu.SMEM)
 
     own = params.reshape(-1, C).astype(BF16)
     by_distance = {0: own}
-    with jax.named_scope("weights"):
-        for bit in reversed(range(node_bits)):
-            for distance in list(by_distance):
-                with jax.named_scope(f"hop{bit}"):
-                    by_distance[distance | (1 << bit)] = swap(by_distance[distance], "node", bit)
+    for bit in reversed(range(node_bits)):
+        for distance in list(by_distance):
+            by_distance[distance | (1 << bit)] = swap(by_distance[distance], "node", bit)
     shard_list = [by_distance[distance] for distance in range(node_size)]
 
-    def call(kernel, outs, ins, name, scratch=(), scalars=0):
+    spaces = {"vmem": pltpu.VMEM, "smem": pltpu.SMEM, "hbm": pltpu.HBM, "auto": pltpu.VMEM}
+
+    def call(kernel, outs, ins, scratch=(), megabytes=None):
+        def typed_out(place, shape, dtype):
+            if place in ("vmem", "hbm"):
+                return spaces[place](shape, dtype)
+            return jax.ShapeDtypeStruct(shape, dtype)
+
+        def typed_in(place, value):
+            if place in ("vmem", "hbm"):
+                return pltpu.with_memory_space_constraint(value, spaces[place])
+            return value
+
+        limit = None if megabytes is None else megabytes << 20
         return pl.pallas_call(
             kernel,
-            out_shape=tuple(jax.ShapeDtypeStruct(*out) for out in outs),
-            in_specs=[smem] * scalars + [vmem] * (len(ins) - scalars),
-            out_specs=(vmem,) * len(outs),
-            scratch_shapes=[pltpu.VMEM(*part) for part in scratch],
-            name=name,
-        )(*ins)
+            out_shape=tuple(typed_out(*out) for out in outs),
+            in_specs=[pl.BlockSpec(memory_space=spaces[place]) for place, _ in ins],
+            out_specs=tuple(pl.BlockSpec(memory_space=spaces[out[0]]) for out in outs),
+            scratch_shapes=list(scratch),
+            compiler_params=pltpu.CompilerParams(vmem_limit_bytes=limit),
+        )(*(typed_in(*each_in) for each_in in ins))
 
     def peers_exchange(value):
         value = value.reshape(edge_size, per_peer, features)
@@ -464,67 +483,71 @@
     slots_t, index_t, gains_t = edge_slot.T, rot_index.T, edge_gain.T
     table_t = jnp.transpose(rot_table, (1, 2, 0)).reshape(HARM * HARM, ROTS)
     wide = HARM * atoms_n
-    with jax.named_scope("pick"):
-        (outgoing,) = call(pick_kernel, [((slots_n, features), BF16)], (send_rows, atoms), "pick")
-    with jax.named_scope("rows"):
-        slot_rows = peers_exchange(outgoing)
-    with jax.named_scope("prepare"):
-        prepared = call(
-            functools.partial(prepare_kernel, node_size),
-            [
-                ((ZERO, ZERO), BF16),
-                ((ONE, ONE), BF16),
-                ((TWO, TWO), BF16),
-                ((ZERO, ZERO), BF16),
-                ((ONE, ONE), BF16),
-                ((TWO, TWO), BF16),
-                ((C, FFH), BF16),
-                ((C, FFH), BF16),
-                ((FFH, C), BF16),
-                ((FFH, C), BF16),
-                ((FFH, C), BF16),
-                ((C, FFH), BF16),
-                ((C, wide), BF16),
-                ((C, wide), BF16),
-                ((K * TURN_ROWS, atoms_n), F32),
-            ],
-            (atoms, cotangent, index_t, table_t, *shard_list),
-            "prepare",
-            [((PACK_ROWS, C), F32)],
-        )
-    with jax.named_scope("layer"):
-        output, height_grad, grad_mixed, keep, send = call(
-            functools.partial(main_kernel, edge_parts, node_size, atoms_n * node_size * edge_size),
-            [
-                ((atoms_n, features), BF16),
-                ((C, wide), F32),
-                ((features, edges_n), BF16),
-                ((PACK_ROWS // 2, C), BF16),
-                ((PACK_ROWS // 2, C), BF16),
-            ],
-            (live_tiles, slot_rows, slots_t, gains_t, *prepared[3:]),
-            "layer",
-            [
-                ((features, edges_n), F32),
-                ((features, edges_n), BF16),
-                ((features, edges_n), F32),
-                ((C, wide), F32),
-                ((C, wide), BF16),
-                ((FFH, wide), F32),
-                ((FFH, wide), BF16),
-                ((FFH, wide), BF16),
-                ((PACK_ROWS, C), F32),
-            ],
-            scalars=1,
-        )
-    with jax.named_scope("slots"):
-        slot_grad, height_rows = call(
-            slot_kernel,
-            [((slots_n, features), F32), ((atoms_n, features), F32)],
-            (slots_t, *prepared[:3], prepared[-1], grad_mixed, height_grad),
-            "slots",
-            [((features, edges_n), F32), ((features, edges_n), F32)],
-        )
+    (outgoing,) = call(
+        pick_kernel, [("auto", (slots_n, features), BF16)], [("auto", send_rows), ("auto", atoms)]
+    )
+    slot_rows = peers_exchange(outgoing)
+    matrix_shapes = [(ZERO, ZERO), (ONE, ONE), (TWO, TWO)]
+    side_shapes = matrix_shapes + [(C, FFH)] * 2 + [(FFH, C)] * 3 + [(C, FFH)] + [(C, wide)] * 2
+    prepared = call(
+        functools.partial(prepare_kernel, node_size),
+        [("auto", shape, BF16) for shape in matrix_shapes + side_shapes]
+        + [
+            ("auto", (K * TURN_ROWS, atoms_n), F32),
+            ("auto", (K, atoms_n), jnp.int32),
+            ("auto", (K, atoms_n), F32),
+        ],
+        [("smem", live_tiles)]
+        + [("auto", value) for value in (atoms, cotangent, index_t, slots_t, gains_t, table_t)]
+        + [("auto", value) for value in shard_list],
+        [pltpu.VMEM((PACK_ROWS, C), F32)],
+    )
+    matrices, sides, (turn, slots_kept, gains_kept) = prepared[:3], prepared[3:-3], prepared[-3:]
+    forwarded = (slots_kept, turn, *matrices)
+    output, height_grad, grad_mixed, keep, send, *kept = call(
+        functools.partial(main_kernel, edge_parts, node_size, atoms_n * node_size * edge_size),
+        [
+            ("hbm", (atoms_n, features), BF16),
+            ("vmem", (C, wide), F32),
+            ("vmem", (features, edges_n), BF16),
+            ("vmem", (PACK_ROWS // 2, C), BF16),
+            ("vmem", (PACK_ROWS // 2, C), BF16),
+        ]
+        + [("vmem", value.shape, value.dtype) for value in forwarded],
+        [("vmem", slot_rows)]
+        + [("hbm", value) for value in (gains_kept, *sides, *forwarded)],
+        [
+            pltpu.VMEM((K, atoms_n), F32),
+            *(pltpu.VMEM(shape, BF16) for shape in side_shapes),
+            pltpu.VMEM((atoms_n, features), BF16),
+            pltpu.SemaphoreType.DMA((len(side_shapes) + len(forwarded) + 2,)),
+            pltpu.VMEM((features, edges_n), F32),
+            pltpu.VMEM((features, edges_n), BF16),
+            pltpu.VMEM((features, edges_n), F32),
+            pltpu.VMEM((C, wide), F32),
+            pltpu.VMEM((C, wide), BF16),
+            pltpu.VMEM((FFH, wide), F32),
+            pltpu.VMEM((FFH, wide), BF16),
+            pltpu.VMEM((FFH, wide), BF16),
+            pltpu.VMEM((PACK_ROWS, C), F32),
+        ],
+        megabytes=28,
+    )
+    slot_grad, height_rows = call(
+        slot_kernel,
+        [("hbm", (slots_n, features), F32), ("vmem", (atoms_n, features), F32)],
+        [
+            ("vmem", value)
+            for value in (*kept, grad_mixed, height_grad)
+        ],
+        [
+            pltpu.VMEM((features, edges_n), F32),
+            pltpu.VMEM((features, edges_n), F32),
+            pltpu.VMEM((slots_n, features), F32),
+            pltpu.SemaphoreType.DMA,
+        ],
+        megabytes=20,
+    )
 
     def add_low(left, right):
         return (left.astype(F32) + right.astype(F32)).astype(BF16)
@@ -534,29 +557,24 @@
         if number:
             half = keep.shape[0] // 2
             keep, send = keep[:half], keep[half:]
-        with jax.named_scope(f"grads_{axis}{bit}"):
-            keep = add_low(keep, swap(send, axis, bit))
+        keep = add_low(keep, swap(send, axis, bit))
     grads = keep
     for bit in range(1, edge_bits):
-        with jax.named_scope(f"grads_edge{bit}"):
-            grads = add_low(grads, swap(grads, "edge", bit))
+        grads = add_low(grads, swap(grads, "edge", bit))
     if edge_bits:
-        with jax.named_scope("grads_back"):
-            other = swap(grads, "edge", 0)
+        other = swap(grads, "edge", 0)
         is_low = (lax.axis_index("edge") & 1) == 0
         grads = jnp.concatenate(
             [jnp.where(is_low, grads, other), jnp.where(is_low, other, grads)], axis=0
         )
 
-    with jax.named_scope("back"):
-        returned = peers_exchange(slot_grad)
-    with jax.named_scope("finish"):
-        (grad_atoms,) = call(
-            finish_kernel,
-            [((atoms_n, features), BF16)],
-            (send_rows, height_rows, returned),
-            "finish",
-        )
+    returned = peers_exchange(slot_grad)
+    (grad_atoms,) = call(
+        finish_kernel,
+        [("auto", (atoms_n, features), BF16)],
+        [("auto", send_rows), ("vmem", height_rows), ("vmem", returned)],
+        megabytes=8,
+    )
 
     def rows_of_lanes(value):
         return value.reshape(-1, C)

time: 86.6 us -> 81.8 us (0.945)
  Pallas kernels: 22.5 us -> 18.1 us
  waiting for transfers between devices: 31.8 us -> 30.6 us
    pallas_call x5, Pallas kernels: 22.5 us -> 18.1 us  [call(): pl.pallas_call(kernel, out_shape=tuple((typed_out(*out) for out in outs))...]
    all_to_all x2, waiting for transfers between devices: 10.6 us -> 9.61 us  [peers_exchange(): lax.all_to_all(value, 'edge', split_axis=0, concat_axis=0, tiled=True)]
    select_n x1, other arithmetic: 0.03 us -> 0.97 us  [shards(): jnp.where(is_low, grads, other)]
    unnamed x20 -> x28, local copies, waits for them, and re-layouts: 2.25 us -> 2.57 us
  transfers between devices with their start and end apart: 11 -> 11, of which waited for: 8 -> 8; matrix products, arithmetic and copies ran while one was open for 2% -> 4% of each run, Pallas kernels for 11% -> 9%
where the time goes in v3:
time: 81.8 us; the launch traced here: 81.4 us
  waiting for transfers between devices  30.6 us (37%)
  starting transfers between devices  24.8 us (30%)
  Pallas kernels  18.1 us (22%)
  local copies, waits for them, and re-layouts  3.26 us (4%)
  other arithmetic  3.1 us (4%)
  between operations  1.5 us (2%)
    ppermute x9, waiting for transfers between devices, swap(): return lax.ppermute(value, axis, [(i, i ^ 1 << bit) for i in range(size)])  21 us
    pallas_call x5, Pallas kernels, call(): pl.pallas_call(kernel, out_shape=tuple((typed_out(*out) for out in outs))...  18.1 us
    ppermute x9, starting transfers between devices, swap(): return lax.ppermute(value, axis, [(i, i ^ 1 << bit) for i in range(size)])  12.9 us
    all_to_all x2, starting transfers between devices, peers_exchange(): lax.all_to_all(value, 'edge', split_axis=0, concat_axis=0, tiled=True)  12 us
    all_to_all x2, waiting for transfers between devices, peers_exchange(): lax.all_to_all(value, 'edge', split_axis=0, concat_axis=0, tiled=True)  9.61 us
    unnamed x28, local copies, waits for them, and re-layouts  2.57 us
  transfers between devices with their start and end apart: 11, of which 8 were waited for; matrix products, arithmetic and copies ran while one was open for 4% of the time, Pallas kernels for 9%

profile of v3, /device:TPU:0, one launch (start us, length us, event | category | flops | bytes accessed | tf_op | source)
XLA Modules:
  0.0 81.4 jit_solution(2450784464105429521)
XLA Ops:
  0.6 0.0 copy-start.5
  0.7 2.0 %shard_map.146 = bf16[128,1152]{1,0:T(8,128)(2,1)} custom-call(s32[1,128]{1,0:T(1,128)} %bitcast.22, bf16[128,1152]{1,0:T(8,128)(2,1)} %refs_1_.1), custom_call_target="tpu_custom_call" | custom-call | tf_op jit(solution)/shard_map/pallas_call | solution.py:468
  2.7 7.3 %all-to-all-start = ((bf16[8,16,1152]{2,1,0:T(8,128)(2,1)}), bf16[8,16,1152]{2,1,0:T(8,128)(2,1)S(1)}, u32[]{:S(2)}, u32[]{:S(2)}) async-start(bf16[8,16,1152]{2,1,0:T(8,128)(2,1)} %bitcast.24), calls=%async_computation | async-start | bytes 589824 | tf_op jit(solution)/shard_map/all_to_all | solution.py:479
  10.0 0.0 copy-start.7
  10.0 1.6 %collective-permute-start.1 = (bf16[800,128]{1,0:T(8,128)(2,1)S(1)}, bf16[800,128]{1,0:T(8,128)(2,1)S(1)}, u32[]{:S(2)}, u32[]{:S(2)}) collective-permute-start(bf16[800,128]{1,0:T(8,128)(2,1)S(1)} %convert_bitcast_fusion.refs_7_), channel_id=1, source_target_pairs={{0,16},{8,24},{16,0},{24,8},{1,17},{9,25},{17,1},{25,9},{2,18},{10... | collective-permute-start | bytes 614408 | tf_op jit(solution)/shard_map/ppermute | solution.py:421
  11.6 0.0 collective-permute-start
  11.6 5.0 %collective-permute-done.1.refs_9_ = bf16[800,128]{1,0:T(8,128)(2,1)S(1)} collective-permute-done((bf16[800,128]{1,0:T(8,128)(2,1)S(1)}, bf16[800,128]{1,0:T(8,128)(2,1)S(1)}, u32[]{:S(2)}, u32[]{:S(2)}) %collective-permute-start.1) | collective-permute-done | bytes 204832 | tf_op jit(solution)/shard_map/ppermute | solution.py:421
  16.6 0.0 collective-permute-start.2
  16.6 0.0 copy-done.13
  16.6 0.7 reshape.44.refs_6_
  17.9 0.0 collective-permute-done.refs_8_
  17.9 0.0 copy-start.11
  17.9 0.1 collective-permute-done.2.refs_10_
  18.1 0.0 copy-done.7
  18.1 0.6 copy-done.11
  18.6 0.1 copy-done.12
  18.7 3.3 %shard_map.147 = (bf16[384,384]{1,0:T(8,128)(2,1)}, bf16[512,512]{1,0:T(8,128)(2,1)}, bf16[256,256]{1,0:T(8,128)(2,1)}, bf16[384,384]{1,0:T(8,128)(2,1)}, bf16[5...) custom-call(s32[1,1]{1,0:T(1,128)S(6)} %copy.16.refs_0_, ...), custom_call_target="tpu_custom_call" | custom-call | tf_op jit(solution)/shard_map/pallas_call | solution.py:468
  22.0 0.0 all-to-all-done
  22.1 7.6 %shard_map.148 = (bf16[128,1152]{1,0:T(8,128)(2,1)}, f32[128,1152]{1,0:T(8,128)S(1)}, bf16[1152,512]{1,0:T(8,128)(2,1)S(1)}, bf16[1600,128]{1,0:T(8,128)(2,1)S(1...) custom-call(bf16[128,1152]{1,0:T(8,128)(2,1)S(1)} %bitcast.21, ...), custom_call_target="tpu_custom_call" | custom-call | tf_op jit(solution)/shard_map/pallas_call | solution.py:468
  29.7 0.0 copy-start
  29.7 0.0 copy-start.2
  29.7 0.5 collective-permute-start.3
  30.1 1.4 %collective-permute-done.3 = bf16[1600,128]{1,0:T(8,128)(2,1)S(1)} collective-permute-done((bf16[1600,128]{1,0:T(8,128)(2,1)S(1)}, bf16[1600,128]{1,0:T(8,128)(2,1)S(1)}, u32[]{:S(2)}, u32[]{:S(2)}) %collective-permute-start.3) | collective-permute-done | bytes 409632 | tf_op jit(solution)/shard_map/ppermute | solution.py:421
  31.5 0.1 add_convert_fusion
  31.7 1.6 %collective-permute-start.4 = (bf16[800,128]{1,0:T(8,128)(2,1)S(1)}, bf16[800,128]{1,0:T(8,128)(2,1)S(1)}, u32[]{:S(2)}, u32[]{:S(2)}) collective-permute-start(bf16[800,128]{1,0:T(8,128)(2,1)S(1)} %slice.17), channel_id=1, source_target_pairs={{0,16},{8,24},{16,0},{24,8},{1,17},{9,25},{17,1},{25,9},{2,18},{10... | collective-permute-start | bytes 614408 | tf_op jit(solution)/shard_map/ppermute | solution.py:421
  33.2 5.8 %collective-permute-done.4 = bf16[800,128]{1,0:T(8,128)(2,1)S(1)} collective-permute-done((bf16[800,128]{1,0:T(8,128)(2,1)S(1)}, bf16[800,128]{1,0:T(8,128)(2,1)S(1)}, u32[]{:S(2)}, u32[]{:S(2)}) %collective-permute-start.4) | collective-permute-done | bytes 204832 | tf_op jit(solution)/shard_map/ppermute | solution.py:421
  39.1 0.1 add_convert_fusion.1
  39.2 1.8 %collective-permute-start.5 = (bf16[400,128]{1,0:T(8,128)(2,1)S(1)}, bf16[400,128]{1,0:T(8,128)(2,1)S(1)}, u32[]{:S(2)}, u32[]{:S(2)}) collective-permute-start(bf16[400,128]{1,0:T(8,128)(2,1)S(1)} %slice.19), channel_id=1, source_target_pairs={{0,1},{1,0},{2,3},{3,2},{4,5},{5,4},{6,7},{7,6},{8,9},{9,8},{10,11... | collective-permute-start | bytes 307208 | tf_op jit(solution)/shard_map/ppermute | solution.py:421
  41.0 2.9 %collective-permute-done.5 = bf16[400,128]{1,0:T(8,128)(2,1)S(1)} collective-permute-done((bf16[400,128]{1,0:T(8,128)(2,1)S(1)}, bf16[400,128]{1,0:T(8,128)(2,1)S(1)}, u32[]{:S(2)}, u32[]{:S(2)}) %collective-permute-start.5) | collective-permute-done | bytes 102432 | tf_op jit(solution)/shard_map/ppermute | solution.py:421
  43.9 1.8 %collective-permute-start.6 = (bf16[400,128]{1,0:T(8,128)(2,1)S(1)}, bf16[400,128]{1,0:T(8,128)(2,1)S(1)}, u32[]{:S(2)}, u32[]{:S(2)}) collective-permute-start(bf16[400,128]{1,0:T(8,128)(2,1)S(1)} %add_convert_fusion.4), channel_id=1, source_target_pairs={{0,2},{1,3},{2,0},{3,1},{4,6},{5,7},{6,4},{7,5},{8,10},{9,11},{10,... | collective-permute-start | bytes 307208 | tf_op jit(solution)/shard_map/ppermute | solution.py:421
  45.7 2.9 %collective-permute-done.6 = bf16[400,128]{1,0:T(8,128)(2,1)S(1)} collective-permute-done((bf16[400,128]{1,0:T(8,128)(2,1)S(1)}, bf16[400,128]{1,0:T(8,128)(2,1)S(1)}, u32[]{:S(2)}, u32[]{:S(2)}) %collective-permute-start.6) | collective-permute-done | bytes 102432 | tf_op jit(solution)/shard_map/ppermute | solution.py:421
  48.7 2.8 %collective-permute-start.7 = (bf16[400,128]{1,0:T(8,128)(2,1)S(1)}, bf16[400,128]{1,0:T(8,128)(2,1)S(1)}, u32[]{:S(2)}, u32[]{:S(2)}) collective-permute-start(bf16[400,128]{1,0:T(8,128)(2,1)S(1)} %add_convert_fusion.3), channel_id=1, source_target_pairs={{0,4},{1,5},{2,6},{3,7},{4,0},{5,1},{6,2},{7,3},{8,12},{9,13},{10,... | collective-permute-start | bytes 307208 | tf_op jit(solution)/shard_map/ppermute | solution.py:421
  51.5 2.8 %collective-permute-done.7 = bf16[400,128]{1,0:T(8,128)(2,1)S(1)} collective-permute-done((bf16[400,128]{1,0:T(8,128)(2,1)S(1)}, bf16[400,128]{1,0:T(8,128)(2,1)S(1)}, u32[]{:S(2)}, u32[]{:S(2)}) %collective-permute-start.7) | collective-permute-done | bytes 102432 | tf_op jit(solution)/shard_map/ppermute | solution.py:421
  54.3 0.7 add_convert_fusion.2
  55.0 2.8 %collective-permute-start.8 = (bf16[400,128]{1,0:T(8,128)(2,1)}, bf16[400,128]{1,0:T(8,128)(2,1)}, u32[]{:S(2)}, u32[]{:S(2)}) collective-permute-start(bf16[400,128]{1,0:T(8,128)(2,1)} %add_convert_fusion.2), channel_id=1, source_target_pairs={{0,1},{1,0},{2,3},{3,2},{4,5},{5,4},{6,7},{7,6},{8,9},{9,8},{10,11... | collective-permute-start | bytes 307208 | tf_op jit(solution)/shard_map/ppermute | solution.py:421
  57.8 0.9 %copy-done.1 = f32[352,128]{1,0:T(8,128)S(1)} copy-done((f32[352,128]{1,0:T(8,128)S(1)}, f32[352,128]{1,0:T(8,128)}, u32[]{:S(2)}) %copy-start.1) | copy-done | bytes 180248
  58.7 0.9 %copy-done.3 = bf16[256,256]{1,0:T(8,128)(2,1)S(1)} copy-done((bf16[256,256]{1,0:T(8,128)(2,1)S(1)}, bf16[256,256]{1,0:T(8,128)(2,1)}, u32[]{:S(2)}) %copy-start.3) | copy-done | bytes 131096
  59.7 4.0 %shard_map.149 = (f32[128,1152]{1,0:T(8,128)}, f32[128,1152]{1,0:T(8,128)S(1)}) custom-call(s32[4,128]{1,0:T(4,128)S(1)} %get-tuple-element.52.slot_ref, f32[352,128]{1,0:T(8,128)S(1)} %copy-done.1, bf16[384,384]{1,0:T(8,128)(2,1)S(1)} %get-tuple-element.54.zero_w, bf16[512,512]{1,0:T(8,128)(2,1)S(1)} %get-tuple-element.55.one_w, ...), custom_call_target="tpu_custom_call" | custom-call | tf_op jit(solution)/shard_map/pallas_call | solution.py:468
  63.7 0.0 copy-start.6
  63.7 0.0 copy-start.8
  63.7 0.0 copy-start.9
  63.7 4.7 %all-to-all-start.1 = ((f32[8,16,1152]{2,1,0:T(8,128)}), f32[8,16,1152]{2,1,0:T(8,128)S(1)}, u32[]{:S(2)}, u32[]{:S(2)}) async-start(f32[8,16,1152]{2,1,0:T(8,128)} %bitcast.25), calls=%async_computation.1 | async-start | bytes 1179648 | tf_op jit(solution)/shard_map/all_to_all | solution.py:479
  68.4 0.0 collective-permute-done.8
  68.4 1.0 %broadcast_select_fusion.1 = (bf16[400,128]{1,0:T(8,128)(2,1)S(1)}, bf16[400,128]{1,0:T(8,128)(2,1)S(1)}) fusion(bf16[400,128]{1,0:T(8,128)(2,1)} %add_convert_fusion.2, bf16[400,128]{1,0:T(8,128)(2,1)} %collective-permute-done.8, pred[]{:T(512)S(6)} %eq.3), kind=kLoop, calls=%fused_computation.14 | loop fusion | flops 102400 | bytes 409601 | tf_op jit(solution)/shard_map/jit(_where)/select_n | solution.py:568
  69.4 0.0 copy-start.4
  69.4 1.2 %multiply_subtract_fusion = (f32[102400]{0:T(1024)}, f32[102400]{0:T(1024)}, f32[102400]{0:T(1024)}) fusion(f32[102400]{0:T(1024)S(1)} %copy-done.6, bf16[400,128]{1,0:T(8,128)(2,1)S(1)} %get-tuple-element.67, bf16[400,128]{1,0:T(8,128)(2,1)S(1)} %get-tuple-element.66, f32[102400]{0:T(1024)S(1)} %copy-done.8, f32[102400]{0:T(1024)S(1)} %copy-done.9), kind=kLoop, calls=%fused_computation.6 | loop fusion | flops 1945600 | bytes 2662400 | tf_op jit(solution)/shard_map/sub | solution.py:416
  70.6 9.6 %all-to-all-done.1 = f32[8,16,1152]{2,1,0:T(8,128)S(1)} async-done(((f32[8,16,1152]{2,1,0:T(8,128)}), f32[8,16,1152]{2,1,0:T(8,128)S(1)}, u32[]{:S(2)}, u32[]{:S(2)}) %all-to-all-start.1) | async-done | bytes 589856 | tf_op jit(solution)/shard_map/all_to_all | solution.py:479
  80.3 1.1 %shard_map.150 = bf16[128,1152]{1,0:T(8,128)(2,1)} custom-call(s32[1,128]{1,0:T(1,128)S(1)} %bitcast.23, f32[128,1152]{1,0:T(8,128)S(1)} %get-tuple-element.59.height_rows_ref, f32[128,1152]{1,0:T(8,128)S(1)} %bitcast.20), custom_call_target="tpu_custom_call" | custom-call | tf_op jit(solution)/shard_map/pallas_call | solution.py:468
  (18 shorter events, 0.1 us)
Async XLA Ops:
  0.6 9.3 %copy-start.5 = (f32[102400]{0:T(1024)S(1)}, f32[102400]{0:T(1024)}, u32[]{:S(2)}) copy-start(f32[102400]{0:T(1024)} %param.13) | copy-start | bytes 1228804
  0.6 16.0 %copy-start.13 = (f32[64,9,9]{0,2,1:T(8,128)S(1)}, f32[64,9,9]{0,2,1:T(8,128)}, u32[]{:S(2)}) copy-start(f32[64,9,9]{0,2,1:T(8,128)} %param.19) | copy-start | bytes 62212
  2.7 19.4 %all-to-all-start = ((bf16[8,16,1152]{2,1,0:T(8,128)(2,1)}), bf16[8,16,1152]{2,1,0:T(8,128)(2,1)S(1)}, u32[]{:S(2)}, u32[]{:S(2)}) async-start(bf16[8,16,1152]{2,1,0:T(8,128)(2,1)} %bitcast.24), calls=%async_computation | async-start | bytes 589824 | tf_op jit(solution)/shard_map/all_to_all | solution.py:479
  10.0 8.1 %copy-start.7 = (bf16[800,128]{1,0:T(8,128)(2,1)}, bf16[800,128]{1,0:T(8,128)(2,1)S(1)}, u32[]{:S(2)}) copy-start(bf16[800,128]{1,0:T(8,128)(2,1)S(1)} %convert_bitcast_fusion.refs_7_) | copy-start | bytes 614404
  10.0 6.6 %collective-permute-start.1 = (bf16[800,128]{1,0:T(8,128)(2,1)S(1)}, bf16[800,128]{1,0:T(8,128)(2,1)S(1)}, u32[]{:S(2)}, u32[]{:S(2)}) collective-permute-start(bf16[800,128]{1,0:T(8,128)(2,1)S(1)} %convert_bitcast_fusion.refs_7_), channel_id=1, source_target_pairs={{0,16},{8,24},{16,0},{24,8},{1,17},{9,25},{17,1},{25,9},{2,18},{10... | collective-permute-start | bytes 614408 | tf_op jit(solution)/shard_map/ppermute | solution.py:421
  11.6 6.3 %collective-permute-start = (bf16[800,128]{1,0:T(8,128)(2,1)S(1)}, bf16[800,128]{1,0:T(8,128)(2,1)S(1)}, u32[]{:S(2)}, u32[]{:S(2)}) collective-permute-start(bf16[800,128]{1,0:T(8,128)(2,1)S(1)} %convert_bitcast_fusion.refs_7_), channel_id=1, source_target_pairs={{0,8},{8,0},{16,24},{24,16},{1,9},{9,1},{17,25},{25,17},{2,10},{10... | collective-permute-start | bytes 614408 | tf_op jit(solution)/shard_map/ppermute | solution.py:421
  16.6 1.5 %copy-start.10 = (bf16[800,128]{1,0:T(8,128)(2,1)}, bf16[800,128]{1,0:T(8,128)(2,1)S(1)}, u32[]{:S(2)}) copy-start(bf16[800,128]{1,0:T(8,128)(2,1)S(1)} %collective-permute-done.1.refs_9_) | copy-start | bytes 614404
  16.6 1.5 %collective-permute-start.2 = (bf16[800,128]{1,0:T(8,128)(2,1)S(1)}, bf16[800,128]{1,0:T(8,128)(2,1)S(1)}, u32[]{:S(2)}, u32[]{:S(2)}) collective-permute-start(bf16[800,128]{1,0:T(8,128)(2,1)S(1)} %collective-permute-done.1.refs_9_), channel_id=1, source_target_pairs={{0,8},{8,0},{16,24},{24,16},{1,9},{9,1},{17,25},{25,17},{2,10},{10... | collective-permute-start | bytes 614408 | tf_op jit(solution)/shard_map/ppermute | solution.py:421
  17.9 0.7 copy-start.11
  18.1 0.7 copy-start.12
  29.7 9.5 %copy-start = (f32[352,128]{1,0:T(8,128)}, f32[352,128]{1,0:T(8,128)S(1)}, u32[]{:S(2)}) copy-start(f32[352,128]{1,0:T(8,128)S(1)} %get-tuple-element.53.turn) | copy-start | bytes 540676
  29.7 9.5 %copy-start.2 = (bf16[256,256]{1,0:T(8,128)(2,1)}, bf16[256,256]{1,0:T(8,128)(2,1)S(1)}, u32[]{:S(2)}) copy-start(bf16[256,256]{1,0:T(8,128)(2,1)S(1)} %get-tuple-element.56.two_w) | copy-start | bytes 393220
  29.7 1.8 %collective-permute-start.3 = (bf16[1600,128]{1,0:T(8,128)(2,1)S(1)}, bf16[1600,128]{1,0:T(8,128)(2,1)S(1)}, u32[]{:S(2)}, u32[]{:S(2)}) collective-permute-start(bf16[1600,128]{1,0:T(8,128)(2,1)S(1)} %get-tuple-element.62), channel_id=1, source_target_pairs={{0,8},{8,0},{16,24},{24,16},{1,9},{9,1},{17,25},{25,17},{2,10},{10... | collective-permute-start | bytes 1228808 | tf_op jit(solution)/shard_map/ppermute | solution.py:421
  31.7 7.4 %collective-permute-start.4 = (bf16[800,128]{1,0:T(8,128)(2,1)S(1)}, bf16[800,128]{1,0:T(8,128)(2,1)S(1)}, u32[]{:S(2)}, u32[]{:S(2)}) collective-permute-start(bf16[800,128]{1,0:T(8,128)(2,1)S(1)} %slice.17), channel_id=1, source_target_pairs={{0,16},{8,24},{16,0},{24,8},{1,17},{9,25},{17,1},{25,9},{2,18},{10... | collective-permute-start | bytes 614408 | tf_op jit(solution)/shard_map/ppermute | solution.py:421
  39.2 4.7 %collective-permute-start.5 = (bf16[400,128]{1,0:T(8,128)(2,1)S(1)}, bf16[400,128]{1,0:T(8,128)(2,1)S(1)}, u32[]{:S(2)}, u32[]{:S(2)}) collective-permute-start(bf16[400,128]{1,0:T(8,128)(2,1)S(1)} %slice.19), channel_id=1, source_target_pairs={{0,1},{1,0},{2,3},{3,2},{4,5},{5,4},{6,7},{7,6},{8,9},{9,8},{10,11... | collective-permute-start | bytes 307208 | tf_op jit(solution)/shard_map/ppermute | solution.py:421
  43.9 4.7 %collective-permute-start.6 = (bf16[400,128]{1,0:T(8,128)(2,1)S(1)}, bf16[400,128]{1,0:T(8,128)(2,1)S(1)}, u32[]{:S(2)}, u32[]{:S(2)}) collective-permute-start(bf16[400,128]{1,0:T(8,128)(2,1)S(1)} %add_convert_fusion.4), channel_id=1, source_target_pairs={{0,2},{1,3},{2,0},{3,1},{4,6},{5,7},{6,4},{7,5},{8,10},{9,11},{10,... | collective-permute-start | bytes 307208 | tf_op jit(solution)/shard_map/ppermute | solution.py:421
  48.7 5.6 %collective-permute-start.7 = (bf16[400,128]{1,0:T(8,128)(2,1)S(1)}, bf16[400,128]{1,0:T(8,128)(2,1)S(1)}, u32[]{:S(2)}, u32[]{:S(2)}) collective-permute-start(bf16[400,128]{1,0:T(8,128)(2,1)S(1)} %add_convert_fusion.3), channel_id=1, source_target_pairs={{0,4},{1,5},{2,6},{3,7},{4,0},{5,1},{6,2},{7,3},{8,12},{9,13},{10,... | collective-permute-start | bytes 307208 | tf_op jit(solution)/shard_map/ppermute | solution.py:421
  55.0 13.4 %collective-permute-start.8 = (bf16[400,128]{1,0:T(8,128)(2,1)}, bf16[400,128]{1,0:T(8,128)(2,1)}, u32[]{:S(2)}, u32[]{:S(2)}) collective-permute-start(bf16[400,128]{1,0:T(8,128)(2,1)} %add_convert_fusion.2), channel_id=1, source_target_pairs={{0,1},{1,0},{2,3},{3,2},{4,5},{5,4},{6,7},{7,6},{8,9},{9,8},{10,11... | collective-permute-start | bytes 307208 | tf_op jit(solution)/shard_map/ppermute | solution.py:421
  57.8 0.9 %copy-start.1 = (f32[352,128]{1,0:T(8,128)S(1)}, f32[352,128]{1,0:T(8,128)}, u32[]{:S(2)}) copy-start(f32[352,128]{1,0:T(8,128)} %copy-done) | copy-start | bytes 540676
  58.7 0.9 %copy-start.3 = (bf16[256,256]{1,0:T(8,128)(2,1)S(1)}, bf16[256,256]{1,0:T(8,128)(2,1)}, u32[]{:S(2)}) copy-start(bf16[256,256]{1,0:T(8,128)(2,1)} %copy-done.2) | copy-start | bytes 393220
  63.7 5.7 %copy-start.6 = (f32[102400]{0:T(1024)S(1)}, f32[102400]{0:T(1024)}, u32[]{:S(2)}) copy-start(f32[102400]{0:T(1024)} %param.13) | copy-start | bytes 1228804
  63.7 5.7 %copy-start.8 = (f32[102400]{0:T(1024)S(1)}, f32[102400]{0:T(1024)}, u32[]{:S(2)}) copy-start(f32[102400]{0:T(1024)} %param.15) | copy-start | bytes 1228804
  63.7 5.7 %copy-start.9 = (f32[102400]{0:T(1024)S(1)}, f32[102400]{0:T(1024)}, u32[]{:S(2)}) copy-start(f32[102400]{0:T(1024)} %param.14) | copy-start | bytes 1228804
  63.7 16.5 %all-to-all-start.1 = ((f32[8,16,1152]{2,1,0:T(8,128)}), f32[8,16,1152]{2,1,0:T(8,128)S(1)}, u32[]{:S(2)}, u32[]{:S(2)}) async-start(f32[8,16,1152]{2,1,0:T(8,128)} %bitcast.25), calls=%async_computation.1 | async-start | bytes 1179648 | tf_op jit(solution)/shard_map/all_to_all | solution.py:479
  69.4 10.8 %copy-start.4 = (s32[1,1,128]{2,1,0:T(1,128)S(1)}, s32[1,1,128]{2,1,0:T(1,128)}, u32[]{:S(2)}) copy-start(s32[1,1,128]{2,1,0:T(1,128)} %param.16) | copy-start | bytes 1540

commit v4 on v3

--- a/solution.py
+++ b/solution.py
@@ -16,6 +16,7 @@
 ROTS = 64
 SUB = 8
 TURN_ROWS = 88
+GROUPS = 2
 
 harmonic_order = (0, 2, 6, 3, 7, 1, 5, 8, 4)
 norm_epsilon = 1e-06
@@ -70,15 +71,33 @@
     return jnp.where(mask, 1.0, 0.0).astype(BF16)
 
 
-def pick_kernel(sends_ref, atoms_ref, rows_ref):
+def pick_kernel(sends_ref, atoms_ref, params_ref, rows_ref, own_ref):
     shape = (atoms_ref.shape[0], sends_ref.shape[1])
     picks = as_low(lax.broadcasted_iota(jnp.int32, shape, 0) == sends_ref[...])
     rows_ref[...] = dot(picks, atoms_ref[...], 0, 0).astype(BF16)
-
-
-def prepare_kernel(node_count, *refs):
-    live_ref, atoms_ref, cot_ref, index_ref, slot_ref, gain_ref, table_ref = refs[:7]
-    shard_refs = refs[7 : 7 + node_count]
+    own_ref[...] = params_ref[...].astype(BF16)
+
+
+def arrange_kernel(live_ref, atoms_ref, cot_ref, index_ref, gain_ref, table_ref, *outs):
+    atoms_t_ref, cot_t_ref, turn_ref, gain_out_ref = outs
+    atoms_n = atoms_ref.shape[0]
+    is_live = lax.broadcasted_iota(jnp.int32, (K, atoms_n), 1) < live_ref[0, 0] * TILE_ATOMS
+    gain_out_ref[...] = jnp.where(is_live, gain_ref[...], 0.0) * K**-0.5
+    for col in range(HARM):
+        atoms_t_ref[:, lanes(col, atoms_n)] = atoms_ref[:, lanes(col)].T
+        cot_t_ref[:, lanes(col, atoms_n)] = cot_ref[:, lanes(col)].T
+    pieces = split_parts(table_ref[...], 3)
+    range_of_table = lax.broadcasted_iota(jnp.int32, (ROTS, atoms_n), 0)
+    for k in range(K):
+        chosen = as_low(range_of_table == index_ref[k : k + 1, :])
+        turn_ref[pl.ds(k * TURN_ROWS, HARM * HARM), :] = sum(dot(piece, chosen) for piece in pieces)
+
+
+def unpack_kernel(node_count, *refs):
+    shard_refs = refs[:node_count]
+    out_refs = refs[node_count : node_count + 12]
+    built = refs[node_count + 12 : node_count + 24]
+    packed, arrived = refs[node_count + 24 :]
     (
         zero_ref,
         one_ref,
@@ -92,17 +111,11 @@
         gate_t_ref,
         up_t_ref,
         down_t_ref,
-        atoms_t_ref,
-        cot_t_ref,
-        turn_ref,
-        slot_out_ref,
-        gain_out_ref,
-        packed,
-    ) = refs[7 + node_count :]
-    atoms_n = atoms_ref.shape[0]
-    slot_out_ref[...] = slot_ref[...]
-    is_live = lax.broadcasted_iota(jnp.int32, (K, atoms_n), 1) < live_ref[0, 0] * TILE_ATOMS
-    gain_out_ref[...] = jnp.where(is_live, gain_ref[...], 0.0) * K**-0.5
+    ) = built
+    copies = [
+        pltpu.make_async_copy(source, target, arrived.at[number])
+        for number, (source, target) in enumerate(zip(built, out_refs))
+    ]
     node = lax.axis_index("node")
 
     shard_rows = PACK_ROWS // node_count
@@ -114,50 +127,51 @@
         for part in range(width):
             first = piece_start[piece] + part
             block = packed[pl.ds(first, rows, stride=width), :].astype(BF16)
+            turned_block = block.T
             for target, turned, row, col, sign in targets:
-                value = block if sign > 0 else -block
+                value = turned_block if turned else block
+                value = value if sign > 0 else -value
                 if turned:
-                    target[col + part * C : col + (part + 1) * C, row : row + rows] = value.T
+                    target[col + part * C : col + (part + 1) * C, row : row + rows] = value
                 else:
                     target[row : row + rows, col + part * C : col + (part + 1) * C] = value
 
     half = 2 * C
-    unpack(0, ZERO, 3, (zero_ref, False, 0, 0, 1), (zero_t_ref, True, 0, 0, 1))
-    for piece, (matrix, turned, rows) in (
-        (1, (one_ref, one_t_ref, half)),
-        (3, (two_ref, two_t_ref, C)),
+    unpack(0, ZERO, 3, (zero_t_ref, True, 0, 0, 1), (zero_ref, False, 0, 0, 1))
+    copies[3].start()
+    copies[0].start()
+    for piece, matrix, turned, rows, places in (
+        (1, one_ref, one_t_ref, half, (1, 4)),
+        (3, two_ref, two_t_ref, C, (2, 5)),
     ):
         width = rows // C
         unpack(
             piece,
             rows,
             width,
+            (turned, True, 0, 0, 1),
+            (turned, True, rows, rows, 1),
             (matrix, False, 0, 0, 1),
             (matrix, False, rows, rows, 1),
-            (turned, True, 0, 0, 1),
-            (turned, True, rows, rows, 1),
         )
         unpack(
             piece + 1,
             rows,
             width,
+            (turned, True, 0, rows, 1),
+            (turned, True, rows, 0, -1),
             (matrix, False, 0, rows, 1),
             (matrix, False, rows, 0, -1),
-            (turned, True, 0, rows, 1),
-            (turned, True, rows, 0, -1),
         )
+        for place in places:
+            copies[place].start()
     unpack(5, C, 2, (gate_ref, False, 0, 0, 1), (gate_t_ref, True, 0, 0, 1))
     unpack(6, C, 2, (up_ref, False, 0, 0, 1), (up_t_ref, True, 0, 0, 1))
     unpack(7, FFH, 1, (down_ref, False, 0, 0, 1), (down_t_ref, True, 0, 0, 1))
-
-    for col in range(HARM):
-        atoms_t_ref[:, lanes(col, atoms_n)] = atoms_ref[:, lanes(col)].T
-        cot_t_ref[:, lanes(col, atoms_n)] = cot_ref[:, lanes(col)].T
-    pieces = split_parts(table_ref[...], 3)
-    range_of_table = lax.broadcasted_iota(jnp.int32, (ROTS, atoms_n), 0)
-    for k in range(K):
-        chosen = as_low(range_of_table == index_ref[k : k + 1, :])
-        turn_ref[pl.ds(k * TURN_ROWS, HARM * HARM), :] = sum(dot(piece, chosen) for piece in pieces)
+    for copy in copies[6:]:
+        copy.start()
+    for copy in copies:
+        copy.wait()
 
 
 def turns_of(turn_ref, k, factors=None):
@@ -170,25 +184,27 @@
 
 def over_channels(body):
     def step(number, carry):
-        body(pl.multiple_of(number * 2 * SUB, 2 * SUB))
+        for part in range(GROUPS):
+            body(pl.multiple_of((number * GROUPS + part) * 2 * SUB, 2 * SUB))
         return carry
 
-    lax.fori_loop(0, C // (2 * SUB), step, 0)
-
-
-def rows_at(harmonic, first, count=SUB):
-    return pl.ds(pl.multiple_of(harmonic * C + first, SUB), count)
+    lax.fori_loop(0, C // (2 * SUB * GROUPS), step, 0)
+
+
+def flat(value):
+    return value.reshape(value.shape[0] * value.shape[1], value.shape[2])
+
+
+ZERO_PART, ONE_PART, TWO_PART = slice(0, 3), slice(3, 7), slice(7, 9)
 
 
 def main_kernel(edge_parts, node_count, all_atoms, *refs):
     rows_ref = refs[0]
-    sides = refs[1:18]
-    output_ref, height_grad, grad_mixed, keep_ref, send_ref, *kept = refs[18:28]
-    held = (*refs[28:40], *kept)
-    (gain_ref, zero_t, one_t, two_t, gate_w, up_w, down_w, gate_t, up_t, down_t, atoms_t, cot_t) = (
-        held[:12]
-    )
-    slot_ref, turn = kept[:2]
+    sides = refs[1:15]
+    output_ref, height_grad, grad_mixed, keep_ref, send_ref = refs[15:20]
+    held = refs[20:34]
+    slot_ref, turn, gain_ref = held[:3]
+    (zero_t, one_t, two_t, gate_w, up_w, down_w, gate_t, up_t, down_t, atoms_t, cot_t) = held[3:]
     (
         output_rows,
         arrived,
@@ -201,12 +217,12 @@
         hidden,
         grad_up,
         packed,
-    ) = refs[40:]
+    ) = refs[34:]
     copies = [
         pltpu.make_async_copy(side, target, arrived.at[number])
         for number, (side, target) in enumerate(zip(sides, held))
     ]
-    early, late = [copies[i] for i in (12, 13, 0)], copies[1:12] + copies[14:]
+    early, late = copies[:3], copies[3:]
     for copy in early + late:
         copy.start()
     output_copy = pltpu.make_async_copy(output_rows, output_ref, arrived.at[len(copies)])
@@ -217,9 +233,10 @@
     slot_range = lax.broadcasted_iota(jnp.int32, (slots_n, atoms_n), 0)
     for copy in early:
         copy.wait()
-    for k in range(K):
-        taken = as_low(slot_range == slot_ref[k : k + 1, :])
-        source[:, lanes(k, atoms_n)] = dot(rows_ref[...], taken, 0, 0)
+    taken = jnp.concatenate(
+        [as_low(slot_range == slot_ref[k : k + 1, :]) for k in range(K)], axis=1
+    )
+    source[...] = dot(rows_ref[...], taken, 0, 0).reshape(source.shape)
     gains = gain_ref[...]
 
     for k in range(K):
@@ -229,7 +246,7 @@
         def rotate(first, here=here, turns=turns):
             halves = []
             for start in (0, SUB):
-                values = [source[rows_at(col, first + start), here] for col in range(HARM)]
+                values = [source[col, pl.ds(first + start, SUB), here] for col in range(HARM)]
                 halves.append(
                     [
                         sum(turns[row, col] * values[col] for col in cols_of[row])
@@ -238,16 +255,13 @@
                 )
             for row in range(HARM):
                 pair = jnp.concatenate([halves[0][row], halves[1][row]], axis=0)
-                rotated[rows_at(row, first, 2 * SUB), here] = pair.astype(BF16)
+                rotated[row, pl.ds(first, 2 * SUB), here] = pair.astype(BF16)
 
         over_channels(rotate)
     for copy in late:
         copy.wait()
-    one_rows = slice(ZERO, ZERO + ONE)
-    two_rows = slice(ZERO + ONE, HARM * C)
-    mixed[0:ZERO, :] = dot(zero_t[...], rotated[0:ZERO, :])
-    mixed[one_rows, :] = dot(one_t[...], rotated[one_rows, :])
-    mixed[two_rows, :] = dot(two_t[...], rotated[two_rows, :])
+    for part, matrix in ((ZERO_PART, zero_t), (ONE_PART, one_t), (TWO_PART, two_t)):
+        mixed[part] = dot(matrix[...], flat(rotated[part])).reshape(mixed[part].shape)
 
     for k in range(K):
         here = lanes(k, atoms_n)
@@ -261,8 +275,8 @@
                     for col in range(HARM)
                 ]
             for start in (0, SUB):
-                values = [mixed[rows_at(row, first + start), here] for row in range(HARM)]
-                target = pl.ds(pl.multiple_of(first + start, SUB), SUB)
+                values = [mixed[row, pl.ds(first + start, SUB), here] for row in range(HARM)]
+                target = pl.ds(first + start, SUB)
                 for col in range(HARM):
                     there = lanes(col, atoms_n)
                     base = starts[col][start : start + SUB] if k == 0 else height[target, there]
@@ -282,18 +296,24 @@
     inverse = lax.rsqrt(mean + norm_epsilon)
     normed_low[...] = (height[...] * each(inverse)).astype(BF16)
     gate = jax.nn.sigmoid(dot(gate_t[...], normed_low[:, 0:atoms_n]) * C**-0.5)
-    gate_each = each(gate)
-    up_value[...] = dot(up_t[...], normed_low[...]) * C**-0.5
-    hidden[...] = (up_value[...] * gate_each).astype(BF16)
-    result = height[...] + dot(down_t[...], hidden[...]) * FFH**-0.5
-    result = result.astype(BF16)
+    up_gate, down_gate = gate * C**-0.5, gate * FFH**-0.5
+    up_value[...] = dot(up_t[...], normed_low[...])
     for col in range(HARM):
-        output_rows[:, lanes(col)] = result[:, lanes(col, atoms_n)].T
+        here = lanes(col, atoms_n)
+        hidden[:, here] = (up_value[:, here] * up_gate).astype(BF16)
+    projected = dot(down_t[...], hidden[...])
+    for col in range(HARM):
+        here = lanes(col, atoms_n)
+        result = (height[:, here] + projected[:, here] * FFH**-0.5).astype(BF16)
+        output_rows[:, lanes(col)] = result.T
     output_copy.start()
-    grad_hidden = dot(down_w[...], cot_t[...]) * FFH**-0.5
-    grad_up[...] = (grad_hidden * gate_each).astype(BF16)
-    gate_sum = grad_hidden * up_value[...]
-    gate_sum = sum(gate_sum[:, lanes(col, atoms_n)] for col in range(HARM))
+    gate_sum = jnp.zeros_like(gate)
+    for col in range(HARM):
+        here = lanes(col, atoms_n)
+        grad_hidden = dot(down_w[...], cot_t[:, here])
+        grad_up[:, here] = (grad_hidden * down_gate).astype(BF16)
+        gate_sum = gate_sum + grad_hidden * up_value[:, here]
+    gate_sum = gate_sum * (C**-0.5 * FFH**-0.5)
     grad_gate = (gate_sum * gate * (1.0 - gate)).astype(BF16)
     along = dot(up_w[...], grad_up[...]) * C**-0.5
     gate_along = dot(gate_w[...], grad_gate) * C**-0.5
@@ -311,7 +331,7 @@
         def rotate_grads(first, here=here, turns=turns):
             halves = []
             for start in (0, SUB):
-                target = pl.ds(pl.multiple_of(first + start, SUB), SUB)
+                target = pl.ds(first + start, SUB)
                 values = [height_grad[target, lanes(col, atoms_n)] for col in range(HARM)]
                 halves.append(
                     [
@@ -321,7 +341,7 @@
                 )
             for row in range(HARM):
                 pair = jnp.concatenate([halves[0][row], halves[1][row]], axis=0)
-                grad_mixed[rows_at(row, first, 2 * SUB), here] = pair.astype(BF16)
+                grad_mixed[row, pl.ds(first, 2 * SUB), here] = pair.astype(BF16)
 
         over_channels(rotate_grads)
     boost = grad_boost * all_atoms**-0.5
@@ -333,13 +353,13 @@
     def weight_grad(left, right, scale):
         return dot(left, right, 1, 1) * (scale * boost)
 
-    zero_grad = weight_grad(rotated[0:ZERO, :], grad_mixed[0:ZERO, :], row_scale[0])
+    zero_grad = weight_grad(flat(rotated[ZERO_PART]), flat(grad_mixed[ZERO_PART]), row_scale[0])
     pack_piece(0, ZERO, 3, zero_grad)
-    one_grad = weight_grad(rotated[one_rows, :], grad_mixed[one_rows, :], row_scale[3])
+    one_grad = weight_grad(flat(rotated[ONE_PART]), flat(grad_mixed[ONE_PART]), row_scale[3])
     half = 2 * C
     pack_piece(1, half, 2, one_grad[:half, :half] + one_grad[half:, half:])
     pack_piece(2, half, 2, one_grad[:half, half:] - one_grad[half:, :half])
-    two_grad = weight_grad(rotated[two_rows, :], grad_mixed[two_rows, :], row_scale[7])
+    two_grad = weight_grad(flat(rotated[TWO_PART]), flat(grad_mixed[TWO_PART]), row_scale[7])
     pack_piece(3, C, 1, two_grad[:C, :C] + two_grad[C:, C:])
     pack_piece(4, C, 1, two_grad[:C, C:] - two_grad[C:, :C])
     pack_piece(5, C, 2, weight_grad(normed_low[:, 0:atoms_n], grad_gate, C**-0.5))
@@ -362,38 +382,56 @@
     output_copy.wait()
 
 
-def slot_kernel(slot_ref, turn, zero_w, one_w, two_w, grad_mixed, height_grad, *refs):
-    slot_grad_ref, height_rows_ref, mixed, source, slot_rows, arrived = refs
+def slot_kernel(grad_mixed, height_grad, *refs):
+    sides, held = refs[:5], refs[7:12]
+    slot_grad_ref, height_rows_ref = refs[5:7]
+    zero_w, one_w, two_w, turn, slot_ref = held
+    mixed, source_high, source_low, slot_rows, arrived = refs[12:]
+    copies = [
+        pltpu.make_async_copy(side, target, arrived.at[number])
+        for number, (side, target) in enumerate(zip(sides, held))
+    ]
+    for copy in copies:
+        copy.start()
     slots_n = slot_grad_ref.shape[0]
     atoms_n = slot_ref.shape[1]
-    one_rows = slice(ZERO, ZERO + ONE)
-    two_rows = slice(ZERO + ONE, HARM * C)
-    mixed[0:ZERO, :] = dot(zero_w[...], grad_mixed[0:ZERO, :])
-    mixed[one_rows, :] = dot(one_w[...], grad_mixed[one_rows, :])
-    mixed[two_rows, :] = dot(two_w[...], grad_mixed[two_rows, :])
+    for col in range(HARM):
+        height_rows_ref[:, lanes(col)] = height_grad[:, lanes(col, atoms_n)].T
+    parts = ((ZERO_PART, zero_w), (ONE_PART, one_w), (TWO_PART, two_w))
+    for (part, matrix), copy in zip(parts, copies):
+        copy.wait()
+        mixed[part] = dot(matrix[...], flat(grad_mixed[part])).reshape(mixed[part].shape)
+    for copy in copies[3:]:
+        copy.wait()
     for k in range(K):
         here = lanes(k, atoms_n)
         turns = turns_of(turn, k, row_scale)
 
         def rotate_back(first, here=here, turns=turns):
+            halves = []
             for start in (0, SUB):
-                values = [mixed[rows_at(row, first + start), here] for row in range(HARM)]
-                for col in range(HARM):
-                    source[rows_at(col, first + start), here] = sum(
-                        turns[row, col] * values[row] for row in rows_of[col]
-                    )
+                values = [mixed[row, pl.ds(first + start, SUB), here] for row in range(HARM)]
+                halves.append(
+                    [
+                        sum(turns[row, col] * values[row] for row in rows_of[col])
+                        for col in range(HARM)
+                    ]
+                )
+            for col in range(HARM):
+                pair = jnp.concatenate([halves[0][col], halves[1][col]], axis=0)
+                for target, part in zip((source_high, source_low), split_parts(pair, 2)):
+                    target[col, pl.ds(first, 2 * SUB), here] = part
 
         over_channels(rotate_back)
     slot_range = lax.broadcasted_iota(jnp.int32, (slots_n, atoms_n), 0)
     taken = jnp.concatenate(
         [as_low(slot_range == slot_ref[k : k + 1, :]) for k in range(K)], axis=1
     )
-    pieces = split_parts(source[...], 3)
-    slot_rows[...] = sum(dot(taken, piece, 1, 1) for piece in pieces)
-    slot_copy = pltpu.make_async_copy(slot_rows, slot_grad_ref, arrived)
+    slot_rows[...] = dot(taken, flat(source_high[...]), 1, 1) + dot(
+        taken, flat(source_low[...]), 1, 1
+    )
+    slot_copy = pltpu.make_async_copy(slot_rows, slot_grad_ref, arrived.at[len(copies)])
     slot_copy.start()
-    for col in range(HARM):
-        height_rows_ref[:, lanes(col)] = height_grad[:, lanes(col, atoms_n)].T
     slot_copy.wait()
 
 
@@ -419,6 +457,16 @@
 def swap(value, axis, bit):
     size = lax.axis_size(axis)
     return lax.ppermute(value, axis, [(i, i ^ (1 << bit)) for i in range(size)])
+
+
+def swap_both(value, node_step, edge_step):
+    nodes, edges = lax.axis_size("node"), lax.axis_size("edge")
+    pairs = [
+        (n * edges + e, (n ^ node_step) * edges + (e ^ edge_step))
+        for n in range(nodes)
+        for e in range(edges)
+    ]
+    return lax.ppermute(value, ("node", "edge"), pairs)
 
 
 def shards(
@@ -442,14 +490,7 @@
     slots_n = sends.shape[-1]
     per_peer = slots_n // edge_size
     edges_n = atoms_n * K
-    edge_parts = 2 if edge_bits else 1
-
-    own = params.reshape(-1, C).astype(BF16)
-    by_distance = {0: own}
-    for bit in reversed(range(node_bits)):
-        for distance in list(by_distance):
-            by_distance[distance | (1 << bit)] = swap(by_distance[distance], "node", bit)
-    shard_list = [by_distance[distance] for distance in range(node_size)]
+    edge_parts = 2
 
     spaces = {"vmem": pltpu.VMEM, "smem": pltpu.SMEM, "hbm": pltpu.HBM, "auto": pltpu.VMEM}
 
@@ -483,47 +524,60 @@
     slots_t, index_t, gains_t = edge_slot.T, rot_index.T, edge_gain.T
     table_t = jnp.transpose(rot_table, (1, 2, 0)).reshape(HARM * HARM, ROTS)
     wide = HARM * atoms_n
-    (outgoing,) = call(
-        pick_kernel, [("auto", (slots_n, features), BF16)], [("auto", send_rows), ("auto", atoms)]
+    outgoing, own = call(
+        pick_kernel,
+        [("auto", (slots_n, features), BF16), ("auto", (PACK_ROWS // node_size, C), BF16)],
+        [("auto", value) for value in (send_rows, atoms, params.reshape(-1, C))],
     )
     slot_rows = peers_exchange(outgoing)
+    by_distance = {0: own}
+    for bit in reversed(range(node_bits)):
+        for distance in list(by_distance):
+            by_distance[distance | (1 << bit)] = swap(by_distance[distance], "node", bit)
     matrix_shapes = [(ZERO, ZERO), (ONE, ONE), (TWO, TWO)]
-    side_shapes = matrix_shapes + [(C, FFH)] * 2 + [(FFH, C)] * 3 + [(C, FFH)] + [(C, wide)] * 2
-    prepared = call(
-        functools.partial(prepare_kernel, node_size),
-        [("auto", shape, BF16) for shape in matrix_shapes + side_shapes]
-        + [
+    unpacked_shapes = matrix_shapes * 2 + [(C, FFH)] * 2 + [(FFH, C)] * 3 + [(C, FFH)]
+    atoms_t, cot_t, turn, gains_kept = call(
+        arrange_kernel,
+        [
+            ("auto", (C, wide), BF16),
+            ("auto", (C, wide), BF16),
             ("auto", (K * TURN_ROWS, atoms_n), F32),
-            ("auto", (K, atoms_n), jnp.int32),
             ("auto", (K, atoms_n), F32),
         ],
         [("smem", live_tiles)]
-        + [("auto", value) for value in (atoms, cotangent, index_t, slots_t, gains_t, table_t)]
-        + [("auto", value) for value in shard_list],
-        [pltpu.VMEM((PACK_ROWS, C), F32)],
-    )
-    matrices, sides, (turn, slots_kept, gains_kept) = prepared[:3], prepared[3:-3], prepared[-3:]
-    forwarded = (slots_kept, turn, *matrices)
-    output, height_grad, grad_mixed, keep, send, *kept = call(
+        + [("auto", value) for value in (atoms, cotangent, index_t, gains_t, table_t)],
+    )
+    unpacked = call(
+        functools.partial(unpack_kernel, node_size),
+        [("hbm", shape, BF16) for shape in unpacked_shapes],
+        [("vmem", by_distance[distance]) for distance in range(node_size)],
+        [
+            *(pltpu.VMEM(shape, BF16) for shape in unpacked_shapes),
+            pltpu.VMEM((PACK_ROWS, C), F32),
+            pltpu.SemaphoreType.DMA((len(unpacked_shapes),)),
+        ],
+        megabytes=16,
+    )
+    sides = (slots_t, turn, gains_kept, *unpacked[3:], atoms_t, cot_t)
+    read_again = (*unpacked[:3], turn, slots_t)
+    output, height_grad, grad_mixed, keep, send = call(
         functools.partial(main_kernel, edge_parts, node_size, atoms_n * node_size * edge_size),
         [
             ("hbm", (atoms_n, features), BF16),
             ("vmem", (C, wide), F32),
-            ("vmem", (features, edges_n), BF16),
+            ("vmem", (HARM, C, edges_n), BF16),
             ("vmem", (PACK_ROWS // 2, C), BF16),
             ("vmem", (PACK_ROWS // 2, C), BF16),
-        ]
-        + [("vmem", value.shape, value.dtype) for value in forwarded],
+        ],
         [("vmem", slot_rows)]
-        + [("hbm", value) for value in (gains_kept, *sides, *forwarded)],
+        + [("hbm", value) for value in sides],
         [
-            pltpu.VMEM((K, atoms_n), F32),
-            *(pltpu.VMEM(shape, BF16) for shape in side_shapes),
+            *(pltpu.VMEM(value.shape, value.dtype) for value in sides),
             pltpu.VMEM((atoms_n, features), BF16),
-            pltpu.SemaphoreType.DMA((len(side_shapes) + len(forwarded) + 2,)),
-            pltpu.VMEM((features, edges_n), F32),
-            pltpu.VMEM((features, edges_n), BF16),
-            pltpu.VMEM((features, edges_n), F32),
+            pltpu.SemaphoreType.DMA((len(sides) + 1,)),
+            pltpu.VMEM((HARM, C, edges_n), F32),
+            pltpu.VMEM((HARM, C, edges_n), BF16),
+            pltpu.VMEM((HARM, C, edges_n), F32),
             pltpu.VMEM((C, wide), F32),
             pltpu.VMEM((C, wide), BF16),
             pltpu.VMEM((FFH, wide), F32),
@@ -536,15 +590,15 @@
     slot_grad, height_rows = call(
         slot_kernel,
         [("hbm", (slots_n, features), F32), ("vmem", (atoms_n, features), F32)],
+        [("vmem", grad_mixed), ("vmem", height_grad)]
+        + [("hbm", value) for value in read_again],
         [
-            ("vmem", value)
-            for value in (*kept, grad_mixed, height_grad)
-        ],
-        [
-            pltpu.VMEM((features, edges_n), F32),
-            pltpu.VMEM((features, edges_n), F32),
+            *(pltpu.VMEM(value.shape, value.dtype) for value in read_again),
+            pltpu.VMEM((HARM, C, edges_n), F32),
+            pltpu.VMEM((HARM, C, edges_n), BF16),
+            pltpu.VMEM((HARM, C, edges_n), BF16),
             pltpu.VMEM((slots_n, features), F32),
-            pltpu.SemaphoreType.DMA,
+            pltpu.SemaphoreType.DMA((len(read_again) + 1,)),
         ],
         megabytes=20,
     )
@@ -552,21 +606,28 @@
     def add_low(left, right):
         return (left.astype(F32) + right.astype(F32)).astype(BF16)
 
-    hops = [("node", bit) for bit in range(node_bits)] + [("edge", 0)] * (edge_parts - 1)
-    for number, (axis, bit) in enumerate(hops):
-        if number:
+    for bit in range(node_bits - 1):
+        if bit:
             half = keep.shape[0] // 2
             keep, send = keep[:half], keep[half:]
-        keep = add_low(keep, swap(send, axis, bit))
-    grads = keep
+        keep = add_low(keep, swap(send, "node", bit))
+    quarter = keep.shape[0] // 4
+    total = keep[:quarter].astype(F32)
+    for number in (2, 3, 1):
+        came = swap_both(
+            keep[number * quarter : (number + 1) * quarter],
+            (number >> 1) << (node_bits - 1),
+            number & 1,
+        )
+        total = total + came.astype(F32)
+    grads = total.astype(BF16)
     for bit in range(1, edge_bits):
         grads = add_low(grads, swap(grads, "edge", bit))
-    if edge_bits:
-        other = swap(grads, "edge", 0)
-        is_low = (lax.axis_index("edge") & 1) == 0
-        grads = jnp.concatenate(
-            [jnp.where(is_low, grads, other), jnp.where(is_low, other, grads)], axis=0
-        )
+    other = swap(grads, "edge", 0)
+    is_low = (lax.axis_index("edge") & 1) == 0
+    grads = jnp.concatenate(
+        [jnp.where(is_low, grads, other), jnp.where(is_low, other, grads)], axis=0
+    )
 
     returned = peers_exchange(slot_grad)
     (grad_atoms,) = call(

time: 81.8 us -> 77.7 us (0.950)
  local copies, waits for them, and re-layouts: 3.26 us -> 0.68 us
  other arithmetic: 3.1 us -> 1.48 us
  Pallas kernels: 18.1 us -> 19.6 us
  waiting for transfers between devices: 30.6 us -> 29.1 us
    ppermute x9 -> x7, waiting for transfers between devices: 21 us -> 12.6 us  [swap(): return lax.ppermute(value, axis, [(i, i ^ 1 << bit) for i in range(size)])]
    ppermute x0 -> x3, waiting for transfers between devices: none -> 5.16 us  [swap_both(): return lax.ppermute(value, ('node', 'edge'), pairs)]
    ppermute x9 -> x7, starting transfers between devices: 12.9 us -> 9.32 us  [swap(): return lax.ppermute(value, axis, [(i, i ^ 1 << bit) for i in range(size)])]
    ppermute x0 -> x3, starting transfers between devices: none -> 3.55 us  [swap_both(): return lax.ppermute(value, ('node', 'edge'), pairs)]
    unnamed x28 -> x12, local copies, waits for them, and re-layouts: 2.57 us -> 0.03 us
    all_to_all x2, waiting for transfers between devices: 9.61 us -> 11.4 us  [peers_exchange(): lax.all_to_all(value, 'edge', split_axis=0, concat_axis=0, tiled=True)]
    pallas_call x5 -> x6, Pallas kernels: 18.1 us -> 19.6 us  [call(): pl.pallas_call(kernel, out_shape=tuple((typed_out(*out) for out in outs))...]
    select_n x1, other arithmetic: 0.97 us -> 0.03 us  [shards(): jnp.where(is_low, grads, other)]
  transfers between devices with their start and end apart: 11 -> 12, of which waited for: 8 -> 8; matrix products, arithmetic and copies ran while one was open for 4% -> 2% of each run, Pallas kernels for 9% -> 12%
where the time goes in v4:
time: 77.7 us; the launch traced here: 77.3 us
  waiting for transfers between devices  29.1 us (37%)
  starting transfers between devices  25 us (32%)
  Pallas kernels  19.6 us (25%)
  other arithmetic  1.48 us (2%)
  between operations  1.43 us (2%)
    pallas_call x6, Pallas kernels, call(): pl.pallas_call(kernel, out_shape=tuple((typed_out(*out) for out in outs))...  19.6 us
    ppermute x7, waiting for transfers between devices, swap(): return lax.ppermute(value, axis, [(i, i ^ 1 << bit) for i in range(size)])  12.6 us
    all_to_all x2, starting transfers between devices, peers_exchange(): lax.all_to_all(value, 'edge', split_axis=0, concat_axis=0, tiled=True)  12.1 us
    all_to_all x2, waiting for transfers between devices, peers_exchange(): lax.all_to_all(value, 'edge', split_axis=0, concat_axis=0, tiled=True)  11.4 us
    ppermute x7, starting transfers between devices, swap(): return lax.ppermute(value, axis, [(i, i ^ 1 << bit) for i in range(size)])  9.32 us
    ppermute x3, waiting for transfers between devices, swap_both(): return lax.ppermute(value, ('node', 'edge'), pairs)  5.16 us
    ppermute x3, starting transfers between devices, swap_both(): return lax.ppermute(value, ('node', 'edge'), pairs)  3.55 us
  transfers between devices with their start and end apart: 12, of which 8 were waited for; matrix products, arithmetic and copies ran while one was open for 2% of the time, Pallas kernels for 12%

profile of v4, /device:TPU:0, one launch (start us, length us, event | category | flops | bytes accessed | tf_op | source)
XLA Modules:
  0.0 77.3 jit_solution(7417168333720919451)
XLA Ops:
  0.6 0.0 copy-start.5
  0.6 2.1 %shard_map.146 = (bf16[128,1152]{1,0:T(8,128)(2,1)}, bf16[800,128]{1,0:T(8,128)(2,1)}) custom-call(s32[1,128]{1,0:T(1,128)} %bitcast.21, bf16[128,1152]{1,0:T(8,128)(2,1)} %atoms_ref.3, f32[800,128]{1,0:T(8,128)} %bitcast.23), custom_call_target="tpu_custom_call" | custom-call | tf_op jit(solution)/shard_map/pallas_call | solution.py:509
  2.8 0.0 copy-start
  2.8 7.4 %all-to-all-start = ((bf16[8,16,1152]{2,1,0:T(8,128)(2,1)}), bf16[8,16,1152]{2,1,0:T(8,128)(2,1)S(1)}, u32[]{:S(2)}, u32[]{:S(2)}) async-start(bf16[8,16,1152]{2,1,0:T(8,128)(2,1)} %bitcast.25), calls=%async_computation | async-start | bytes 589824 | tf_op jit(solution)/shard_map/all_to_all | solution.py:520
  10.2 1.5 %collective-permute-start.1 = (bf16[800,128]{1,0:T(8,128)(2,1)}, bf16[800,128]{1,0:T(8,128)(2,1)S(1)}, u32[]{:S(2)}, u32[]{:S(2)}) collective-permute-start(bf16[800,128]{1,0:T(8,128)(2,1)} %get-tuple-element.33.refs_0_), channel_id=1, source_target_pairs={{0,16},{8,24},{16,0},{24,8},{1,17},{9,25},{17,1},{25,9},{2,18},{10... | collective-permute-start | bytes 614408 | tf_op jit(solution)/shard_map/ppermute | solution.py:459
  11.7 0.0 collective-permute-start
  11.7 5.2 %collective-permute-done.1.refs_2_ = bf16[800,128]{1,0:T(8,128)(2,1)S(1)} collective-permute-done((bf16[800,128]{1,0:T(8,128)(2,1)}, bf16[800,128]{1,0:T(8,128)(2,1)S(1)}, u32[]{:S(2)}, u32[]{:S(2)}) %collective-permute-start.1) | collective-permute-done | bytes 204832 | tf_op jit(solution)/shard_map/ppermute | solution.py:459
  16.9 0.0 collective-permute-start.2
  16.9 0.0 copy-done.5
  16.9 0.6 reshape.46.table_ref
  18.2 2.2 %shard_map.147 = (bf16[128,1152]{1,0:T(8,128)(2,1)}, bf16[128,1152]{1,0:T(8,128)(2,1)}, f32[352,128]{1,0:T(8,128)}, f32[4,128]{1,0:T(4,128)}) custom-call(s32[1,1]{1,0:T(1,128)S(6)} %copy.16.live_ref, bf16[128,1152]{1,0:T(8,128)(2,1)} %atoms_ref.3, bf16[128,1152]{1,0:T(8,128)(2,1)} %cot_ref.1, s32[4,128]{1,0:T(4,128)} %bitcast.29, f32[4,128]{1,0:T(4,128)} %bitcast.30, ...), custom_call_target="tpu_custom_call" | custom-call | tf_op jit(solution)/shard_map/pallas_call | solution.py:509
  20.4 0.0 collective-permute-done.refs_1_
  20.4 0.0 collective-permute-done.2.refs_3_
  20.4 0.0 copy-done
  20.4 1.8 %shard_map.148 = (bf16[384,384]{1,0:T(8,128)(2,1)}, bf16[512,512]{1,0:T(8,128)(2,1)}, bf16[256,256]{1,0:T(8,128)(2,1)}, bf16[384,384]{1,0:T(8,128)(2,1)}, bf16[5...) custom-call(bf16[800,128]{1,0:T(8,128)(2,1)S(1)} %copy-done, ...), custom_call_target="tpu_custom_call" | custom-call | tf_op jit(solution)/shard_map/pallas_call | solution.py:509
  22.2 0.0 all-to-all-done
  22.2 7.3 %shard_map.149 = (bf16[128,1152]{1,0:T(8,128)(2,1)}, f32[128,1152]{1,0:T(8,128)S(1)}, bf16[9,128,512]{2,1,0:T(8,128)(2,1)S(1)}, bf16[1600,128]{1,0:T(8,128)(2,1)S(1)}, bf16[1600,128]{1,0:T(8,128)(2,1)S(1)}) custom-call(bf16[128,1152]{1,0:T(8,128)(2,1)S(1)} %bitcast.20, s32[4,128]{1,0:T(4,128)} %bitcast.27, f32[352,128]{1,0:T(8,128)} %get-tuple-element.31.refs_2_.refs_3_, ...), custom_call_target="tpu_custom_call" | custom-call | tf_op jit(solution)/shard_map/pallas_call | solution.py:509
  29.5 0.6 collective-permute-start.3
  30.1 1.4 %collective-permute-done.3 = bf16[1600,128]{1,0:T(8,128)(2,1)S(1)} collective-permute-done((bf16[1600,128]{1,0:T(8,128)(2,1)S(1)}, bf16[1600,128]{1,0:T(8,128)(2,1)S(1)}, u32[]{:S(2)}, u32[]{:S(2)}) %collective-permute-start.3) | collective-permute-done | bytes 409632 | tf_op jit(solution)/shard_map/ppermute | solution.py:459
  31.5 0.1 add_convert_fusion
  31.6 1.6 %collective-permute-start.4 = (bf16[400,128]{1,0:T(8,128)(2,1)S(1)}, bf16[400,128]{1,0:T(8,128)(2,1)S(1)}, u32[]{:S(2)}, u32[]{:S(2)}) collective-permute-start(bf16[400,128]{1,0:T(8,128)(2,1)S(1)} %get-tuple-element.58), channel_id=1, source_target_pairs={{0,16},{1,17},{2,18},{3,19},{4,20},{5,21},{6,22},{7,23},{8,24},{9,... | collective-permute-start | bytes 307208 | tf_op jit(solution)/shard_map/ppermute | solution.py:469
  33.2 1.7 %collective-permute-start.5 = (bf16[400,128]{1,0:T(8,128)(2,1)S(1)}, bf16[400,128]{1,0:T(8,128)(2,1)S(1)}, u32[]{:S(2)}, u32[]{:S(2)}) collective-permute-start(bf16[400,128]{1,0:T(8,128)(2,1)S(1)} %get-tuple-element.60), channel_id=1, source_target_pairs={{0,17},{1,16},{2,19},{3,18},{4,21},{5,20},{6,23},{7,22},{8,25},{9,... | collective-permute-start | bytes 307208 | tf_op jit(solution)/shard_map/ppermute | solution.py:469
  34.9 0.3 collective-permute-start.6
  35.2 2.9 %collective-permute-done.4 = bf16[400,128]{1,0:T(8,128)(2,1)S(1)} collective-permute-done((bf16[400,128]{1,0:T(8,128)(2,1)S(1)}, bf16[400,128]{1,0:T(8,128)(2,1)S(1)}, u32[]{:S(2)}, u32[]{:S(2)}) %collective-permute-start.4) | collective-permute-done | bytes 102432 | tf_op jit(solution)/shard_map/ppermute | solution.py:469
  38.1 1.6 %collective-permute-done.5 = bf16[400,128]{1,0:T(8,128)(2,1)S(1)} collective-permute-done((bf16[400,128]{1,0:T(8,128)(2,1)S(1)}, bf16[400,128]{1,0:T(8,128)(2,1)S(1)}, u32[]{:S(2)}, u32[]{:S(2)}) %collective-permute-start.5) | collective-permute-done | bytes 102432 | tf_op jit(solution)/shard_map/ppermute | solution.py:469
  39.7 0.6 collective-permute-done.6
  40.3 0.1 add_convert_fusion.3
  40.4 1.7 %collective-permute-start.7 = (bf16[400,128]{1,0:T(8,128)(2,1)S(1)}, bf16[400,128]{1,0:T(8,128)(2,1)S(1)}, u32[]{:S(2)}, u32[]{:S(2)}) collective-permute-start(bf16[400,128]{1,0:T(8,128)(2,1)S(1)} %add_convert_fusion.3), channel_id=1, source_target_pairs={{0,2},{1,3},{2,0},{3,1},{4,6},{5,7},{6,4},{7,5},{8,10},{9,11},{10,... | collective-permute-start | bytes 307208 | tf_op jit(solution)/shard_map/ppermute | solution.py:459
  42.1 3.0 %collective-permute-done.7 = bf16[400,128]{1,0:T(8,128)(2,1)S(1)} collective-permute-done((bf16[400,128]{1,0:T(8,128)(2,1)S(1)}, bf16[400,128]{1,0:T(8,128)(2,1)S(1)}, u32[]{:S(2)}, u32[]{:S(2)}) %collective-permute-start.7) | collective-permute-done | bytes 102432 | tf_op jit(solution)/shard_map/ppermute | solution.py:459
  45.2 2.6 %collective-permute-start.8 = (bf16[400,128]{1,0:T(8,128)(2,1)S(1)}, bf16[400,128]{1,0:T(8,128)(2,1)S(1)}, u32[]{:S(2)}, u32[]{:S(2)}) collective-permute-start(bf16[400,128]{1,0:T(8,128)(2,1)S(1)} %add_convert_fusion.2), channel_id=1, source_target_pairs={{0,4},{1,5},{2,6},{3,7},{4,0},{5,1},{6,2},{7,3},{8,12},{9,13},{10,... | collective-permute-start | bytes 307208 | tf_op jit(solution)/shard_map/ppermute | solution.py:459
  47.8 3.0 %collective-permute-done.8 = bf16[400,128]{1,0:T(8,128)(2,1)S(1)} collective-permute-done((bf16[400,128]{1,0:T(8,128)(2,1)S(1)}, bf16[400,128]{1,0:T(8,128)(2,1)S(1)}, u32[]{:S(2)}, u32[]{:S(2)}) %collective-permute-start.8) | collective-permute-done | bytes 102432 | tf_op jit(solution)/shard_map/ppermute | solution.py:459
  50.8 2.8 %collective-permute-start.9 = (bf16[400,128]{1,0:T(8,128)(2,1)S(1)}, bf16[400,128]{1,0:T(8,128)(2,1)S(1)}, u32[]{:S(2)}, u32[]{:S(2)}) collective-permute-start(bf16[400,128]{1,0:T(8,128)(2,1)S(1)} %add_convert_fusion.1), channel_id=1, source_target_pairs={{0,1},{1,0},{2,3},{3,2},{4,5},{5,4},{6,7},{7,6},{8,9},{9,8},{10,11... | collective-permute-start | bytes 307208 | tf_op jit(solution)/shard_map/ppermute | solution.py:459
  53.7 5.0 %shard_map.150 = (f32[128,1152]{1,0:T(8,128)}, f32[128,1152]{1,0:T(8,128)S(1)}) custom-call(bf16[9,128,512]{2,1,0:T(8,128)(2,1)S(1)} %get-tuple-element.46.grad_mixed, f32[128,1152]{1,0:T(8,128)S(1)} %get-tuple-element.47.height_grad, bf16[384,384]{1,0:T(8,128)(2,1)} %get-tuple-element.48.refs_0_, bf16[512,512]{1,0:T(8,128)(2,1)} %get-tuple-element.49.refs_1_, ...), custom_call_target="tpu_custom_call" | custom-call | tf_op jit(solution)/shard_map/pallas_call | solution.py:509
  58.7 0.0 copy-start.2
  58.7 0.0 copy-start.3
  58.7 0.0 copy-start.4
  58.7 4.7 %all-to-all-start.1 = ((f32[8,16,1152]{2,1,0:T(8,128)}), f32[8,16,1152]{2,1,0:T(8,128)S(1)}, u32[]{:S(2)}, u32[]{:S(2)}) async-start(f32[8,16,1152]{2,1,0:T(8,128)} %bitcast.24), calls=%async_computation.1 | async-start | bytes 1179648 | tf_op jit(solution)/shard_map/all_to_all | solution.py:520
  63.4 0.0 collective-permute-done.9
  63.5 0.0 copy-done.2
  63.5 0.0 copy-done.3
  63.5 0.0 copy-done.4
  63.5 0.0 copy-start.1
  63.5 1.2 %multiply_subtract_fusion = (f32[102400]{0:T(1024)}, f32[102400]{0:T(1024)}, f32[102400]{0:T(1024)}) fusion(f32[102400]{0:T(1024)S(1)} %copy-done.2, bf16[400,128]{1,0:T(8,128)(2,1)S(1)} %get-tuple-element.62, bf16[400,128]{1,0:T(8,128)(2,1)S(1)} %get-tuple-element.61, f32[102400]{0:T(1024)S(1)} %copy-done.3, f32[102400]{0:T(1024)S(1)} %copy-done.4), kind=kLoop, calls=%fused_computation.6 | loop fusion | flops 1945600 | bytes 2662400 | tf_op jit(solution)/shard_map/sub | solution.py:454
  64.7 11.4 %all-to-all-done.1 = f32[8,16,1152]{2,1,0:T(8,128)S(1)} async-done(((f32[8,16,1152]{2,1,0:T(8,128)}), f32[8,16,1152]{2,1,0:T(8,128)S(1)}, u32[]{:S(2)}, u32[]{:S(2)}) %all-to-all-start.1) | async-done | bytes 589856 | tf_op jit(solution)/shard_map/all_to_all | solution.py:520
  76.1 0.0 copy-done.1
  76.1 1.1 %shard_map.151 = bf16[128,1152]{1,0:T(8,128)(2,1)} custom-call(s32[1,128]{1,0:T(1,128)S(1)} %bitcast.22, f32[128,1152]{1,0:T(8,128)S(1)} %get-tuple-element.51.height_rows_ref, f32[128,1152]{1,0:T(8,128)S(1)} %bitcast.19), custom_call_target="tpu_custom_call" | custom-call | tf_op jit(solution)/shard_map/pallas_call | solution.py:509
  (4 shorter events, 0.1 us)
Async XLA Ops:
  0.6 16.3 %copy-start.5 = (f32[64,9,9]{0,2,1:T(8,128)S(1)}, f32[64,9,9]{0,2,1:T(8,128)}, u32[]{:S(2)}) copy-start(f32[64,9,9]{0,2,1:T(8,128)} %param.19) | copy-start | bytes 62212
  2.8 17.6 %copy-start = (bf16[800,128]{1,0:T(8,128)(2,1)S(1)}, bf16[800,128]{1,0:T(8,128)(2,1)}, u32[]{:S(2)}) copy-start(bf16[800,128]{1,0:T(8,128)(2,1)} %get-tuple-element.33.refs_0_) | copy-start | bytes 614404
  2.8 19.4 %all-to-all-start = ((bf16[8,16,1152]{2,1,0:T(8,128)(2,1)}), bf16[8,16,1152]{2,1,0:T(8,128)(2,1)S(1)}, u32[]{:S(2)}, u32[]{:S(2)}) async-start(bf16[8,16,1152]{2,1,0:T(8,128)(2,1)} %bitcast.25), calls=%async_computation | async-start | bytes 589824 | tf_op jit(solution)/shard_map/all_to_all | solution.py:520
  10.2 6.7 %collective-permute-start.1 = (bf16[800,128]{1,0:T(8,128)(2,1)}, bf16[800,128]{1,0:T(8,128)(2,1)S(1)}, u32[]{:S(2)}, u32[]{:S(2)}) collective-permute-start(bf16[800,128]{1,0:T(8,128)(2,1)} %get-tuple-element.33.refs_0_), channel_id=1, source_target_pairs={{0,16},{8,24},{16,0},{24,8},{1,17},{9,25},{17,1},{25,9},{2,18},{10... | collective-permute-start | bytes 614408 | tf_op jit(solution)/shard_map/ppermute | solution.py:459
  11.7 8.7 %collective-permute-start = (bf16[800,128]{1,0:T(8,128)(2,1)}, bf16[800,128]{1,0:T(8,128)(2,1)S(1)}, u32[]{:S(2)}, u32[]{:S(2)}) collective-permute-start(bf16[800,128]{1,0:T(8,128)(2,1)} %get-tuple-element.33.refs_0_), channel_id=1, source_target_pairs={{0,8},{8,0},{16,24},{24,16},{1,9},{9,1},{17,25},{25,17},{2,10},{10... | collective-permute-start | bytes 614408 | tf_op jit(solution)/shard_map/ppermute | solution.py:459
  16.9 3.5 %collective-permute-start.2 = (bf16[800,128]{1,0:T(8,128)(2,1)S(1)}, bf16[800,128]{1,0:T(8,128)(2,1)S(1)}, u32[]{:S(2)}, u32[]{:S(2)}) collective-permute-start(bf16[800,128]{1,0:T(8,128)(2,1)S(1)} %collective-permute-done.1.refs_2_), channel_id=1, source_target_pairs={{0,8},{8,0},{16,24},{24,16},{1,9},{9,1},{17,25},{25,17},{2,10},{10... | collective-permute-start | bytes 614408 | tf_op jit(solution)/shard_map/ppermute | solution.py:459
  29.5 1.9 %collective-permute-start.3 = (bf16[1600,128]{1,0:T(8,128)(2,1)S(1)}, bf16[1600,128]{1,0:T(8,128)(2,1)S(1)}, u32[]{:S(2)}, u32[]{:S(2)}) collective-permute-start(bf16[1600,128]{1,0:T(8,128)(2,1)S(1)} %get-tuple-element.54), channel_id=1, source_target_pairs={{0,8},{8,0},{16,24},{24,16},{1,9},{9,1},{17,25},{25,17},{2,10},{10... | collective-permute-start | bytes 1228808 | tf_op jit(solution)/shard_map/ppermute | solution.py:459
  31.6 6.5 %collective-permute-start.4 = (bf16[400,128]{1,0:T(8,128)(2,1)S(1)}, bf16[400,128]{1,0:T(8,128)(2,1)S(1)}, u32[]{:S(2)}, u32[]{:S(2)}) collective-permute-start(bf16[400,128]{1,0:T(8,128)(2,1)S(1)} %get-tuple-element.58), channel_id=1, source_target_pairs={{0,16},{1,17},{2,18},{3,19},{4,20},{5,21},{6,22},{7,23},{8,24},{9,... | collective-permute-start | bytes 307208 | tf_op jit(solution)/shard_map/ppermute | solution.py:469
  33.2 6.5 %collective-permute-start.5 = (bf16[400,128]{1,0:T(8,128)(2,1)S(1)}, bf16[400,128]{1,0:T(8,128)(2,1)S(1)}, u32[]{:S(2)}, u32[]{:S(2)}) collective-permute-start(bf16[400,128]{1,0:T(8,128)(2,1)S(1)} %get-tuple-element.60), channel_id=1, source_target_pairs={{0,17},{1,16},{2,19},{3,18},{4,21},{5,20},{6,23},{7,22},{8,25},{9,... | collective-permute-start | bytes 307208 | tf_op jit(solution)/shard_map/ppermute | solution.py:469
  34.9 5.4 %collective-permute-start.6 = (bf16[400,128]{1,0:T(8,128)(2,1)S(1)}, bf16[400,128]{1,0:T(8,128)(2,1)S(1)}, u32[]{:S(2)}, u32[]{:S(2)}) collective-permute-start(bf16[400,128]{1,0:T(8,128)(2,1)S(1)} %get-tuple-element.59), channel_id=1, source_target_pairs={{0,1},{1,0},{2,3},{3,2},{4,5},{5,4},{6,7},{7,6},{8,9},{9,8},{10,11... | collective-permute-start | bytes 307208 | tf_op jit(solution)/shard_map/ppermute | solution.py:469
  40.4 4.7 %collective-permute-start.7 = (bf16[400,128]{1,0:T(8,128)(2,1)S(1)}, bf16[400,128]{1,0:T(8,128)(2,1)S(1)}, u32[]{:S(2)}, u32[]{:S(2)}) collective-permute-start(bf16[400,128]{1,0:T(8,128)(2,1)S(1)} %add_convert_fusion.3), channel_id=1, source_target_pairs={{0,2},{1,3},{2,0},{3,1},{4,6},{5,7},{6,4},{7,5},{8,10},{9,11},{10,... | collective-permute-start | bytes 307208 | tf_op jit(solution)/shard_map/ppermute | solution.py:459
  45.2 5.6 %collective-permute-start.8 = (bf16[400,128]{1,0:T(8,128)(2,1)S(1)}, bf16[400,128]{1,0:T(8,128)(2,1)S(1)}, u32[]{:S(2)}, u32[]{:S(2)}) collective-permute-start(bf16[400,128]{1,0:T(8,128)(2,1)S(1)} %add_convert_fusion.2), channel_id=1, source_target_pairs={{0,4},{1,5},{2,6},{3,7},{4,0},{5,1},{6,2},{7,3},{8,12},{9,13},{10,... | collective-permute-start | bytes 307208 | tf_op jit(solution)/shard_map/ppermute | solution.py:459
  50.8 12.6 %collective-permute-start.9 = (bf16[400,128]{1,0:T(8,128)(2,1)S(1)}, bf16[400,128]{1,0:T(8,128)(2,1)S(1)}, u32[]{:S(2)}, u32[]{:S(2)}) collective-permute-start(bf16[400,128]{1,0:T(8,128)(2,1)S(1)} %add_convert_fusion.1), channel_id=1, source_target_pairs={{0,1},{1,0},{2,3},{3,2},{4,5},{5,4},{6,7},{7,6},{8,9},{9,8},{10,11... | collective-permute-start | bytes 307208 | tf_op jit(solution)/shard_map/ppermute | solution.py:459
  58.7 4.8 %copy-start.2 = (f32[102400]{0:T(1024)S(1)}, f32[102400]{0:T(1024)}, u32[]{:S(2)}) copy-start(f32[102400]{0:T(1024)} %param.13) | copy-start | bytes 1228804
  58.7 4.8 %copy-start.3 = (f32[102400]{0:T(1024)S(1)}, f32[102400]{0:T(1024)}, u32[]{:S(2)}) copy-start(f32[102400]{0:T(1024)} %param.15) | copy-start | bytes 1228804
  58.7 4.8 %copy-start.4 = (f32[102400]{0:T(1024)S(1)}, f32[102400]{0:T(1024)}, u32[]{:S(2)}) copy-start(f32[102400]{0:T(1024)} %param.14) | copy-start | bytes 1228804
  58.7 17.4 %all-to-all-start.1 = ((f32[8,16,1152]{2,1,0:T(8,128)}), f32[8,16,1152]{2,1,0:T(8,128)S(1)}, u32[]{:S(2)}, u32[]{:S(2)}) async-start(f32[8,16,1152]{2,1,0:T(8,128)} %bitcast.24), calls=%async_computation.1 | async-start | bytes 1179648 | tf_op jit(solution)/shard_map/all_to_all | solution.py:520
  63.5 12.6 %copy-start.1 = (s32[1,1,128]{2,1,0:T(1,128)S(1)}, s32[1,1,128]{2,1,0:T(1,128)}, u32[]{:S(2)}) copy-start(s32[1,1,128]{2,1,0:T(1,128)} %param.16) | copy-start | bytes 1540

commit v5 on v4

--- a/solution.py
+++ b/solution.py
@@ -16,7 +16,7 @@
 ROTS = 64
 SUB = 8
 TURN_ROWS = 88
-GROUPS = 2
+GROUPS = 4
 
 harmonic_order = (0, 2, 6, 3, 7, 1, 5, 8, 4)
 norm_epsilon = 1e-06
@@ -384,16 +384,16 @@
 
 def slot_kernel(grad_mixed, height_grad, *refs):
     sides, held = refs[:5], refs[7:12]
-    slot_grad_ref, height_rows_ref = refs[5:7]
+    slot_rows, height_rows_ref = refs[5:7]
     zero_w, one_w, two_w, turn, slot_ref = held
-    mixed, source_high, source_low, slot_rows, arrived = refs[12:]
+    mixed, source_high, source_low, arrived = refs[12:]
     copies = [
         pltpu.make_async_copy(side, target, arrived.at[number])
         for number, (side, target) in enumerate(zip(sides, held))
     ]
     for copy in copies:
         copy.start()
-    slots_n = slot_grad_ref.shape[0]
+    slots_n = slot_rows.shape[0]
     atoms_n = slot_ref.shape[1]
     for col in range(HARM):
         height_rows_ref[:, lanes(col)] = height_grad[:, lanes(col, atoms_n)].T
@@ -430,9 +430,6 @@
     slot_rows[...] = dot(taken, flat(source_high[...]), 1, 1) + dot(
         taken, flat(source_low[...]), 1, 1
     )
-    slot_copy = pltpu.make_async_copy(slot_rows, slot_grad_ref, arrived.at[len(copies)])
-    slot_copy.start()
-    slot_copy.wait()
 
 
 def finish_kernel(sends_ref, height_rows_ref, back_ref, grad_ref):
@@ -526,7 +523,7 @@
     wide = HARM * atoms_n
     outgoing, own = call(
         pick_kernel,
-        [("auto", (slots_n, features), BF16), ("auto", (PACK_ROWS // node_size, C), BF16)],
+        [("vmem", (slots_n, features), BF16), ("vmem", (PACK_ROWS // node_size, C), BF16)],
         [("auto", value) for value in (send_rows, atoms, params.reshape(-1, C))],
     )
     slot_rows = peers_exchange(outgoing)
@@ -589,7 +586,7 @@
     )
     slot_grad, height_rows = call(
         slot_kernel,
-        [("hbm", (slots_n, features), F32), ("vmem", (atoms_n, features), F32)],
+        [("vmem", (slots_n, features), F32), ("vmem", (atoms_n, features), F32)],
         [("vmem", grad_mixed), ("vmem", height_grad)]
         + [("hbm", value) for value in read_again],
         [
@@ -597,8 +594,7 @@
             pltpu.VMEM((HARM, C, edges_n), F32),
             pltpu.VMEM((HARM, C, edges_n), BF16),
             pltpu.VMEM((HARM, C, edges_n), BF16),
-            pltpu.VMEM((slots_n, features), F32),
-            pltpu.SemaphoreType.DMA((len(read_again) + 1,)),
+            pltpu.SemaphoreType.DMA((len(read_again),)),
         ],
         megabytes=20,
     )
@@ -621,12 +617,17 @@
         )
         total = total + came.astype(F32)
     grads = total.astype(BF16)
-    for bit in range(1, edge_bits):
+    for bit in reversed(range(2, edge_bits)):
         grads = add_low(grads, swap(grads, "edge", bit))
-    other = swap(grads, "edge", 0)
+    far = swap_both(grads, 0, 2)
+    both = swap_both(grads, 0, 3)
+    near = swap_both(grads, 0, 1)
+    own_half = grads.astype(F32) + far.astype(F32)
+    other_half = near.astype(F32) + both.astype(F32)
     is_low = (lax.axis_index("edge") & 1) == 0
     grads = jnp.concatenate(
-        [jnp.where(is_low, grads, other), jnp.where(is_low, other, grads)], axis=0
+        [jnp.where(is_low, own_half, other_half), jnp.where(is_low, other_half, own_half)],
+        axis=0,
     )
 
     returned = peers_exchange(slot_grad)
@@ -641,7 +642,7 @@
         return value.reshape(-1, C)
 
     new_params, new_one, new_two = adam_step(
-        rows_of_lanes(params), rows_of_lanes(adam_m), rows_of_lanes(adam_v), grads.astype(F32)
+        rows_of_lanes(params), rows_of_lanes(adam_m), rows_of_lanes(adam_v), grads
     )
     return (
         output,

time: 77.7 us -> 77.8 us (level)
    ppermute x7 -> x5, starting transfers between devices: 9.32 us -> 4.75 us  [swap(): return lax.ppermute(value, axis, [(i, i ^ 1 << bit) for i in range(size)])]
    ppermute x3 -> x6, starting transfers between devices: 3.55 us -> 7.11 us  [swap_both(): return lax.ppermute(value, ('node', 'edge'), pairs)]
    all_to_all x2, waiting for transfers between devices: 11.4 us -> 13.3 us  [peers_exchange(): lax.all_to_all(value, 'edge', split_axis=0, concat_axis=0, tiled=True)]
    ppermute x7 -> x5, waiting for transfers between devices: 12.6 us -> 11 us  [swap(): return lax.ppermute(value, axis, [(i, i ^ 1 << bit) for i in range(size)])]
    all_to_all x2, starting transfers between devices: 12.1 us -> 13 us  [peers_exchange(): lax.all_to_all(value, 'edge', split_axis=0, concat_axis=0, tiled=True)]
    ppermute x3 -> x6, waiting for transfers between devices: 5.16 us -> 5.16 us  [swap_both(): return lax.ppermute(value, ('node', 'edge'), pairs)]
  transfers between devices with their start and end apart: 12 -> 13, of which waited for: 8 -> 7; matrix products, arithmetic and copies ran while one was open for 2% -> 2% of each run, Pallas kernels for 12% -> 12%
where the time goes in v5:
time: 77.8 us; the launch traced here: 77.4 us
  waiting for transfers between devices  29.5 us (38%)
  starting transfers between devices  24.9 us (32%)
  Pallas kernels  19.5 us (25%)
  other arithmetic  1.48 us (2%)
  between operations  1.44 us (2%)
    pallas_call x6, Pallas kernels, call(): pl.pallas_call(kernel, out_shape=tuple((typed_out(*out) for out in outs))...  19.5 us
    all_to_all x2, waiting for transfers between devices, peers_exchange(): lax.all_to_all(value, 'edge', split_axis=0, concat_axis=0, tiled=True)  13.3 us
    all_to_all x2, starting transfers between devices, peers_exchange(): lax.all_to_all(value, 'edge', split_axis=0, concat_axis=0, tiled=True)  13 us
    ppermute x5, waiting for transfers between devices, swap(): return lax.ppermute(value, axis, [(i, i ^ 1 << bit) for i in range(size)])  11 us
    ppermute x6, starting transfers between devices, swap_both(): return lax.ppermute(value, ('node', 'edge'), pairs)  7.11 us
    ppermute x6, waiting for transfers between devices, swap_both(): return lax.ppermute(value, ('node', 'edge'), pairs)  5.16 us
    ppermute x5, starting transfers between devices, swap(): return lax.ppermute(value, axis, [(i, i ^ 1 << bit) for i in range(size)])  4.75 us
  transfers between devices with their start and end apart: 13, of which 7 were waited for; matrix products, arithmetic and copies ran while one was open for 2% of the time, Pallas kernels for 12%

profile of v5, /device:TPU:0, one launch (start us, length us, event | category | flops | bytes accessed | tf_op | source)
XLA Modules:
  0.0 77.4 jit_solution(13393045519629976976)
XLA Ops:
  0.6 0.0 copy-start.4
  0.6 2.1 %shard_map.146 = (bf16[128,1152]{1,0:T(8,128)(2,1)}, bf16[800,128]{1,0:T(8,128)(2,1)S(1)}) custom-call(s32[1,128]{1,0:T(1,128)} %bitcast.20, bf16[128,1152]{1,0:T(8,128)(2,1)} %atoms_ref.3, f32[800,128]{1,0:T(8,128)} %bitcast.22), custom_call_target="tpu_custom_call" | custom-call | tf_op jit(solution)/shard_map/pallas_call | solution.py:506
  2.8 7.3 %all-to-all-start = ((bf16[8,16,1152]{2,1,0:T(8,128)(2,1)}), bf16[8,16,1152]{2,1,0:T(8,128)(2,1)S(1)}, u32[]{:S(2)}, u32[]{:S(2)}) async-start(bf16[8,16,1152]{2,1,0:T(8,128)(2,1)} %bitcast.2), calls=%async_computation | async-start | bytes 589824 | tf_op jit(solution)/shard_map/all_to_all | solution.py:517
  10.1 1.5 %collective-permute-start.1 = (bf16[800,128]{1,0:T(8,128)(2,1)S(1)}, bf16[800,128]{1,0:T(8,128)(2,1)S(1)}, u32[]{:S(2)}, u32[]{:S(2)}) collective-permute-start(bf16[800,128]{1,0:T(8,128)(2,1)S(1)} %get-tuple-element.33.refs_0_), channel_id=1, source_target_pairs={{0,16},{8,24},{16,0},{24,8},{1,17},{9,25},{17,1},{25,9},{2,18},{10... | collective-permute-start | bytes 614408 | tf_op jit(solution)/shard_map/ppermute | solution.py:456
  11.6 0.0 collective-permute-start
  11.6 5.0 %collective-permute-done.1.refs_2_ = bf16[800,128]{1,0:T(8,128)(2,1)S(1)} collective-permute-done((bf16[800,128]{1,0:T(8,128)(2,1)S(1)}, bf16[800,128]{1,0:T(8,128)(2,1)S(1)}, u32[]{:S(2)}, u32[]{:S(2)}) %collective-permute-start.1) | collective-permute-done | bytes 204832 | tf_op jit(solution)/shard_map/ppermute | solution.py:456
  16.6 0.0 collective-permute-start.2
  16.6 0.0 copy-done.4
  16.6 0.6 reshape.44.table_ref
  17.9 2.2 %shard_map.147 = (bf16[128,1152]{1,0:T(8,128)(2,1)}, bf16[128,1152]{1,0:T(8,128)(2,1)}, f32[352,128]{1,0:T(8,128)}, f32[4,128]{1,0:T(4,128)}) custom-call(s32[1,1]{1,0:T(1,128)S(6)} %copy.16.live_ref, bf16[128,1152]{1,0:T(8,128)(2,1)} %atoms_ref.3, bf16[128,1152]{1,0:T(8,128)(2,1)} %cot_ref.1, s32[4,128]{1,0:T(4,128)} %bitcast.26, f32[4,128]{1,0:T(4,128)} %bitcast.27, ...), custom_call_target="tpu_custom_call" | custom-call | tf_op jit(solution)/shard_map/pallas_call | solution.py:506
  20.1 0.0 collective-permute-done.refs_1_
  20.1 0.0 collective-permute-done.2.refs_3_
  20.1 1.8 %shard_map.148 = (bf16[384,384]{1,0:T(8,128)(2,1)}, bf16[512,512]{1,0:T(8,128)(2,1)}, bf16[256,256]{1,0:T(8,128)(2,1)}, bf16[384,384]{1,0:T(8,128)(2,1)}, bf16[5...) custom-call(bf16[800,128]{1,0:T(8,128)(2,1)S(1)} %get-tuple-element., ...), custom_call_target="tpu_custom_call" | custom-call | tf_op jit(solution)/shard_map/pallas_call | solution.py:506
  21.9 0.0 all-to-all-done
  21.9 7.2 %shard_map.149 = (bf16[128,1152]{1,0:T(8,128)(2,1)}, f32[128,1152]{1,0:T(8,128)S(1)}, bf16[9,128,512]{2,1,0:T(8,128)(2,1)S(1)}, bf16[1600,128]{1,0:T(8,128)(2,1)S(1)}, bf16[1600,128]{1,0:T(8,128)(2,1)S(1)}) custom-call(bf16[128,1152]{1,0:T(8,128)(2,1)S(1)} %bitcast.19, s32[4,128]{1,0:T(4,128)} %bitcast.24, f32[352,128]{1,0:T(8,128)} %get-tuple-element.31.refs_2_.refs_3_, ...), custom_call_target="tpu_custom_call" | custom-call | tf_op jit(solution)/shard_map/pallas_call | solution.py:506
  29.1 0.6 collective-permute-start.3
  29.6 1.4 %collective-permute-done.3 = bf16[1600,128]{1,0:T(8,128)(2,1)S(1)} collective-permute-done((bf16[1600,128]{1,0:T(8,128)(2,1)S(1)}, bf16[1600,128]{1,0:T(8,128)(2,1)S(1)}, u32[]{:S(2)}, u32[]{:S(2)}) %collective-permute-start.3) | collective-permute-done | bytes 409632 | tf_op jit(solution)/shard_map/ppermute | solution.py:456
  31.0 0.1 add_convert_fusion
  31.2 1.6 %collective-permute-start.4 = (bf16[400,128]{1,0:T(8,128)(2,1)S(1)}, bf16[400,128]{1,0:T(8,128)(2,1)S(1)}, u32[]{:S(2)}, u32[]{:S(2)}) collective-permute-start(bf16[400,128]{1,0:T(8,128)(2,1)S(1)} %get-tuple-element.60), channel_id=1, source_target_pairs={{0,16},{1,17},{2,18},{3,19},{4,20},{5,21},{6,22},{7,23},{8,24},{9,... | collective-permute-start | bytes 307208 | tf_op jit(solution)/shard_map/ppermute | solution.py:466
  32.7 1.7 %collective-permute-start.5 = (bf16[400,128]{1,0:T(8,128)(2,1)S(1)}, bf16[400,128]{1,0:T(8,128)(2,1)S(1)}, u32[]{:S(2)}, u32[]{:S(2)}) collective-permute-start(bf16[400,128]{1,0:T(8,128)(2,1)S(1)} %get-tuple-element.62), channel_id=1, source_target_pairs={{0,17},{1,16},{2,19},{3,18},{4,21},{5,20},{6,23},{7,22},{8,25},{9,... | collective-permute-start | bytes 307208 | tf_op jit(solution)/shard_map/ppermute | solution.py:466
  34.4 0.3 collective-permute-start.6
  34.7 2.9 %collective-permute-done.4 = bf16[400,128]{1,0:T(8,128)(2,1)S(1)} collective-permute-done((bf16[400,128]{1,0:T(8,128)(2,1)S(1)}, bf16[400,128]{1,0:T(8,128)(2,1)S(1)}, u32[]{:S(2)}, u32[]{:S(2)}) %collective-permute-start.4) | collective-permute-done | bytes 102432 | tf_op jit(solution)/shard_map/ppermute | solution.py:466
  37.6 1.6 %collective-permute-done.5 = bf16[400,128]{1,0:T(8,128)(2,1)S(1)} collective-permute-done((bf16[400,128]{1,0:T(8,128)(2,1)S(1)}, bf16[400,128]{1,0:T(8,128)(2,1)S(1)}, u32[]{:S(2)}, u32[]{:S(2)}) %collective-permute-start.5) | collective-permute-done | bytes 102432 | tf_op jit(solution)/shard_map/ppermute | solution.py:466
  39.3 0.6 collective-permute-done.6
  39.9 0.1 add_convert_fusion.2
  39.9 2.7 %collective-permute-start.7 = (bf16[400,128]{1,0:T(8,128)(2,1)S(1)}, bf16[400,128]{1,0:T(8,128)(2,1)S(1)}, u32[]{:S(2)}, u32[]{:S(2)}) collective-permute-start(bf16[400,128]{1,0:T(8,128)(2,1)S(1)} %add_convert_fusion.2), channel_id=1, source_target_pairs={{0,4},{1,5},{2,6},{3,7},{4,0},{5,1},{6,2},{7,3},{8,12},{9,13},{10,... | collective-permute-start | bytes 307208 | tf_op jit(solution)/shard_map/ppermute | solution.py:456
  42.6 4.6 %collective-permute-done.7 = bf16[400,128]{1,0:T(8,128)(2,1)S(1)} collective-permute-done((bf16[400,128]{1,0:T(8,128)(2,1)S(1)}, bf16[400,128]{1,0:T(8,128)(2,1)S(1)}, u32[]{:S(2)}, u32[]{:S(2)}) %collective-permute-start.7) | collective-permute-done | bytes 102432 | tf_op jit(solution)/shard_map/ppermute | solution.py:456
  47.2 1.6 %collective-permute-start.10 = (bf16[400,128]{1,0:T(8,128)(2,1)S(1)}, bf16[400,128]{1,0:T(8,128)(2,1)S(1)}, u32[]{:S(2)}, u32[]{:S(2)}) collective-permute-start(bf16[400,128]{1,0:T(8,128)(2,1)S(1)} %add_convert_fusion.1), channel_id=1, source_target_pairs={{0,3},{1,2},{2,1},{3,0},{4,7},{5,6},{6,5},{7,4},{8,11},{9,10},{10,... | collective-permute-start | bytes 307208 | tf_op jit(solution)/shard_map/ppermute | solution.py:466
  48.8 1.6 %collective-permute-start.8 = (bf16[400,128]{1,0:T(8,128)(2,1)S(1)}, bf16[400,128]{1,0:T(8,128)(2,1)S(1)}, u32[]{:S(2)}, u32[]{:S(2)}) collective-permute-start(bf16[400,128]{1,0:T(8,128)(2,1)S(1)} %add_convert_fusion.1), channel_id=1, source_target_pairs={{0,2},{1,3},{2,0},{3,1},{4,6},{5,7},{6,4},{7,5},{8,10},{9,11},{10,... | collective-permute-start | bytes 307208 | tf_op jit(solution)/shard_map/ppermute | solution.py:466
  50.4 0.4 collective-permute-start.9
  50.8 5.0 %shard_map.150 = (f32[128,1152]{1,0:T(8,128)}, f32[128,1152]{1,0:T(8,128)S(1)}) custom-call(bf16[9,128,512]{2,1,0:T(8,128)(2,1)S(1)} %get-tuple-element.46.grad_mixed, f32[128,1152]{1,0:T(8,128)S(1)} %get-tuple-element.47.height_grad, bf16[384,384]{1,0:T(8,128)(2,1)} %get-tuple-element.48.refs_0_, bf16[512,512]{1,0:T(8,128)(2,1)} %get-tuple-element.49.refs_1_, ...), custom_call_target="tpu_custom_call" | custom-call | tf_op jit(solution)/shard_map/pallas_call | solution.py:506
  55.8 0.0 copy-start.1
  55.8 0.0 copy-start.2
  55.8 0.0 copy-start.3
  55.8 5.7 %all-to-all-start.1 = ((f32[8,16,1152]{2,1,0:T(8,128)}), f32[8,16,1152]{2,1,0:T(8,128)S(1)}, u32[]{:S(2)}, u32[]{:S(2)}) async-start(f32[8,16,1152]{2,1,0:T(8,128)} %bitcast.8), calls=%async_computation.1 | async-start | bytes 1179648 | tf_op jit(solution)/shard_map/all_to_all | solution.py:517
  61.6 0.0 collective-permute-done.10
  61.6 0.0 collective-permute-done.8
  61.6 0.0 collective-permute-done.9
  61.6 0.1 fusion.2
  61.7 0.0 copy-done.1
  61.7 0.0 copy-done.2
  61.7 0.0 copy-done.3
  61.7 0.0 copy-start
  61.7 1.2 %multiply_subtract_fusion = (f32[102400]{0:T(1024)}, f32[102400]{0:T(1024)}, f32[102400]{0:T(1024)}) fusion(f32[102400]{0:T(1024)S(1)} %copy-done.1, f32[400,128]{1,0:T(8,128)S(1)} %get-tuple-element.59, f32[400,128]{1,0:T(8,128)S(1)} %get-tuple-element.58, f32[102400]{0:T(1024)S(1)} %copy-done.2, f32[102400]{0:T(1024)S(1)} %copy-done.3), kind=kLoop, calls=%fused_computation.4 | loop fusion | flops 1536000 | bytes 2867200 | tf_op jit(solution)/shard_map/sub | solution.py:451
  62.9 13.3 %all-to-all-done.1 = f32[8,16,1152]{2,1,0:T(8,128)S(1)} async-done(((f32[8,16,1152]{2,1,0:T(8,128)}), f32[8,16,1152]{2,1,0:T(8,128)S(1)}, u32[]{:S(2)}, u32[]{:S(2)}) %all-to-all-start.1) | async-done | bytes 589856 | tf_op jit(solution)/shard_map/all_to_all | solution.py:517
  76.3 0.0 copy-done
  76.3 1.1 %shard_map.151 = bf16[128,1152]{1,0:T(8,128)(2,1)} custom-call(s32[1,128]{1,0:T(1,128)S(1)} %bitcast.21, f32[128,1152]{1,0:T(8,128)S(1)} %get-tuple-element.51.height_rows_ref, f32[128,1152]{1,0:T(8,128)S(1)} %bitcast.18), custom_call_target="tpu_custom_call" | custom-call | tf_op jit(solution)/shard_map/pallas_call | solution.py:506
  (2 shorter events, 0.1 us)
Async XLA Ops:
  0.6 16.0 %copy-start.4 = (f32[64,9,9]{0,2,1:T(8,128)S(1)}, f32[64,9,9]{0,2,1:T(8,128)}, u32[]{:S(2)}) copy-start(f32[64,9,9]{0,2,1:T(8,128)} %param.19) | copy-start | bytes 62212
  2.8 19.1 %all-to-all-start = ((bf16[8,16,1152]{2,1,0:T(8,128)(2,1)}), bf16[8,16,1152]{2,1,0:T(8,128)(2,1)S(1)}, u32[]{:S(2)}, u32[]{:S(2)}) async-start(bf16[8,16,1152]{2,1,0:T(8,128)(2,1)} %bitcast.2), calls=%async_computation | async-start | bytes 589824 | tf_op jit(solution)/shard_map/all_to_all | solution.py:517
  10.1 6.5 %collective-permute-start.1 = (bf16[800,128]{1,0:T(8,128)(2,1)S(1)}, bf16[800,128]{1,0:T(8,128)(2,1)S(1)}, u32[]{:S(2)}, u32[]{:S(2)}) collective-permute-start(bf16[800,128]{1,0:T(8,128)(2,1)S(1)} %get-tuple-element.33.refs_0_), channel_id=1, source_target_pairs={{0,16},{8,24},{16,0},{24,8},{1,17},{9,25},{17,1},{25,9},{2,18},{10... | collective-permute-start | bytes 614408 | tf_op jit(solution)/shard_map/ppermute | solution.py:456
  11.6 8.5 %collective-permute-start = (bf16[800,128]{1,0:T(8,128)(2,1)S(1)}, bf16[800,128]{1,0:T(8,128)(2,1)S(1)}, u32[]{:S(2)}, u32[]{:S(2)}) collective-permute-start(bf16[800,128]{1,0:T(8,128)(2,1)S(1)} %get-tuple-element.33.refs_0_), channel_id=1, source_target_pairs={{0,8},{8,0},{16,24},{24,16},{1,9},{9,1},{17,25},{25,17},{2,10},{10... | collective-permute-start | bytes 614408 | tf_op jit(solution)/shard_map/ppermute | solution.py:456
  16.6 3.5 %collective-permute-start.2 = (bf16[800,128]{1,0:T(8,128)(2,1)S(1)}, bf16[800,128]{1,0:T(8,128)(2,1)S(1)}, u32[]{:S(2)}, u32[]{:S(2)}) collective-permute-start(bf16[800,128]{1,0:T(8,128)(2,1)S(1)} %collective-permute-done.1.refs_2_), channel_id=1, source_target_pairs={{0,8},{8,0},{16,24},{24,16},{1,9},{9,1},{17,25},{25,17},{2,10},{10... | collective-permute-start | bytes 614408 | tf_op jit(solution)/shard_map/ppermute | solution.py:456
  29.1 1.9 %collective-permute-start.3 = (bf16[1600,128]{1,0:T(8,128)(2,1)S(1)}, bf16[1600,128]{1,0:T(8,128)(2,1)S(1)}, u32[]{:S(2)}, u32[]{:S(2)}) collective-permute-start(bf16[1600,128]{1,0:T(8,128)(2,1)S(1)} %get-tuple-element.54), channel_id=1, source_target_pairs={{0,8},{8,0},{16,24},{24,16},{1,9},{9,1},{17,25},{25,17},{2,10},{10... | collective-permute-start | bytes 1228808 | tf_op jit(solution)/shard_map/ppermute | solution.py:456
  31.2 6.5 %collective-permute-start.4 = (bf16[400,128]{1,0:T(8,128)(2,1)S(1)}, bf16[400,128]{1,0:T(8,128)(2,1)S(1)}, u32[]{:S(2)}, u32[]{:S(2)}) collective-permute-start(bf16[400,128]{1,0:T(8,128)(2,1)S(1)} %get-tuple-element.60), channel_id=1, source_target_pairs={{0,16},{1,17},{2,18},{3,19},{4,20},{5,21},{6,22},{7,23},{8,24},{9,... | collective-permute-start | bytes 307208 | tf_op jit(solution)/shard_map/ppermute | solution.py:466
  32.7 6.5 %collective-permute-start.5 = (bf16[400,128]{1,0:T(8,128)(2,1)S(1)}, bf16[400,128]{1,0:T(8,128)(2,1)S(1)}, u32[]{:S(2)}, u32[]{:S(2)}) collective-permute-start(bf16[400,128]{1,0:T(8,128)(2,1)S(1)} %get-tuple-element.62), channel_id=1, source_target_pairs={{0,17},{1,16},{2,19},{3,18},{4,21},{5,20},{6,23},{7,22},{8,25},{9,... | collective-permute-start | bytes 307208 | tf_op jit(solution)/shard_map/ppermute | solution.py:466
  34.4 5.4 %collective-permute-start.6 = (bf16[400,128]{1,0:T(8,128)(2,1)S(1)}, bf16[400,128]{1,0:T(8,128)(2,1)S(1)}, u32[]{:S(2)}, u32[]{:S(2)}) collective-permute-start(bf16[400,128]{1,0:T(8,128)(2,1)S(1)} %get-tuple-element.61), channel_id=1, source_target_pairs={{0,1},{1,0},{2,3},{3,2},{4,5},{5,4},{6,7},{7,6},{8,9},{9,8},{10,11... | collective-permute-start | bytes 307208 | tf_op jit(solution)/shard_map/ppermute | solution.py:466
  39.9 7.2 %collective-permute-start.7 = (bf16[400,128]{1,0:T(8,128)(2,1)S(1)}, bf16[400,128]{1,0:T(8,128)(2,1)S(1)}, u32[]{:S(2)}, u32[]{:S(2)}) collective-permute-start(bf16[400,128]{1,0:T(8,128)(2,1)S(1)} %add_convert_fusion.2), channel_id=1, source_target_pairs={{0,4},{1,5},{2,6},{3,7},{4,0},{5,1},{6,2},{7,3},{8,12},{9,13},{10,... | collective-permute-start | bytes 307208 | tf_op jit(solution)/shard_map/ppermute | solution.py:456
  47.2 14.4 %collective-permute-start.10 = (bf16[400,128]{1,0:T(8,128)(2,1)S(1)}, bf16[400,128]{1,0:T(8,128)(2,1)S(1)}, u32[]{:S(2)}, u32[]{:S(2)}) collective-permute-start(bf16[400,128]{1,0:T(8,128)(2,1)S(1)} %add_convert_fusion.1), channel_id=1, source_target_pairs={{0,3},{1,2},{2,1},{3,0},{4,7},{5,6},{6,5},{7,4},{8,11},{9,10},{10,... | collective-permute-start | bytes 307208 | tf_op jit(solution)/shard_map/ppermute | solution.py:466
  48.8 12.8 %collective-permute-start.8 = (bf16[400,128]{1,0:T(8,128)(2,1)S(1)}, bf16[400,128]{1,0:T(8,128)(2,1)S(1)}, u32[]{:S(2)}, u32[]{:S(2)}) collective-permute-start(bf16[400,128]{1,0:T(8,128)(2,1)S(1)} %add_convert_fusion.1), channel_id=1, source_target_pairs={{0,2},{1,3},{2,0},{3,1},{4,6},{5,7},{6,4},{7,5},{8,10},{9,11},{10,... | collective-permute-start | bytes 307208 | tf_op jit(solution)/shard_map/ppermute | solution.py:466
  50.4 11.2 %collective-permute-start.9 = (bf16[400,128]{1,0:T(8,128)(2,1)S(1)}, bf16[400,128]{1,0:T(8,128)(2,1)S(1)}, u32[]{:S(2)}, u32[]{:S(2)}) collective-permute-start(bf16[400,128]{1,0:T(8,128)(2,1)S(1)} %add_convert_fusion.1), channel_id=1, source_target_pairs={{0,1},{1,0},{2,3},{3,2},{4,5},{5,4},{6,7},{7,6},{8,9},{9,8},{10,11... | collective-permute-start | bytes 307208 | tf_op jit(solution)/shard_map/ppermute | solution.py:466
  55.8 5.9 %copy-start.1 = (f32[102400]{0:T(1024)S(1)}, f32[102400]{0:T(1024)}, u32[]{:S(2)}) copy-start(f32[102400]{0:T(1024)} %param.13) | copy-start | bytes 1228804
  55.8 5.9 %copy-start.2 = (f32[102400]{0:T(1024)S(1)}, f32[102400]{0:T(1024)}, u32[]{:S(2)}) copy-start(f32[102400]{0:T(1024)} %param.15) | copy-start | bytes 1228804
  55.8 5.9 %copy-start.3 = (f32[102400]{0:T(1024)S(1)}, f32[102400]{0:T(1024)}, u32[]{:S(2)}) copy-start(f32[102400]{0:T(1024)} %param.14) | copy-start | bytes 1228804
  55.8 20.4 %all-to-all-start.1 = ((f32[8,16,1152]{2,1,0:T(8,128)}), f32[8,16,1152]{2,1,0:T(8,128)S(1)}, u32[]{:S(2)}, u32[]{:S(2)}) async-start(f32[8,16,1152]{2,1,0:T(8,128)} %bitcast.8), calls=%async_computation.1 | async-start | bytes 1179648 | tf_op jit(solution)/shard_map/all_to_all | solution.py:517
  61.7 14.6 %copy-start = (s32[1,1,128]{2,1,0:T(1,128)S(1)}, s32[1,1,128]{2,1,0:T(1,128)}, u32[]{:S(2)}) copy-start(s32[1,1,128]{2,1,0:T(1,128)} %param.16) | copy-start | bytes 1540

commit v6 on v5

--- a/solution.py
+++ b/solution.py
@@ -17,6 +17,7 @@
 SUB = 8
 TURN_ROWS = 88
 GROUPS = 4
+CHUNK = 4
 
 harmonic_order = (0, 2, 6, 3, 7, 1, 5, 8, 4)
 norm_epsilon = 1e-06
@@ -213,7 +214,6 @@
         mixed,
         height,
         normed_low,
-        up_value,
         hidden,
         grad_up,
         packed,
@@ -285,43 +285,55 @@
 
         over_channels(gather_messages)
 
-    def atom_sum(value):
-        total = sum(value[:, lanes(col, atoms_n)] for col in range(HARM))
-        return jnp.sum(total, axis=0, keepdims=True)
-
-    def each(value):
-        return jnp.concatenate([value] * HARM, axis=1)
-
-    mean = atom_sum(height[...] * height[...]) * (1.0 / (HARM * C))
-    inverse = lax.rsqrt(mean + norm_epsilon)
-    normed_low[...] = (height[...] * each(inverse)).astype(BF16)
+    squares = jnp.zeros((C, atoms_n), F32)
+    for col in range(HARM):
+        value = height[:, lanes(col, atoms_n)]
+        squares = squares + value * value
+    mean = jnp.sum(squares, axis=0, keepdims=True) * (1.0 / (HARM * C))
+    inverse = jnp.broadcast_to(lax.rsqrt(mean + norm_epsilon), (C, atoms_n))
+    for col in range(HARM):
+        here = lanes(col, atoms_n)
+        normed_low[:, here] = (height[:, here] * inverse).astype(BF16)
     gate = jax.nn.sigmoid(dot(gate_t[...], normed_low[:, 0:atoms_n]) * C**-0.5)
     up_gate, down_gate = gate * C**-0.5, gate * FFH**-0.5
-    up_value[...] = dot(up_t[...], normed_low[...])
+    chunks = [list(range(col, min(col + CHUNK, HARM))) for col in range(0, HARM, CHUNK)]
+    gate_sum = jnp.zeros_like(gate)
+    for chunk in chunks:
+        wide = slice(chunk[0] * atoms_n, (chunk[-1] + 1) * atoms_n)
+        up_here = dot(up_t[...], normed_low[:, wide])
+        grad_here = dot(down_w[...], cot_t[:, wide])
+        for place, col in enumerate(chunk):
+            here, there = lanes(col, atoms_n), lanes(place, atoms_n)
+            hidden[:, here] = (up_here[:, there] * up_gate).astype(BF16)
+            grad_up[:, here] = (grad_here[:, there] * down_gate).astype(BF16)
+            gate_sum = gate_sum + grad_here[:, there] * up_here[:, there]
+    gate_sum = gate_sum * (C**-0.5 * FFH**-0.5)
+    grad_gate = (gate_sum * gate * (1.0 - gate)).astype(BF16)
+    overlap = jnp.zeros((C, atoms_n), F32)
+    for chunk in chunks:
+        wide = slice(chunk[0] * atoms_n, (chunk[-1] + 1) * atoms_n)
+        projected = dot(down_t[...], hidden[:, wide])
+        along = dot(up_w[...], grad_up[:, wide])
+        for place, col in enumerate(chunk):
+            here, there = lanes(col, atoms_n), lanes(place, atoms_n)
+            value = height[:, here]
+            output_rows[:, lanes(col)] = (
+                (value + projected[:, there] * FFH**-0.5).astype(BF16).T
+            )
+            along_here = along[:, there]
+            if col == 0:
+                along_here = along_here + dot(gate_w[...], grad_gate)
+            height_grad[:, here] = along_here
+            overlap = overlap + along_here * value
+    output_copy.start()
+    overlap = jnp.sum(overlap, axis=0, keepdims=True) * (C**-0.5 / (HARM * C))
+    scale = inverse * C**-0.5
+    weight = inverse * inverse * (inverse * overlap)
     for col in range(HARM):
         here = lanes(col, atoms_n)
-        hidden[:, here] = (up_value[:, here] * up_gate).astype(BF16)
-    projected = dot(down_t[...], hidden[...])
-    for col in range(HARM):
-        here = lanes(col, atoms_n)
-        result = (height[:, here] + projected[:, here] * FFH**-0.5).astype(BF16)
-        output_rows[:, lanes(col)] = result.T
-    output_copy.start()
-    gate_sum = jnp.zeros_like(gate)
-    for col in range(HARM):
-        here = lanes(col, atoms_n)
-        grad_hidden = dot(down_w[...], cot_t[:, here])
-        grad_up[:, here] = (grad_hidden * down_gate).astype(BF16)
-        gate_sum = gate_sum + grad_hidden * up_value[:, here]
-    gate_sum = gate_sum * (C**-0.5 * FFH**-0.5)
-    grad_gate = (gate_sum * gate * (1.0 - gate)).astype(BF16)
-    along = dot(up_w[...], grad_up[...]) * C**-0.5
-    gate_along = dot(gate_w[...], grad_gate) * C**-0.5
-    along = jnp.concatenate([along[:, 0:atoms_n] + gate_along, along[:, atoms_n:]], axis=1)
-    overlap = atom_sum(along * height[...]) * (inverse * (1.0 / (HARM * C)))
-    height_grad[...] = cot_t[...].astype(F32) + each(inverse) * (
-        along - height[...] * each(inverse * overlap)
-    )
+        height_grad[:, here] = (
+            cot_t[:, here].astype(F32) + scale * height_grad[:, here] - weight * height[:, here]
+        )
 
     for k in range(K):
         here = lanes(k, atoms_n)
@@ -368,15 +380,19 @@
     shard_rows = PACK_ROWS // node_count
     part_rows = shard_rows // edge_parts
     edge_low = lax.axis_index("edge") & (edge_parts - 1)
-    bits = node_count.bit_length() - 1
+    high_bits = node_count.bit_length() - 2
     blocks = []
-    for place in range(node_count):
-        distance = int(format(place, "b").zfill(bits)[::-1], 2) if bits else 0
+    for low in range(2):
         for part in range(edge_parts):
-            blocks.append((node ^ distance) * shard_rows + (edge_low ^ part) * part_rows)
+            for place in range(node_count // 2):
+                high = int(format(place, "b").zfill(high_bits)[::-1], 2) if high_bits else 0
+                distance = low | (high << 1)
+                blocks.append((node ^ distance) * shard_rows + (edge_low ^ part) * part_rows)
     half = len(blocks) // 2
     for number, first in enumerate(blocks):
-        values = packed[pl.ds(pl.multiple_of(first, 8), part_rows), :].astype(BF16)
+        if part_rows % SUB == 0:
+            first = pl.multiple_of(first, SUB)
+        values = packed[pl.ds(first, part_rows), :].astype(BF16)
         target = keep_ref if number < half else send_ref
         target[lanes(number % half, part_rows), :] = values
     output_copy.wait()
@@ -456,14 +472,8 @@
     return lax.ppermute(value, axis, [(i, i ^ (1 << bit)) for i in range(size)])
 
 
-def swap_both(value, node_step, edge_step):
-    nodes, edges = lax.axis_size("node"), lax.axis_size("edge")
-    pairs = [
-        (n * edges + e, (n ^ node_step) * edges + (e ^ edge_step))
-        for n in range(nodes)
-        for e in range(edges)
-    ]
-    return lax.ppermute(value, ("node", "edge"), pairs)
+def swap_edge(value, step):
+    return lax.ppermute(value, "edge", [(e, e ^ step) for e in range(lax.axis_size("edge"))])
 
 
 def shards(
@@ -487,7 +497,6 @@
     slots_n = sends.shape[-1]
     per_peer = slots_n // edge_size
     edges_n = atoms_n * K
-    edge_parts = 2
 
     spaces = {"vmem": pltpu.VMEM, "smem": pltpu.SMEM, "hbm": pltpu.HBM, "auto": pltpu.VMEM}
 
@@ -558,7 +567,7 @@
     sides = (slots_t, turn, gains_kept, *unpacked[3:], atoms_t, cot_t)
     read_again = (*unpacked[:3], turn, slots_t)
     output, height_grad, grad_mixed, keep, send = call(
-        functools.partial(main_kernel, edge_parts, node_size, atoms_n * node_size * edge_size),
+        functools.partial(main_kernel, 4, node_size, atoms_n * node_size * edge_size),
         [
             ("hbm", (atoms_n, features), BF16),
             ("vmem", (C, wide), F32),
@@ -577,7 +586,6 @@
             pltpu.VMEM((HARM, C, edges_n), F32),
             pltpu.VMEM((C, wide), F32),
             pltpu.VMEM((C, wide), BF16),
-            pltpu.VMEM((FFH, wide), F32),
             pltpu.VMEM((FFH, wide), BF16),
             pltpu.VMEM((FFH, wide), BF16),
             pltpu.VMEM((PACK_ROWS, C), F32),
@@ -602,33 +610,33 @@
     def add_low(left, right):
         return (left.astype(F32) + right.astype(F32)).astype(BF16)
 
-    for bit in range(node_bits - 1):
-        if bit:
-            half = keep.shape[0] // 2
-            keep, send = keep[:half], keep[half:]
-        keep = add_low(keep, swap(send, "node", bit))
+    keep = add_low(keep, swap(send, "node", 0))
     quarter = keep.shape[0] // 4
     total = keep[:quarter].astype(F32)
     for number in (2, 3, 1):
-        came = swap_both(
-            keep[number * quarter : (number + 1) * quarter],
-            (number >> 1) << (node_bits - 1),
-            number & 1,
-        )
+        came = swap_edge(keep[number * quarter : (number + 1) * quarter], number)
         total = total + came.astype(F32)
     grads = total.astype(BF16)
     for bit in reversed(range(2, edge_bits)):
         grads = add_low(grads, swap(grads, "edge", bit))
-    far = swap_both(grads, 0, 2)
-    both = swap_both(grads, 0, 3)
-    near = swap_both(grads, 0, 1)
-    own_half = grads.astype(F32) + far.astype(F32)
-    other_half = near.astype(F32) + both.astype(F32)
-    is_low = (lax.axis_index("edge") & 1) == 0
-    grads = jnp.concatenate(
-        [jnp.where(is_low, own_half, other_half), jnp.where(is_low, other_half, own_half)],
-        axis=0,
-    )
+    for bit in range(1, node_bits):
+        half = grads.shape[0] // 2
+        grads = add_low(grads[:half], swap(grads[half:], "node", bit))
+    pieces = [grads]
+    for number in (2, 3, 1):
+        pieces.append(swap_edge(grads, number))
+    first, third, fourth, second = pieces
+    low = lax.axis_index("edge") & 1
+    high = lax.axis_index("edge") & 2
+
+    def exchange_if(flag, left, right):
+        return jnp.where(flag, right, left), jnp.where(flag, left, right)
+
+    first, second = exchange_if(low != 0, first, second)
+    third, fourth = exchange_if(low != 0, third, fourth)
+    first, third = exchange_if(high != 0, first, third)
+    second, fourth = exchange_if(high != 0, second, fourth)
+    grads = jnp.concatenate([first, second, third, fourth], axis=0).astype(F32)
 
     returned = peers_exchange(slot_grad)
     (grad_atoms,) = call(

time: 77.8 us -> 81.3 us (1.045)
  waiting for transfers between devices: 29.5 us -> 33 us
    ppermute x5 -> x6, waiting for transfers between devices: 11 us -> 14 us  [swap(): return lax.ppermute(value, axis, [(i, i ^ 1 << bit) for i in range(size)])]
    ppermute x6, waiting for transfers between devices: 5.16 us -> 6.52 us  [swap_edge(): lax.ppermute(value, 'edge', [(e, e ^ step) for e in range(lax.axis_size('...]
    ppermute x5 -> x6, starting transfers between devices: 4.75 us -> 6.1 us  [swap(): return lax.ppermute(value, axis, [(i, i ^ 1 << bit) for i in range(size)])]
    all_to_all x2, starting transfers between devices: 13 us -> 12 us  [peers_exchange(): lax.all_to_all(value, 'edge', split_axis=0, concat_axis=0, tiled=True)]
    all_to_all x2, waiting for transfers between devices: 13.3 us -> 12.5 us  [peers_exchange(): lax.all_to_all(value, 'edge', split_axis=0, concat_axis=0, tiled=True)]
  transfers between devices with their start and end apart: 13 -> 14, of which waited for: 7 -> 8; matrix products, arithmetic and copies ran while one was open for 2% -> 2% of each run, Pallas kernels for 12% -> 11%
where the time goes in v6:
time: 81.3 us; the launch traced here: 80.9 us
  waiting for transfers between devices  33 us (41%)
  starting transfers between devices  25.2 us (31%)
  Pallas kernels  19.2 us (24%)
  other arithmetic  1.5 us (2%)
  between operations  1.45 us (2%)
    pallas_call x6, Pallas kernels, call(): pl.pallas_call(kernel, out_shape=tuple((typed_out(*out) for out in outs))...  19.2 us
    ppermute x6, waiting for transfers between devices, swap(): return lax.ppermute(value, axis, [(i, i ^ 1 << bit) for i in range(size)])  14 us
    all_to_all x2, waiting for transfers between devices, peers_exchange(): lax.all_to_all(value, 'edge', split_axis=0, concat_axis=0, tiled=True)  12.5 us
    all_to_all x2, starting transfers between devices, peers_exchange(): lax.all_to_all(value, 'edge', split_axis=0, concat_axis=0, tiled=True)  12 us
    ppermute x6, starting transfers between devices, swap_edge(): lax.ppermute(value, 'edge', [(e, e ^ step) for e in range(lax.axis_size('...  7.11 us
    ppermute x6, waiting for transfers between devices, swap_edge(): lax.ppermute(value, 'edge', [(e, e ^ step) for e in range(lax.axis_size('...  6.52 us
    ppermute x6, starting transfers between devices, swap(): return lax.ppermute(value, axis, [(i, i ^ 1 << bit) for i in range(size)])  6.1 us
  transfers between devices with their start and end apart: 14, of which 8 were waited for; matrix products, arithmetic and copies ran while one was open for 2% of the time, Pallas kernels for 11%

profile of v6, /device:TPU:0, one launch (start us, length us, event | category | flops | bytes accessed | tf_op | source)
XLA Modules:
  0.0 80.9 jit_solution(11470996832143800500)
XLA Ops:
  0.6 0.0 copy-start.4
  0.6 2.1 %shard_map.146 = (bf16[128,1152]{1,0:T(8,128)(2,1)}, bf16[800,128]{1,0:T(8,128)(2,1)S(1)}) custom-call(s32[1,128]{1,0:T(1,128)} %bitcast.21, bf16[128,1152]{1,0:T(8,128)(2,1)} %atoms_ref.3, f32[800,128]{1,0:T(8,128)} %bitcast.23), custom_call_target="tpu_custom_call" | custom-call | tf_op jit(solution)/shard_map/pallas_call | solution.py:515
  2.8 7.3 %all-to-all-start = ((bf16[8,16,1152]{2,1,0:T(8,128)(2,1)}), bf16[8,16,1152]{2,1,0:T(8,128)(2,1)S(1)}, u32[]{:S(2)}, u32[]{:S(2)}) async-start(bf16[8,16,1152]{2,1,0:T(8,128)(2,1)} %bitcast.2), calls=%async_computation | async-start | bytes 589824 | tf_op jit(solution)/shard_map/all_to_all | solution.py:526
  10.1 1.5 %collective-permute-start.1 = (bf16[800,128]{1,0:T(8,128)(2,1)S(1)}, bf16[800,128]{1,0:T(8,128)(2,1)S(1)}, u32[]{:S(2)}, u32[]{:S(2)}) collective-permute-start(bf16[800,128]{1,0:T(8,128)(2,1)S(1)} %get-tuple-element.33.refs_0_), channel_id=1, source_target_pairs={{0,16},{8,24},{16,0},{24,8},{1,17},{9,25},{17,1},{25,9},{2,18},{10... | collective-permute-start | bytes 614408 | tf_op jit(solution)/shard_map/ppermute | solution.py:472
  11.6 0.0 collective-permute-start
  11.6 5.0 %collective-permute-done.1.refs_2_ = bf16[800,128]{1,0:T(8,128)(2,1)S(1)} collective-permute-done((bf16[800,128]{1,0:T(8,128)(2,1)S(1)}, bf16[800,128]{1,0:T(8,128)(2,1)S(1)}, u32[]{:S(2)}, u32[]{:S(2)}) %collective-permute-start.1) | collective-permute-done | bytes 204832 | tf_op jit(solution)/shard_map/ppermute | solution.py:472
  16.6 0.0 collective-permute-start.2
  16.6 0.0 copy-done.4
  16.6 0.6 reshape.46.table_ref
  17.9 2.2 %shard_map.147 = (bf16[128,1152]{1,0:T(8,128)(2,1)}, bf16[128,1152]{1,0:T(8,128)(2,1)}, f32[352,128]{1,0:T(8,128)}, f32[4,128]{1,0:T(4,128)}) custom-call(s32[1,1]{1,0:T(1,128)S(6)} %copy.16.live_ref, bf16[128,1152]{1,0:T(8,128)(2,1)} %atoms_ref.3, bf16[128,1152]{1,0:T(8,128)(2,1)} %cot_ref.1, s32[4,128]{1,0:T(4,128)} %bitcast.27, f32[4,128]{1,0:T(4,128)} %bitcast.28, ...), custom_call_target="tpu_custom_call" | custom-call | tf_op jit(solution)/shard_map/pallas_call | solution.py:515
  20.1 0.0 collective-permute-done.refs_1_
  20.1 0.0 collective-permute-done.2.refs_3_
  20.1 1.8 %shard_map.148 = (bf16[384,384]{1,0:T(8,128)(2,1)}, bf16[512,512]{1,0:T(8,128)(2,1)}, bf16[256,256]{1,0:T(8,128)(2,1)}, bf16[384,384]{1,0:T(8,128)(2,1)}, bf16[5...) custom-call(bf16[800,128]{1,0:T(8,128)(2,1)S(1)} %get-tuple-element., ...), custom_call_target="tpu_custom_call" | custom-call | tf_op jit(solution)/shard_map/pallas_call | solution.py:515
  21.9 0.0 all-to-all-done
  21.9 6.9 %shard_map.149 = (bf16[128,1152]{1,0:T(8,128)(2,1)}, f32[128,1152]{1,0:T(8,128)S(1)}, bf16[9,128,512]{2,1,0:T(8,128)(2,1)S(1)}, bf16[1600,128]{1,0:T(8,128)(2,1)S(1)}, bf16[1600,128]{1,0:T(8,128)(2,1)S(1)}) custom-call(bf16[128,1152]{1,0:T(8,128)(2,1)S(1)} %bitcast.20, s32[4,128]{1,0:T(4,128)} %bitcast.25, f32[352,128]{1,0:T(8,128)} %get-tuple-element.31.refs_2_.refs_3_, ...), custom_call_target="tpu_custom_call" | custom-call | tf_op jit(solution)/shard_map/pallas_call | solution.py:515
  28.8 0.6 collective-permute-start.3
  29.3 1.4 %collective-permute-done.3 = bf16[1600,128]{1,0:T(8,128)(2,1)S(1)} collective-permute-done((bf16[1600,128]{1,0:T(8,128)(2,1)S(1)}, bf16[1600,128]{1,0:T(8,128)(2,1)S(1)}, u32[]{:S(2)}, u32[]{:S(2)}) %collective-permute-start.3) | collective-permute-done | bytes 409632 | tf_op jit(solution)/shard_map/ppermute | solution.py:472
  30.7 0.1 add_convert_fusion
  30.9 1.8 %collective-permute-start.4 = (bf16[400,128]{1,0:T(8,128)(2,1)S(1)}, bf16[400,128]{1,0:T(8,128)(2,1)S(1)}, u32[]{:S(2)}, u32[]{:S(2)}) collective-permute-start(bf16[400,128]{1,0:T(8,128)(2,1)S(1)} %get-tuple-element.58), channel_id=1, source_target_pairs={{0,2},{1,3},{2,0},{3,1},{4,6},{5,7},{6,4},{7,5},{8,10},{9,11},{10,... | collective-permute-start | bytes 307208 | tf_op jit(solution)/shard_map/ppermute | solution.py:476
  32.7 1.5 %collective-permute-start.5 = (bf16[400,128]{1,0:T(8,128)(2,1)S(1)}, bf16[400,128]{1,0:T(8,128)(2,1)S(1)}, u32[]{:S(2)}, u32[]{:S(2)}) collective-permute-start(bf16[400,128]{1,0:T(8,128)(2,1)S(1)} %get-tuple-element.60), channel_id=1, source_target_pairs={{0,3},{1,2},{2,1},{3,0},{4,7},{5,6},{6,5},{7,4},{8,11},{9,10},{10,... | collective-permute-start | bytes 307208 | tf_op jit(solution)/shard_map/ppermute | solution.py:476
  34.1 0.3 collective-permute-start.6
  34.4 1.7 %collective-permute-done.4 = bf16[400,128]{1,0:T(8,128)(2,1)S(1)} collective-permute-done((bf16[400,128]{1,0:T(8,128)(2,1)S(1)}, bf16[400,128]{1,0:T(8,128)(2,1)S(1)}, u32[]{:S(2)}, u32[]{:S(2)}) %collective-permute-start.4) | collective-permute-done | bytes 102432 | tf_op jit(solution)/shard_map/ppermute | solution.py:476
  36.1 3.5 %collective-permute-done.5 = bf16[400,128]{1,0:T(8,128)(2,1)S(1)} collective-permute-done((bf16[400,128]{1,0:T(8,128)(2,1)S(1)}, bf16[400,128]{1,0:T(8,128)(2,1)S(1)}, u32[]{:S(2)}, u32[]{:S(2)}) %collective-permute-start.5) | collective-permute-done | bytes 102432 | tf_op jit(solution)/shard_map/ppermute | solution.py:476
  39.6 1.4 %collective-permute-done.6 = bf16[400,128]{1,0:T(8,128)(2,1)S(1)} collective-permute-done((bf16[400,128]{1,0:T(8,128)(2,1)S(1)}, bf16[400,128]{1,0:T(8,128)(2,1)S(1)}, u32[]{:S(2)}, u32[]{:S(2)}) %collective-permute-start.6) | collective-permute-done | bytes 102432 | tf_op jit(solution)/shard_map/ppermute | solution.py:476
  40.9 0.1 add_convert_fusion.2
  41.0 2.4 %collective-permute-start.7 = (bf16[400,128]{1,0:T(8,128)(2,1)S(1)}, bf16[400,128]{1,0:T(8,128)(2,1)S(1)}, u32[]{:S(2)}, u32[]{:S(2)}) collective-permute-start(bf16[400,128]{1,0:T(8,128)(2,1)S(1)} %add_convert_fusion.2), channel_id=1, source_target_pairs={{0,4},{1,5},{2,6},{3,7},{4,0},{5,1},{6,2},{7,3},{8,12},{9,13},{10,... | collective-permute-start | bytes 307208 | tf_op jit(solution)/shard_map/ppermute | solution.py:472
  43.4 5.0 %collective-permute-done.7 = bf16[400,128]{1,0:T(8,128)(2,1)S(1)} collective-permute-done((bf16[400,128]{1,0:T(8,128)(2,1)S(1)}, bf16[400,128]{1,0:T(8,128)(2,1)S(1)}, u32[]{:S(2)}, u32[]{:S(2)}) %collective-permute-start.7) | collective-permute-done | bytes 102432 | tf_op jit(solution)/shard_map/ppermute | solution.py:472
  48.5 1.6 %collective-permute-start.8 = (bf16[200,128]{1,0:T(8,128)(2,1)S(1)}, bf16[200,128]{1,0:T(8,128)(2,1)S(1)}, u32[]{:S(2)}, u32[]{:S(2)}) collective-permute-start(bf16[200,128]{1,0:T(8,128)(2,1)S(1)} %slice.29), channel_id=1, source_target_pairs={{0,16},{8,24},{16,0},{24,8},{1,17},{9,25},{17,1},{25,9},{2,18},{10... | collective-permute-start | bytes 153608 | tf_op jit(solution)/shard_map/ppermute | solution.py:472
  50.0 2.6 %collective-permute-done.8 = bf16[200,128]{1,0:T(8,128)(2,1)S(1)} collective-permute-done((bf16[200,128]{1,0:T(8,128)(2,1)S(1)}, bf16[200,128]{1,0:T(8,128)(2,1)S(1)}, u32[]{:S(2)}, u32[]{:S(2)}) %collective-permute-start.8) | collective-permute-done | bytes 51232 | tf_op jit(solution)/shard_map/ppermute | solution.py:472
  52.7 0.5 collective-permute-start.10
  53.2 0.4 collective-permute-start.11
  53.5 2.7 %collective-permute-start.9 = (bf16[200,128]{1,0:T(8,128)(2,1)S(1)}, bf16[200,128]{1,0:T(8,128)(2,1)S(1)}, u32[]{:S(2)}, u32[]{:S(2)}) collective-permute-start(bf16[200,128]{1,0:T(8,128)(2,1)S(1)} %add_convert_fusion.3), channel_id=1, source_target_pairs={{0,3},{1,2},{2,1},{3,0},{4,7},{5,6},{6,5},{7,4},{8,11},{9,10},{10,... | collective-permute-start | bytes 153608 | tf_op jit(solution)/shard_map/ppermute | solution.py:476
  56.2 5.0 %shard_map.150 = (f32[128,1152]{1,0:T(8,128)}, f32[128,1152]{1,0:T(8,128)S(1)}) custom-call(bf16[9,128,512]{2,1,0:T(8,128)(2,1)S(1)} %get-tuple-element.46.grad_mixed, f32[128,1152]{1,0:T(8,128)S(1)} %get-tuple-element.47.height_grad, bf16[384,384]{1,0:T(8,128)(2,1)} %get-tuple-element.48.refs_0_, bf16[512,512]{1,0:T(8,128)(2,1)} %get-tuple-element.49.refs_1_, ...), custom_call_target="tpu_custom_call" | custom-call | tf_op jit(solution)/shard_map/pallas_call | solution.py:515
  61.3 0.0 copy-start.1
  61.3 0.0 copy-start.2
  61.3 0.0 copy-start.3
  61.3 4.7 %all-to-all-start.1 = ((f32[8,16,1152]{2,1,0:T(8,128)}), f32[8,16,1152]{2,1,0:T(8,128)S(1)}, u32[]{:S(2)}, u32[]{:S(2)}) async-start(f32[8,16,1152]{2,1,0:T(8,128)} %bitcast.8), calls=%async_computation.1 | async-start | bytes 1179648 | tf_op jit(solution)/shard_map/all_to_all | solution.py:526
  66.0 0.0 collective-permute-done.10
  66.0 0.0 collective-permute-done.11
  66.0 0.0 collective-permute-done.9
  66.0 0.1 broadcast_select_fusion.7
  66.1 0.0 copy-done.1
  66.1 0.0 copy-done.2
  66.1 0.0 copy-done.3
  66.1 0.0 copy-start
  66.1 1.2 %multiply_subtract_fusion = (f32[102400]{0:T(1024)}, f32[102400]{0:T(1024)}, f32[102400]{0:T(1024)}) fusion(f32[102400]{0:T(1024)S(1)} %copy-done.1, bf16[200,128]{1,0:T(8,128)(2,1)S(1)} %get-tuple-element.64, bf16[200,128]{1,0:T(8,128)(2,1)S(1)} %get-tuple-element.63, bf16[200,128]{1,0:T(8,128)(2,1)S(1)} %get-tuple-element.62, ...), kind=kLoop, calls=%fused_computation.6 | loop fusion | flops 2355200 | bytes 2662400 | tf_op jit(solution)/shard_map/sub | solution.py:467
  67.3 12.5 %all-to-all-done.1 = f32[8,16,1152]{2,1,0:T(8,128)S(1)} async-done(((f32[8,16,1152]{2,1,0:T(8,128)}), f32[8,16,1152]{2,1,0:T(8,128)S(1)}, u32[]{:S(2)}, u32[]{:S(2)}) %all-to-all-start.1) | async-done | bytes 589856 | tf_op jit(solution)/shard_map/all_to_all | solution.py:526
  79.8 1.1 %shard_map.151 = bf16[128,1152]{1,0:T(8,128)(2,1)} custom-call(s32[1,128]{1,0:T(1,128)S(1)} %bitcast.22, f32[128,1152]{1,0:T(8,128)S(1)} %get-tuple-element.51.height_rows_ref, f32[128,1152]{1,0:T(8,128)S(1)} %bitcast.19), custom_call_target="tpu_custom_call" | custom-call | tf_op jit(solution)/shard_map/pallas_call | solution.py:515
  (5 shorter events, 0.1 us)
Async XLA Ops:
  0.6 16.0 %copy-start.4 = (f32[64,9,9]{0,2,1:T(8,128)S(1)}, f32[64,9,9]{0,2,1:T(8,128)}, u32[]{:S(2)}) copy-start(f32[64,9,9]{0,2,1:T(8,128)} %param.19) | copy-start | bytes 62212
  2.8 19.1 %all-to-all-start = ((bf16[8,16,1152]{2,1,0:T(8,128)(2,1)}), bf16[8,16,1152]{2,1,0:T(8,128)(2,1)S(1)}, u32[]{:S(2)}, u32[]{:S(2)}) async-start(bf16[8,16,1152]{2,1,0:T(8,128)(2,1)} %bitcast.2), calls=%async_computation | async-start | bytes 589824 | tf_op jit(solution)/shard_map/all_to_all | solution.py:526
  10.1 6.5 %collective-permute-start.1 = (bf16[800,128]{1,0:T(8,128)(2,1)S(1)}, bf16[800,128]{1,0:T(8,128)(2,1)S(1)}, u32[]{:S(2)}, u32[]{:S(2)}) collective-permute-start(bf16[800,128]{1,0:T(8,128)(2,1)S(1)} %get-tuple-element.33.refs_0_), channel_id=1, source_target_pairs={{0,16},{8,24},{16,0},{24,8},{1,17},{9,25},{17,1},{25,9},{2,18},{10... | collective-permute-start | bytes 614408 | tf_op jit(solution)/shard_map/ppermute | solution.py:472
  11.6 8.5 %collective-permute-start = (bf16[800,128]{1,0:T(8,128)(2,1)S(1)}, bf16[800,128]{1,0:T(8,128)(2,1)S(1)}, u32[]{:S(2)}, u32[]{:S(2)}) collective-permute-start(bf16[800,128]{1,0:T(8,128)(2,1)S(1)} %get-tuple-element.33.refs_0_), channel_id=1, source_target_pairs={{0,8},{8,0},{16,24},{24,16},{1,9},{9,1},{17,25},{25,17},{2,10},{10... | collective-permute-start | bytes 614408 | tf_op jit(solution)/shard_map/ppermute | solution.py:472
  16.6 3.5 %collective-permute-start.2 = (bf16[800,128]{1,0:T(8,128)(2,1)S(1)}, bf16[800,128]{1,0:T(8,128)(2,1)S(1)}, u32[]{:S(2)}, u32[]{:S(2)}) collective-permute-start(bf16[800,128]{1,0:T(8,128)(2,1)S(1)} %collective-permute-done.1.refs_2_), channel_id=1, source_target_pairs={{0,8},{8,0},{16,24},{24,16},{1,9},{9,1},{17,25},{25,17},{2,10},{10... | collective-permute-start | bytes 614408 | tf_op jit(solution)/shard_map/ppermute | solution.py:472
  28.8 1.9 %collective-permute-start.3 = (bf16[1600,128]{1,0:T(8,128)(2,1)S(1)}, bf16[1600,128]{1,0:T(8,128)(2,1)S(1)}, u32[]{:S(2)}, u32[]{:S(2)}) collective-permute-start(bf16[1600,128]{1,0:T(8,128)(2,1)S(1)} %get-tuple-element.54), channel_id=1, source_target_pairs={{0,8},{8,0},{16,24},{24,16},{1,9},{9,1},{17,25},{25,17},{2,10},{10... | collective-permute-start | bytes 1228808 | tf_op jit(solution)/shard_map/ppermute | solution.py:472
  30.9 5.2 %collective-permute-start.4 = (bf16[400,128]{1,0:T(8,128)(2,1)S(1)}, bf16[400,128]{1,0:T(8,128)(2,1)S(1)}, u32[]{:S(2)}, u32[]{:S(2)}) collective-permute-start(bf16[400,128]{1,0:T(8,128)(2,1)S(1)} %get-tuple-element.58), channel_id=1, source_target_pairs={{0,2},{1,3},{2,0},{3,1},{4,6},{5,7},{6,4},{7,5},{8,10},{9,11},{10,... | collective-permute-start | bytes 307208 | tf_op jit(solution)/shard_map/ppermute | solution.py:476
  32.7 6.9 %collective-permute-start.5 = (bf16[400,128]{1,0:T(8,128)(2,1)S(1)}, bf16[400,128]{1,0:T(8,128)(2,1)S(1)}, u32[]{:S(2)}, u32[]{:S(2)}) collective-permute-start(bf16[400,128]{1,0:T(8,128)(2,1)S(1)} %get-tuple-element.60), channel_id=1, source_target_pairs={{0,3},{1,2},{2,1},{3,0},{4,7},{5,6},{6,5},{7,4},{8,11},{9,10},{10,... | collective-permute-start | bytes 307208 | tf_op jit(solution)/shard_map/ppermute | solution.py:476
  34.1 6.8 %collective-permute-start.6 = (bf16[400,128]{1,0:T(8,128)(2,1)S(1)}, bf16[400,128]{1,0:T(8,128)(2,1)S(1)}, u32[]{:S(2)}, u32[]{:S(2)}) collective-permute-start(bf16[400,128]{1,0:T(8,128)(2,1)S(1)} %get-tuple-element.59), channel_id=1, source_target_pairs={{0,1},{1,0},{2,3},{3,2},{4,5},{5,4},{6,7},{7,6},{8,9},{9,8},{10,11... | collective-permute-start | bytes 307208 | tf_op jit(solution)/shard_map/ppermute | solution.py:476
  41.0 7.4 %collective-permute-start.7 = (bf16[400,128]{1,0:T(8,128)(2,1)S(1)}, bf16[400,128]{1,0:T(8,128)(2,1)S(1)}, u32[]{:S(2)}, u32[]{:S(2)}) collective-permute-start(bf16[400,128]{1,0:T(8,128)(2,1)S(1)} %add_convert_fusion.2), channel_id=1, source_target_pairs={{0,4},{1,5},{2,6},{3,7},{4,0},{5,1},{6,2},{7,3},{8,12},{9,13},{10,... | collective-permute-start | bytes 307208 | tf_op jit(solution)/shard_map/ppermute | solution.py:472
  48.5 4.2 %collective-permute-start.8 = (bf16[200,128]{1,0:T(8,128)(2,1)S(1)}, bf16[200,128]{1,0:T(8,128)(2,1)S(1)}, u32[]{:S(2)}, u32[]{:S(2)}) collective-permute-start(bf16[200,128]{1,0:T(8,128)(2,1)S(1)} %slice.29), channel_id=1, source_target_pairs={{0,16},{8,24},{16,0},{24,8},{1,17},{9,25},{17,1},{25,9},{2,18},{10... | collective-permute-start | bytes 153608 | tf_op jit(solution)/shard_map/ppermute | solution.py:472
  52.7 13.3 %collective-permute-start.10 = (bf16[200,128]{1,0:T(8,128)(2,1)S(1)}, bf16[200,128]{1,0:T(8,128)(2,1)S(1)}, u32[]{:S(2)}, u32[]{:S(2)}) collective-permute-start(bf16[200,128]{1,0:T(8,128)(2,1)S(1)} %add_convert_fusion.3), channel_id=1, source_target_pairs={{0,2},{1,3},{2,0},{3,1},{4,6},{5,7},{6,4},{7,5},{8,10},{9,11},{10,... | collective-permute-start | bytes 153608 | tf_op jit(solution)/shard_map/ppermute | solution.py:476
  53.2 12.8 %collective-permute-start.11 = (bf16[200,128]{1,0:T(8,128)(2,1)S(1)}, bf16[200,128]{1,0:T(8,128)(2,1)S(1)}, u32[]{:S(2)}, u32[]{:S(2)}) collective-permute-start(bf16[200,128]{1,0:T(8,128)(2,1)S(1)} %add_convert_fusion.3), channel_id=1, source_target_pairs={{0,1},{1,0},{2,3},{3,2},{4,5},{5,4},{6,7},{7,6},{8,9},{9,8},{10,11... | collective-permute-start | bytes 153608 | tf_op jit(solution)/shard_map/ppermute | solution.py:476
  53.5 12.4 %collective-permute-start.9 = (bf16[200,128]{1,0:T(8,128)(2,1)S(1)}, bf16[200,128]{1,0:T(8,128)(2,1)S(1)}, u32[]{:S(2)}, u32[]{:S(2)}) collective-permute-start(bf16[200,128]{1,0:T(8,128)(2,1)S(1)} %add_convert_fusion.3), channel_id=1, source_target_pairs={{0,3},{1,2},{2,1},{3,0},{4,7},{5,6},{6,5},{7,4},{8,11},{9,10},{10,... | collective-permute-start | bytes 153608 | tf_op jit(solution)/shard_map/ppermute | solution.py:476
  61.3 4.8 %copy-start.1 = (f32[102400]{0:T(1024)S(1)}, f32[102400]{0:T(1024)}, u32[]{:S(2)}) copy-start(f32[102400]{0:T(1024)} %param.13) | copy-start | bytes 1228804
  61.3 4.8 %copy-start.2 = (f32[102400]{0:T(1024)S(1)}, f32[102400]{0:T(1024)}, u32[]{:S(2)}) copy-start(f32[102400]{0:T(1024)} %param.15) | copy-start | bytes 1228804
  61.3 4.8 %copy-start.3 = (f32[102400]{0:T(1024)S(1)}, f32[102400]{0:T(1024)}, u32[]{:S(2)}) copy-start(f32[102400]{0:T(1024)} %param.14) | copy-start | bytes 1228804
  61.3 18.5 %all-to-all-start.1 = ((f32[8,16,1152]{2,1,0:T(8,128)}), f32[8,16,1152]{2,1,0:T(8,128)S(1)}, u32[]{:S(2)}, u32[]{:S(2)}) async-start(f32[8,16,1152]{2,1,0:T(8,128)} %bitcast.8), calls=%async_computation.1 | async-start | bytes 1179648 | tf_op jit(solution)/shard_map/all_to_all | solution.py:526
  66.1 13.7 %copy-start = (s32[1,1,128]{2,1,0:T(1,128)S(1)}, s32[1,1,128]{2,1,0:T(1,128)}, u32[]{:S(2)}) copy-start(s32[1,1,128]{2,1,0:T(1,128)} %param.16) | copy-start | bytes 1540

commit v7 on v6

--- a/solution.py
+++ b/solution.py
@@ -451,9 +451,10 @@
 def finish_kernel(sends_ref, height_rows_ref, back_ref, grad_ref):
     shape = (grad_ref.shape[0], sends_ref.shape[1])
     picks = as_low(lax.broadcasted_iota(jnp.int32, shape, 0) == sends_ref[...])
-    pieces = split_parts(back_ref[...], 3)
-    total = sum(dot(picks, piece) for piece in pieces)
-    grad_ref[...] = (height_rows_ref[...] + total).astype(BF16)
+    for col in range(HARM):
+        pieces = split_parts(back_ref[:, lanes(col)], 2)
+        total = sum(dot(picks, piece) for piece in pieces)
+        grad_ref[:, lanes(col)] = (height_rows_ref[:, lanes(col)] + total).astype(BF16)
 
 
 def adam_step(params, moment_one, moment_two, gradient):

time: 81.3 us -> 81.2 us (level)
  no operation moved by 1% of the time
where the time goes in v7:
time: 81.2 us; the launch traced here: 80.8 us
  waiting for transfers between devices  33 us (41%)
  starting transfers between devices  25.2 us (31%)
  Pallas kernels  19.1 us (24%)
  other arithmetic  1.5 us (2%)
  between operations  1.45 us (2%)
    pallas_call x6, Pallas kernels, call(): pl.pallas_call(kernel, out_shape=tuple((typed_out(*out) for out in outs))...  19.1 us
    ppermute x6, waiting for transfers between devices, swap(): return lax.ppermute(value, axis, [(i, i ^ 1 << bit) for i in range(size)])  14 us
    all_to_all x2, waiting for transfers between devices, peers_exchange(): lax.all_to_all(value, 'edge', split_axis=0, concat_axis=0, tiled=True)  12.5 us
    all_to_all x2, starting transfers between devices, peers_exchange(): lax.all_to_all(value, 'edge', split_axis=0, concat_axis=0, tiled=True)  12 us
    ppermute x6, starting transfers between devices, swap_edge(): lax.ppermute(value, 'edge', [(e, e ^ step) for e in range(lax.axis_size('...  7.11 us
    ppermute x6, waiting for transfers between devices, swap_edge(): lax.ppermute(value, 'edge', [(e, e ^ step) for e in range(lax.axis_size('...  6.52 us
    ppermute x6, starting transfers between devices, swap(): return lax.ppermute(value, axis, [(i, i ^ 1 << bit) for i in range(size)])  6.1 us
  transfers between devices with their start and end apart: 14, of which 8 were waited for; matrix products, arithmetic and copies ran while one was open for 2% of the time, Pallas kernels for 11%

profile of v7, /device:TPU:0, one launch (start us, length us, event | category | flops | bytes accessed | tf_op | source)
XLA Modules:
  0.0 80.8 jit_solution(10265204320650813849)
XLA Ops:
  0.6 0.0 copy-start.4
  0.6 2.1 %shard_map.146 = (bf16[128,1152]{1,0:T(8,128)(2,1)}, bf16[800,128]{1,0:T(8,128)(2,1)S(1)}) custom-call(s32[1,128]{1,0:T(1,128)} %bitcast.21, bf16[128,1152]{1,0:T(8,128)(2,1)} %atoms_ref.3, f32[800,128]{1,0:T(8,128)} %bitcast.23), custom_call_target="tpu_custom_call" | custom-call | tf_op jit(solution)/shard_map/pallas_call | solution.py:516
  2.8 7.3 %all-to-all-start = ((bf16[8,16,1152]{2,1,0:T(8,128)(2,1)}), bf16[8,16,1152]{2,1,0:T(8,128)(2,1)S(1)}, u32[]{:S(2)}, u32[]{:S(2)}) async-start(bf16[8,16,1152]{2,1,0:T(8,128)(2,1)} %bitcast.2), calls=%async_computation | async-start | bytes 589824 | tf_op jit(solution)/shard_map/all_to_all | solution.py:527
  10.1 1.5 %collective-permute-start.1 = (bf16[800,128]{1,0:T(8,128)(2,1)S(1)}, bf16[800,128]{1,0:T(8,128)(2,1)S(1)}, u32[]{:S(2)}, u32[]{:S(2)}) collective-permute-start(bf16[800,128]{1,0:T(8,128)(2,1)S(1)} %get-tuple-element.33.refs_0_), channel_id=1, source_target_pairs={{0,16},{8,24},{16,0},{24,8},{1,17},{9,25},{17,1},{25,9},{2,18},{10... | collective-permute-start | bytes 614408 | tf_op jit(solution)/shard_map/ppermute | solution.py:473
  11.6 0.0 collective-permute-start
  11.6 5.0 %collective-permute-done.1.refs_2_ = bf16[800,128]{1,0:T(8,128)(2,1)S(1)} collective-permute-done((bf16[800,128]{1,0:T(8,128)(2,1)S(1)}, bf16[800,128]{1,0:T(8,128)(2,1)S(1)}, u32[]{:S(2)}, u32[]{:S(2)}) %collective-permute-start.1) | collective-permute-done | bytes 204832 | tf_op jit(solution)/shard_map/ppermute | solution.py:473
  16.6 0.0 collective-permute-start.2
  16.6 0.0 copy-done.4
  16.6 0.6 reshape.46.table_ref
  17.9 2.2 %shard_map.147 = (bf16[128,1152]{1,0:T(8,128)(2,1)}, bf16[128,1152]{1,0:T(8,128)(2,1)}, f32[352,128]{1,0:T(8,128)}, f32[4,128]{1,0:T(4,128)}) custom-call(s32[1,1]{1,0:T(1,128)S(6)} %copy.16.live_ref, bf16[128,1152]{1,0:T(8,128)(2,1)} %atoms_ref.3, bf16[128,1152]{1,0:T(8,128)(2,1)} %cot_ref.1, s32[4,128]{1,0:T(4,128)} %bitcast.27, f32[4,128]{1,0:T(4,128)} %bitcast.28, ...), custom_call_target="tpu_custom_call" | custom-call | tf_op jit(solution)/shard_map/pallas_call | solution.py:516
  20.1 0.0 collective-permute-done.refs_1_
  20.1 0.0 collective-permute-done.2.refs_3_
  20.1 1.8 %shard_map.148 = (bf16[384,384]{1,0:T(8,128)(2,1)}, bf16[512,512]{1,0:T(8,128)(2,1)}, bf16[256,256]{1,0:T(8,128)(2,1)}, bf16[384,384]{1,0:T(8,128)(2,1)}, bf16[5...) custom-call(bf16[800,128]{1,0:T(8,128)(2,1)S(1)} %get-tuple-element., ...), custom_call_target="tpu_custom_call" | custom-call | tf_op jit(solution)/shard_map/pallas_call | solution.py:516
  21.9 0.0 all-to-all-done
  21.9 6.9 %shard_map.149 = (bf16[128,1152]{1,0:T(8,128)(2,1)}, f32[128,1152]{1,0:T(8,128)S(1)}, bf16[9,128,512]{2,1,0:T(8,128)(2,1)S(1)}, bf16[1600,128]{1,0:T(8,128)(2,1)S(1)}, bf16[1600,128]{1,0:T(8,128)(2,1)S(1)}) custom-call(bf16[128,1152]{1,0:T(8,128)(2,1)S(1)} %bitcast.20, s32[4,128]{1,0:T(4,128)} %bitcast.25, f32[352,128]{1,0:T(8,128)} %get-tuple-element.31.refs_2_.refs_3_, ...), custom_call_target="tpu_custom_call" | custom-call | tf_op jit(solution)/shard_map/pallas_call | solution.py:516
  28.8 0.6 collective-permute-start.3
  29.3 1.4 %collective-permute-done.3 = bf16[1600,128]{1,0:T(8,128)(2,1)S(1)} collective-permute-done((bf16[1600,128]{1,0:T(8,128)(2,1)S(1)}, bf16[1600,128]{1,0:T(8,128)(2,1)S(1)}, u32[]{:S(2)}, u32[]{:S(2)}) %collective-permute-start.3) | collective-permute-done | bytes 409632 | tf_op jit(solution)/shard_map/ppermute | solution.py:473
  30.7 0.1 add_convert_fusion
  30.9 1.8 %collective-permute-start.4 = (bf16[400,128]{1,0:T(8,128)(2,1)S(1)}, bf16[400,128]{1,0:T(8,128)(2,1)S(1)}, u32[]{:S(2)}, u32[]{:S(2)}) collective-permute-start(bf16[400,128]{1,0:T(8,128)(2,1)S(1)} %get-tuple-element.58), channel_id=1, source_target_pairs={{0,2},{1,3},{2,0},{3,1},{4,6},{5,7},{6,4},{7,5},{8,10},{9,11},{10,... | collective-permute-start | bytes 307208 | tf_op jit(solution)/shard_map/ppermute | solution.py:477
  32.7 1.5 %collective-permute-start.5 = (bf16[400,128]{1,0:T(8,128)(2,1)S(1)}, bf16[400,128]{1,0:T(8,128)(2,1)S(1)}, u32[]{:S(2)}, u32[]{:S(2)}) collective-permute-start(bf16[400,128]{1,0:T(8,128)(2,1)S(1)} %get-tuple-element.60), channel_id=1, source_target_pairs={{0,3},{1,2},{2,1},{3,0},{4,7},{5,6},{6,5},{7,4},{8,11},{9,10},{10,... | collective-permute-start | bytes 307208 | tf_op jit(solution)/shard_map/ppermute | solution.py:477
  34.1 0.3 collective-permute-start.6
  34.4 1.7 %collective-permute-done.4 = bf16[400,128]{1,0:T(8,128)(2,1)S(1)} collective-permute-done((bf16[400,128]{1,0:T(8,128)(2,1)S(1)}, bf16[400,128]{1,0:T(8,128)(2,1)S(1)}, u32[]{:S(2)}, u32[]{:S(2)}) %collective-permute-start.4) | collective-permute-done | bytes 102432 | tf_op jit(solution)/shard_map/ppermute | solution.py:477
  36.1 3.5 %collective-permute-done.5 = bf16[400,128]{1,0:T(8,128)(2,1)S(1)} collective-permute-done((bf16[400,128]{1,0:T(8,128)(2,1)S(1)}, bf16[400,128]{1,0:T(8,128)(2,1)S(1)}, u32[]{:S(2)}, u32[]{:S(2)}) %collective-permute-start.5) | collective-permute-done | bytes 102432 | tf_op jit(solution)/shard_map/ppermute | solution.py:477
  39.6 1.4 %collective-permute-done.6 = bf16[400,128]{1,0:T(8,128)(2,1)S(1)} collective-permute-done((bf16[400,128]{1,0:T(8,128)(2,1)S(1)}, bf16[400,128]{1,0:T(8,128)(2,1)S(1)}, u32[]{:S(2)}, u32[]{:S(2)}) %collective-permute-start.6) | collective-permute-done | bytes 102432 | tf_op jit(solution)/shard_map/ppermute | solution.py:477
  40.9 0.1 add_convert_fusion.2
  41.0 2.4 %collective-permute-start.7 = (bf16[400,128]{1,0:T(8,128)(2,1)S(1)}, bf16[400,128]{1,0:T(8,128)(2,1)S(1)}, u32[]{:S(2)}, u32[]{:S(2)}) collective-permute-start(bf16[400,128]{1,0:T(8,128)(2,1)S(1)} %add_convert_fusion.2), channel_id=1, source_target_pairs={{0,4},{1,5},{2,6},{3,7},{4,0},{5,1},{6,2},{7,3},{8,12},{9,13},{10,... | collective-permute-start | bytes 307208 | tf_op jit(solution)/shard_map/ppermute | solution.py:473
  43.4 5.0 %collective-permute-done.7 = bf16[400,128]{1,0:T(8,128)(2,1)S(1)} collective-permute-done((bf16[400,128]{1,0:T(8,128)(2,1)S(1)}, bf16[400,128]{1,0:T(8,128)(2,1)S(1)}, u32[]{:S(2)}, u32[]{:S(2)}) %collective-permute-start.7) | collective-permute-done | bytes 102432 | tf_op jit(solution)/shard_map/ppermute | solution.py:473
  48.5 1.6 %collective-permute-start.8 = (bf16[200,128]{1,0:T(8,128)(2,1)S(1)}, bf16[200,128]{1,0:T(8,128)(2,1)S(1)}, u32[]{:S(2)}, u32[]{:S(2)}) collective-permute-start(bf16[200,128]{1,0:T(8,128)(2,1)S(1)} %slice.29), channel_id=1, source_target_pairs={{0,16},{8,24},{16,0},{24,8},{1,17},{9,25},{17,1},{25,9},{2,18},{10... | collective-permute-start | bytes 153608 | tf_op jit(solution)/shard_map/ppermute | solution.py:473
  50.0 2.6 %collective-permute-done.8 = bf16[200,128]{1,0:T(8,128)(2,1)S(1)} collective-permute-done((bf16[200,128]{1,0:T(8,128)(2,1)S(1)}, bf16[200,128]{1,0:T(8,128)(2,1)S(1)}, u32[]{:S(2)}, u32[]{:S(2)}) %collective-permute-start.8) | collective-permute-done | bytes 51232 | tf_op jit(solution)/shard_map/ppermute | solution.py:473
  52.7 0.5 collective-permute-start.10
  53.2 0.4 collective-permute-start.11
  53.5 2.7 %collective-permute-start.9 = (bf16[200,128]{1,0:T(8,128)(2,1)S(1)}, bf16[200,128]{1,0:T(8,128)(2,1)S(1)}, u32[]{:S(2)}, u32[]{:S(2)}) collective-permute-start(bf16[200,128]{1,0:T(8,128)(2,1)S(1)} %add_convert_fusion.3), channel_id=1, source_target_pairs={{0,3},{1,2},{2,1},{3,0},{4,7},{5,6},{6,5},{7,4},{8,11},{9,10},{10,... | collective-permute-start | bytes 153608 | tf_op jit(solution)/shard_map/ppermute | solution.py:477
  56.2 5.0 %shard_map.150 = (f32[128,1152]{1,0:T(8,128)}, f32[128,1152]{1,0:T(8,128)S(1)}) custom-call(bf16[9,128,512]{2,1,0:T(8,128)(2,1)S(1)} %get-tuple-element.46.grad_mixed, f32[128,1152]{1,0:T(8,128)S(1)} %get-tuple-element.47.height_grad, bf16[384,384]{1,0:T(8,128)(2,1)} %get-tuple-element.48.refs_0_, bf16[512,512]{1,0:T(8,128)(2,1)} %get-tuple-element.49.refs_1_, ...), custom_call_target="tpu_custom_call" | custom-call | tf_op jit(solution)/shard_map/pallas_call | solution.py:516
  61.3 0.0 copy-start.1
  61.3 0.0 copy-start.2
  61.3 0.0 copy-start.3
  61.3 4.7 %all-to-all-start.1 = ((f32[8,16,1152]{2,1,0:T(8,128)}), f32[8,16,1152]{2,1,0:T(8,128)S(1)}, u32[]{:S(2)}, u32[]{:S(2)}) async-start(f32[8,16,1152]{2,1,0:T(8,128)} %bitcast.8), calls=%async_computation.1 | async-start | bytes 1179648 | tf_op jit(solution)/shard_map/all_to_all | solution.py:527
  66.0 0.0 collective-permute-done.10
  66.0 0.0 collective-permute-done.11
  66.0 0.0 collective-permute-done.9
  66.0 0.1 broadcast_select_fusion.7
  66.1 0.0 copy-done.1
  66.1 0.0 copy-done.2
  66.1 0.0 copy-done.3
  66.1 0.0 copy-start
  66.1 1.2 %multiply_subtract_fusion = (f32[102400]{0:T(1024)}, f32[102400]{0:T(1024)}, f32[102400]{0:T(1024)}) fusion(f32[102400]{0:T(1024)S(1)} %copy-done.1, bf16[200,128]{1,0:T(8,128)(2,1)S(1)} %get-tuple-element.64, bf16[200,128]{1,0:T(8,128)(2,1)S(1)} %get-tuple-element.63, bf16[200,128]{1,0:T(8,128)(2,1)S(1)} %get-tuple-element.62, ...), kind=kLoop, calls=%fused_computation.6 | loop fusion | flops 2355200 | bytes 2662400 | tf_op jit(solution)/shard_map/sub | solution.py:468
  67.3 12.5 %all-to-all-done.1 = f32[8,16,1152]{2,1,0:T(8,128)S(1)} async-done(((f32[8,16,1152]{2,1,0:T(8,128)}), f32[8,16,1152]{2,1,0:T(8,128)S(1)}, u32[]{:S(2)}, u32[]{:S(2)}) %all-to-all-start.1) | async-done | bytes 589856 | tf_op jit(solution)/shard_map/all_to_all | solution.py:527
  79.8 1.0 %shard_map.151 = bf16[128,1152]{1,0:T(8,128)(2,1)} custom-call(s32[1,128]{1,0:T(1,128)S(1)} %bitcast.22, f32[128,1152]{1,0:T(8,128)S(1)} %get-tuple-element.51.height_rows_ref, f32[128,1152]{1,0:T(8,128)S(1)} %bitcast.19), custom_call_target="tpu_custom_call" | custom-call | tf_op jit(solution)/shard_map/pallas_call | solution.py:516
  (5 shorter events, 0.1 us)
Async XLA Ops:
  0.6 16.0 %copy-start.4 = (f32[64,9,9]{0,2,1:T(8,128)S(1)}, f32[64,9,9]{0,2,1:T(8,128)}, u32[]{:S(2)}) copy-start(f32[64,9,9]{0,2,1:T(8,128)} %param.19) | copy-start | bytes 62212
  2.8 19.1 %all-to-all-start = ((bf16[8,16,1152]{2,1,0:T(8,128)(2,1)}), bf16[8,16,1152]{2,1,0:T(8,128)(2,1)S(1)}, u32[]{:S(2)}, u32[]{:S(2)}) async-start(bf16[8,16,1152]{2,1,0:T(8,128)(2,1)} %bitcast.2), calls=%async_computation | async-start | bytes 589824 | tf_op jit(solution)/shard_map/all_to_all | solution.py:527
  10.1 6.5 %collective-permute-start.1 = (bf16[800,128]{1,0:T(8,128)(2,1)S(1)}, bf16[800,128]{1,0:T(8,128)(2,1)S(1)}, u32[]{:S(2)}, u32[]{:S(2)}) collective-permute-start(bf16[800,128]{1,0:T(8,128)(2,1)S(1)} %get-tuple-element.33.refs_0_), channel_id=1, source_target_pairs={{0,16},{8,24},{16,0},{24,8},{1,17},{9,25},{17,1},{25,9},{2,18},{10... | collective-permute-start | bytes 614408 | tf_op jit(solution)/shard_map/ppermute | solution.py:473
  11.6 8.5 %collective-permute-start = (bf16[800,128]{1,0:T(8,128)(2,1)S(1)}, bf16[800,128]{1,0:T(8,128)(2,1)S(1)}, u32[]{:S(2)}, u32[]{:S(2)}) collective-permute-start(bf16[800,128]{1,0:T(8,128)(2,1)S(1)} %get-tuple-element.33.refs_0_), channel_id=1, source_target_pairs={{0,8},{8,0},{16,24},{24,16},{1,9},{9,1},{17,25},{25,17},{2,10},{10... | collective-permute-start | bytes 614408 | tf_op jit(solution)/shard_map/ppermute | solution.py:473
  16.6 3.5 %collective-permute-start.2 = (bf16[800,128]{1,0:T(8,128)(2,1)S(1)}, bf16[800,128]{1,0:T(8,128)(2,1)S(1)}, u32[]{:S(2)}, u32[]{:S(2)}) collective-permute-start(bf16[800,128]{1,0:T(8,128)(2,1)S(1)} %collective-permute-done.1.refs_2_), channel_id=1, source_target_pairs={{0,8},{8,0},{16,24},{24,16},{1,9},{9,1},{17,25},{25,17},{2,10},{10... | collective-permute-start | bytes 614408 | tf_op jit(solution)/shard_map/ppermute | solution.py:473
  28.8 1.9 %collective-permute-start.3 = (bf16[1600,128]{1,0:T(8,128)(2,1)S(1)}, bf16[1600,128]{1,0:T(8,128)(2,1)S(1)}, u32[]{:S(2)}, u32[]{:S(2)}) collective-permute-start(bf16[1600,128]{1,0:T(8,128)(2,1)S(1)} %get-tuple-element.54), channel_id=1, source_target_pairs={{0,8},{8,0},{16,24},{24,16},{1,9},{9,1},{17,25},{25,17},{2,10},{10... | collective-permute-start | bytes 1228808 | tf_op jit(solution)/shard_map/ppermute | solution.py:473
  30.9 5.2 %collective-permute-start.4 = (bf16[400,128]{1,0:T(8,128)(2,1)S(1)}, bf16[400,128]{1,0:T(8,128)(2,1)S(1)}, u32[]{:S(2)}, u32[]{:S(2)}) collective-permute-start(bf16[400,128]{1,0:T(8,128)(2,1)S(1)} %get-tuple-element.58), channel_id=1, source_target_pairs={{0,2},{1,3},{2,0},{3,1},{4,6},{5,7},{6,4},{7,5},{8,10},{9,11},{10,... | collective-permute-start | bytes 307208 | tf_op jit(solution)/shard_map/ppermute | solution.py:477
  32.7 6.9 %collective-permute-start.5 = (bf16[400,128]{1,0:T(8,128)(2,1)S(1)}, bf16[400,128]{1,0:T(8,128)(2,1)S(1)}, u32[]{:S(2)}, u32[]{:S(2)}) collective-permute-start(bf16[400,128]{1,0:T(8,128)(2,1)S(1)} %get-tuple-element.60), channel_id=1, source_target_pairs={{0,3},{1,2},{2,1},{3,0},{4,7},{5,6},{6,5},{7,4},{8,11},{9,10},{10,... | collective-permute-start | bytes 307208 | tf_op jit(solution)/shard_map/ppermute | solution.py:477
  34.1 6.8 %collective-permute-start.6 = (bf16[400,128]{1,0:T(8,128)(2,1)S(1)}, bf16[400,128]{1,0:T(8,128)(2,1)S(1)}, u32[]{:S(2)}, u32[]{:S(2)}) collective-permute-start(bf16[400,128]{1,0:T(8,128)(2,1)S(1)} %get-tuple-element.59), channel_id=1, source_target_pairs={{0,1},{1,0},{2,3},{3,2},{4,5},{5,4},{6,7},{7,6},{8,9},{9,8},{10,11... | collective-permute-start | bytes 307208 | tf_op jit(solution)/shard_map/ppermute | solution.py:477
  41.0 7.4 %collective-permute-start.7 = (bf16[400,128]{1,0:T(8,128)(2,1)S(1)}, bf16[400,128]{1,0:T(8,128)(2,1)S(1)}, u32[]{:S(2)}, u32[]{:S(2)}) collective-permute-start(bf16[400,128]{1,0:T(8,128)(2,1)S(1)} %add_convert_fusion.2), channel_id=1, source_target_pairs={{0,4},{1,5},{2,6},{3,7},{4,0},{5,1},{6,2},{7,3},{8,12},{9,13},{10,... | collective-permute-start | bytes 307208 | tf_op jit(solution)/shard_map/ppermute | solution.py:473
  48.5 4.2 %collective-permute-start.8 = (bf16[200,128]{1,0:T(8,128)(2,1)S(1)}, bf16[200,128]{1,0:T(8,128)(2,1)S(1)}, u32[]{:S(2)}, u32[]{:S(2)}) collective-permute-start(bf16[200,128]{1,0:T(8,128)(2,1)S(1)} %slice.29), channel_id=1, source_target_pairs={{0,16},{8,24},{16,0},{24,8},{1,17},{9,25},{17,1},{25,9},{2,18},{10... | collective-permute-start | bytes 153608 | tf_op jit(solution)/shard_map/ppermute | solution.py:473
  52.7 13.3 %collective-permute-start.10 = (bf16[200,128]{1,0:T(8,128)(2,1)S(1)}, bf16[200,128]{1,0:T(8,128)(2,1)S(1)}, u32[]{:S(2)}, u32[]{:S(2)}) collective-permute-start(bf16[200,128]{1,0:T(8,128)(2,1)S(1)} %add_convert_fusion.3), channel_id=1, source_target_pairs={{0,2},{1,3},{2,0},{3,1},{4,6},{5,7},{6,4},{7,5},{8,10},{9,11},{10,... | collective-permute-start | bytes 153608 | tf_op jit(solution)/shard_map/ppermute | solution.py:477
  53.2 12.8 %collective-permute-start.11 = (bf16[200,128]{1,0:T(8,128)(2,1)S(1)}, bf16[200,128]{1,0:T(8,128)(2,1)S(1)}, u32[]{:S(2)}, u32[]{:S(2)}) collective-permute-start(bf16[200,128]{1,0:T(8,128)(2,1)S(1)} %add_convert_fusion.3), channel_id=1, source_target_pairs={{0,1},{1,0},{2,3},{3,2},{4,5},{5,4},{6,7},{7,6},{8,9},{9,8},{10,11... | collective-permute-start | bytes 153608 | tf_op jit(solution)/shard_map/ppermute | solution.py:477
  53.5 12.4 %collective-permute-start.9 = (bf16[200,128]{1,0:T(8,128)(2,1)S(1)}, bf16[200,128]{1,0:T(8,128)(2,1)S(1)}, u32[]{:S(2)}, u32[]{:S(2)}) collective-permute-start(bf16[200,128]{1,0:T(8,128)(2,1)S(1)} %add_convert_fusion.3), channel_id=1, source_target_pairs={{0,3},{1,2},{2,1},{3,0},{4,7},{5,6},{6,5},{7,4},{8,11},{9,10},{10,... | collective-permute-start | bytes 153608 | tf_op jit(solution)/shard_map/ppermute | solution.py:477
  61.3 4.8 %copy-start.1 = (f32[102400]{0:T(1024)S(1)}, f32[102400]{0:T(1024)}, u32[]{:S(2)}) copy-start(f32[102400]{0:T(1024)} %param.13) | copy-start | bytes 1228804
  61.3 4.8 %copy-start.2 = (f32[102400]{0:T(1024)S(1)}, f32[102400]{0:T(1024)}, u32[]{:S(2)}) copy-start(f32[102400]{0:T(1024)} %param.15) | copy-start | bytes 1228804
  61.3 4.8 %copy-start.3 = (f32[102400]{0:T(1024)S(1)}, f32[102400]{0:T(1024)}, u32[]{:S(2)}) copy-start(f32[102400]{0:T(1024)} %param.14) | copy-start | bytes 1228804
  61.3 18.5 %all-to-all-start.1 = ((f32[8,16,1152]{2,1,0:T(8,128)}), f32[8,16,1152]{2,1,0:T(8,128)S(1)}, u32[]{:S(2)}, u32[]{:S(2)}) async-start(f32[8,16,1152]{2,1,0:T(8,128)} %bitcast.8), calls=%async_computation.1 | async-start | bytes 1179648 | tf_op jit(solution)/shard_map/all_to_all | solution.py:527
  66.1 13.7 %copy-start = (s32[1,1,128]{2,1,0:T(1,128)S(1)}, s32[1,1,128]{2,1,0:T(1,128)}, u32[]{:S(2)}) copy-start(s32[1,1,128]{2,1,0:T(1,128)} %param.16) | copy-start | bytes 1540
